TPU v7x, 32 devices: a whole 2x2x4 slice. The times are simulated.
32 devices in a mesh: past: 2 (over y), second: 16 (over z, x, core).
Axes of the slice: x: 2, y: 2, z: 4, core: 2. Of those that a mesh axis runs over, the one named last changes fastest.
Arguments:
- green_row: float32 [256, 64, 128], P('second'), may hold values from -4 to 4
- green_hist: float32 [8, 256, 64, 128], P('past', 'second'), may hold values from -5.25 to 5.25, as said below
- hamiltonian: float32 [64, 128], replicated, may hold values from -0.75 to 0.75
- quad_table: float32 [8], replicated, may hold values from 0.2 to 2
- weight_index: int32 [8], P('past'), may hold values from 0 to 7
- block_start: int32 [1], replicated, may hold values from 0 to 248
Outputs:
- green_next: float32 [256, 64, 128], P('second')
- change_norm: float32 [1], replicated
Inputs may be any that keep to these rules, and one draw needn't show every extreme that they name: `green_hist`: real numbers of order one; magnitudes differ between second times.
All inputs are finite; a program needn't handle non-finite values.
Results may differ from a plain program's by a relative error of at most 0.0003.
Values sent between devices are 32-bit elements; how exact they have to be, the bound alone decides.
No kernel may reach another device: no remote copies, remote signals or barrier semaphores. Data moves between devices by JAX's collectives and lax.ppermute only.
A program may use at most 64 MiB of HBM per device.

v0:
```python
import math

import jax
import jax.numpy as jnp
from jax import lax
from jax.sharding import PartitionSpec as P

coupling = 0.5
step_size = 0.25


def rotate(tiles, orbits):
    return jnp.concatenate([-tiles[..., orbits:], tiles[..., :orbits]], axis=-1)


def self_energy(tiles, orbits):
    magnitude = tiles[..., :orbits] ** 2 + tiles[..., orbits:] ** 2
    return -coupling * jnp.concatenate([magnitude, magnitude], axis=-1) * tiles


def local(green_row, green_hist, hamiltonian, quad_table, weight_index, block_start):
    orbits = hamiltonian.shape[0]
    sec_rows = green_row.shape[0]
    past_rows = green_hist.shape[0]
    total_past = past_rows * lax.axis_size("past")
    window_start = block_start[0]
    offset = lax.axis_index("second") * sec_rows
    past_first = lax.axis_index("past") * past_rows
    weights = jnp.take(quad_table, weight_index, axis=0)
    norm_scale = 1.0 / math.sqrt(orbits * total_past)
    ham_real = hamiltonian[:, :orbits]
    ham_imag = hamiltonian[:, orbits:]
    herm_real = 0.5 * (ham_real + ham_real.T)
    herm_imag = 0.5 * (ham_imag - ham_imag.T)
    right_side = jnp.stack([green_hist, self_energy(green_hist, orbits)])

    def select(tiles_in, wanted):
        local_pos = wanted - offset
        inside = (local_pos >= 0) & (local_pos < sec_rows)
        picked = jnp.take(tiles_in, jnp.clip(local_pos, 0, sec_rows - 1), axis=0)
        return jnp.where(inside[:, None, None], picked, jnp.zeros_like(picked))

    def window_of(tiles_in):
        wanted = window_start + jnp.arange(total_past, dtype=jnp.int32)
        every_tile = lax.psum(select(tiles_in, wanted), "second")
        return lax.dynamic_slice_in_dim(every_tile, past_first, past_rows, 0)

    def memory(tiles_in):
        window = window_of(tiles_in)
        weight_col = weights[:, None, None]
        left_side = jnp.stack([weight_col * self_energy(window, orbits), weight_col * window])
        left_side = jnp.stack([left_side[..., :orbits], left_side[..., orbits:]])
        contracted = jnp.einsum(
            "cqpij,qpsjk->csik", left_side, right_side, precision=lax.Precision.HIGHEST
        )
        return norm_scale * (contracted[0] + rotate(contracted[1], orbits))

    def derive(tiles_in, integral):
        first = jnp.einsum("ij,sjk->sik", herm_real, tiles_in, precision=lax.Precision.HIGHEST)
        second = jnp.einsum(
            "ij,sjk->sik", herm_imag, rotate(tiles_in, orbits), precision=lax.Precision.HIGHEST
        )
        combined = first + second + integral
        return jnp.concatenate([combined[..., orbits:], -combined[..., :orbits]], axis=-1)

    share_rows = sec_rows // lax.axis_size("past")
    share_first = lax.axis_index("past") * share_rows
    row_share = lax.dynamic_slice_in_dim(green_row, share_first, share_rows, 0)

    def shared(tiles_in):
        return lax.psum_scatter(memory(tiles_in), "past", scatter_dimension=0, tiled=True)

    def spread(piece):
        return lax.all_gather(piece, "past", axis=0, tiled=True)

    slope_one = derive(row_share, shared(green_row))
    predicted = row_share + step_size * slope_one
    predicted_full = spread(predicted)
    slope_two = derive(predicted, shared(predicted_full))
    corrected = row_share + 0.5 * step_size * (slope_one + slope_two)
    square_sum = lax.psum(jnp.sum((corrected - predicted) ** 2), ("past", "second"))
    green_next = spread(corrected)
    entry_count = sec_rows * lax.axis_size("second") * orbits * 2 * orbits
    change = jnp.sqrt(square_sum / entry_count) / step_size
    return (green_next, change.reshape(1))


def solution(mesh):
    placed = (P("second", None, None), P("past", "second", None, None), P(), P(), P("past"), P())
    return jax.shard_map(
        local, mesh=mesh, in_specs=placed, out_specs=(P("second", None, None), P()), check_vma=False
    )
```

profile of v0, /device:TPU:0, one launch (start us, length us, event | category | flops | bytes accessed | tf_op | source)
XLA Modules:
  0.0 314.5 jit_solution(17041485729284683921)
XLA Ops:
  7.2 0.0 all-reduce.3.cloned.1.call-start
  7.9 1.6 gather_fusion.1
  9.5 0.8 select_select_fusion.1
  10.3 0.0 all-reduce.3.cloned.1.call-update
  10.3 0.0 reduce-scatter.3.cloned.1.call-start
  10.4 0.7 compare_select_fusion.1
  11.1 3.0 fusion.2
  14.1 2.2 copy_bitcast_fusion
  16.2 0.6 gather_fusion
  16.9 87.6 %all-reduce.3.cloned.1.call-done = f32[8,64,128]{2,1,0:T(8,128)} async-done(((f32[8,64,128]{2,1,0:T(8,128)}), f32[8,64,128]{2,1,0:T(8,128)}) %all-reduce.3.cloned.1.call-update) | async-done | bytes 262160 | tf_op jit(solution)/shard_map/psum | solution.py:45
  104.5 1.1 fusion.31
  105.6 1.0 fusion.34
  106.6 0.1 maximum_bitcast_fusion.11
  106.8 4.1 %fusion.5 = f32[2,16,64,128]{3,2,1,0:T(8,128)S(1)} fusion(f32[1,4,16,64,128]{4,3,0,1,2:T(8,128)} %get-tuple-element.8, f32[1,4,16,64,128]{4,3,0,1,2:T(8,128)S(1)} %get-tuple-element.7, f32[1,2,4,64,64]{4,3,1,2,0:T(8,128)S(1)} %get-tuple-element.28, f32[1,2,4,64,64]{4,3,1,2,0:T(8,128)S(1)} %get-tuple-element.27), kind=kOutput, calls=%fused_computation.12 | convolution fusion | flops 1611726848 | bytes 5505024 | tf_op jit(solution)/shard_map/cqpij,qpsjk->csik/dot_general | solution.py:53
  111.0 0.2 slice_negate_fusion.1
  111.2 1.0 fusion.14
  112.2 0.0 reduce-scatter.3.cloned.1.call-update
  112.2 0.0 all-reduce.5.cloned.1.call-start
  112.3 0.1 fusion.65
  112.4 0.1 copy.49
  112.4 0.1 copy.32
  112.5 0.1 dynamic-slice_negate_fusion
  112.7 0.4 fusion.28
  113.1 14.4 %reduce-scatter.3.cloned.1.call-done = f32[8,64,128]{2,1,0:T(8,128)} async-done(((f32[16,64,128]{2,1,0:T(8,128)}), f32[8,64,128]{2,1,0:T(8,128)}) %reduce-scatter.3.cloned.1.call-update) | async-done | bytes 262160 | tf_op jit(solution)/shard_map/reduce_scatter | solution.py:71
  127.5 1.5 fusion.10
  128.9 0.1 fusion.64
  129.1 0.1 multiply_add_fusion
  129.2 8.6 %all_gather.6 = f32[16,64,128]{2,1,0:T(8,128)} all-gather(f32[8,64,128]{2,1,0:T(8,128)S(1)} %multiply_add_fusion), channel_id=1, replica_groups=mesh['past'=2,'second'=16] {'past'}, dimensions={0}, use_global_device_ids=true | all-gather | bytes 786432 | tf_op jit(solution)/shard_map/all_gather | solution.py:74
  137.9 2.3 gather_fusion.2
  140.2 1.7 select_select_fusion
  141.9 0.0 all-reduce.5.cloned.1.call-update
  142.0 0.0 reduce-scatter.5.cloned.1.call-start
  142.0 89.9 %all-reduce.5.cloned.1.call-done = f32[8,64,128]{2,1,0:T(8,128)} async-done(((f32[8,64,128]{2,1,0:T(8,128)}), f32[8,64,128]{2,1,0:T(8,128)}) %all-reduce.5.cloned.1.call-update) | async-done | bytes 262160 | tf_op jit(solution)/shard_map/psum | solution.py:45
  231.9 1.1 fusion.30
  233.0 1.0 fusion.37
  234.1 0.1 maximum_bitcast_fusion.10
  234.2 4.1 %fusion.6 = f32[2,16,64,128]{3,2,1,0:T(8,128)S(1)} fusion(f32[1,4,16,64,128]{4,3,0,1,2:T(8,128)} %get-tuple-element.8, f32[1,4,16,64,128]{4,3,0,1,2:T(8,128)S(1)} %get-tuple-element.7, f32[1,2,4,64,64]{4,3,2,1,0:T(8,128)S(1)} %get-tuple-element.24, f32[1,2,4,64,64]{4,3,2,1,0:T(8,128)S(1)} %get-tuple-element.23), kind=kOutput, calls=%fused_computation.13 | convolution fusion | flops 1611726848 | bytes 5505024 | tf_op jit(solution)/shard_map/cqpij,qpsjk->csik/dot_general | solution.py:53
  238.4 0.2 slice_negate_fusion
  238.6 1.0 fusion.12
  239.6 0.4 fusion.41
  240.0 0.1 slice_negate_fusion.3
  240.1 14.8 %reduce-scatter.5.cloned.1.call-done = f32[8,64,128]{2,1,0:T(8,128)} async-done(((f32[16,64,128]{2,1,0:T(8,128)}), f32[8,64,128]{2,1,0:T(8,128)}) %reduce-scatter.5.cloned.1.call-update) | async-done | bytes 262160 | tf_op jit(solution)/shard_map/reduce_scatter | solution.py:71
  254.9 1.4 fusion.8
  256.4 0.1 fusion.63
  256.5 0.8 multiply_reduce_fusion
  257.3 8.5 %all_gather.7 = f32[16,64,128]{2,1,0:T(8,128)S(1)} all-gather(f32[8,64,128]{2,1,0:T(8,128)S(1)} %get-tuple-element.4), channel_id=1, replica_groups=mesh['past'=2,'second'=16] {'past'}, dimensions={0}, use_global_device_ids=true | all-gather | bytes 786432 | tf_op jit(solution)/shard_map/all_gather | solution.py:74
  265.8 39.5 %psum.23 = f32[]{:T(128)} all-reduce(f32[]{:T(128)} %get-tuple-element.3), channel_id=1, replica_groups=mesh['past'=2,'second'=16] {'past','second'}, use_global_device_ids=true, to_apply=%region_5.7 | all-reduce | flops 1 | bytes 8 | tf_op jit(solution)/shard_map/psum | solution.py:81
  306.0 0.8 copy.60
  (17 shorter events, 0.2 us)
Async XLA Ops:
  7.2 9.1 %copy-start = (f32[8]{0:T(128)S(1)}, f32[8]{0:T(128)}, u32[]{:S(2)}) copy-start(f32[8]{0:T(128)} %param.11) | copy-start | bytes 100
  7.2 97.3 %all-reduce.3.cloned.1.call-start = ((), (), s32[]{:S(2)}) async-start(), calls=%async_computation.2 | async-start | bytes 524288 | tf_op jit(solution)/shard_map/psum | solution.py:45
  10.3 117.1 %reduce-scatter.3.cloned.1.call-start = ((), (), s32[]{:S(2)}) async-start(), calls=%async_computation.3 | async-start | bytes 786432 | tf_op jit(solution)/shard_map/reduce_scatter | solution.py:71
  11.1 3.0 copy-start.1
  14.1 2.8 copy-start.4
  110.9 1.3 copy-start.3
  111.0 1.6 copy-start.2
  112.2 119.7 %all-reduce.5.cloned.1.call-start = ((), (), s32[]{:S(2)}) async-start(), calls=%async_computation.4 | async-start | bytes 524288 | tf_op jit(solution)/shard_map/psum | solution.py:45
  142.0 112.9 %reduce-scatter.5.cloned.1.call-start = ((), (), s32[]{:S(2)}) async-start(), calls=%async_computation.5 | async-start | bytes 786432 | tf_op jit(solution)/shard_map/reduce_scatter | solution.py:71
Sparse Core Ops, SparseCore 0:
  12.0 92.5 all-reduce.2
  112.3 15.1 reduce-scatter.2
  142.1 89.8 all-reduce.4
  239.8 15.1 reduce-scatter.4
where the time goes:
time: 315 us; the launch traced here: 314 us
  waiting for transfers between devices  207 us (66%)
  blocking collectives  56.7 us (18%)
  other arithmetic  16.8 us (5%)
  between operations  16.5 us (5%)
  matrix products  11.9 us (4%)
  local copies, waits for them, and re-layouts  5.69 us (2%)
    psum x2, waiting for transfers between devices, window_of(): every_tile = lax.psum(select(tiles_in, wanted), 'second')  178 us
    psum x1, blocking collectives, local(): lax.psum(jnp.sum((corrected - predicted) ** 2), ('past', 'second'))  39.5 us
    reduce_scatter x2, waiting for transfers between devices, shared(): lax.psum_scatter(memory(tiles_in), 'past', scatter_dimension=0, tiled=True)  29.2 us
    all_gather x2, blocking collectives, spread(): return lax.all_gather(piece, 'past', axis=0, tiled=True)  17.2 us
    dot_general x2, matrix products, memory(): jnp.einsum('cqpij,qpsjk->csik', left_side, right_side, precision=lax.Prec...  8.27 us
  transfers between devices with their start and end apart: 4, of which 4 were waited for; matrix products, arithmetic and copies ran while one was open for 2% of the time, Pallas kernels for 0%

commit v1 on v0

v1 whole, which is shorter than its diff:
```python
import math

import jax
import jax.numpy as jnp
from jax import lax
from jax.experimental import pallas as pl
from jax.experimental.pallas import tpu as pltpu
from jax.sharding import PartitionSpec as P

coupling = 0.5
step_size = 0.25

f32 = jnp.float32
bf16 = jnp.bfloat16
SMEM_SPEC = pl.BlockSpec(memory_space=pltpu.SMEM)
VMEM_SPEC = pl.BlockSpec(memory_space=pltpu.VMEM)


def split(value):
    high = value.astype(bf16)
    return high, (value - high.astype(f32)).astype(bf16)


def dot3(left, right):
    def one(a, b):
        return jnp.dot(a, b, preferred_element_type=f32)

    return one(left[0], right[0]) + (one(left[0], right[1]) + one(left[1], right[0]))


def swap_halves(tile):
    return pltpu.roll(tile, tile.shape[-1] // 2, tile.ndim - 1)


def is_real(shape):
    return lax.broadcasted_iota(jnp.int32, shape, len(shape) - 1) < shape[-1] // 2


def self_energy(tile):
    square = tile * tile
    return -coupling * (square + swap_halves(square)) * tile


def minus_i_times(acc, orbits):
    turned = swap_halves(acc[:orbits])
    return acc[orbits:] + jnp.where(is_real(turned.shape), turned, -turned)


def left_factor(tile, weight):
    scaled = weight * self_energy(tile)
    plain = weight * tile
    real = is_real(tile.shape)
    return jnp.concatenate(
        [jnp.where(real, scaled, swap_halves(plain)), jnp.where(real, swap_halves(scaled), plain)], axis=0
    )


def right_factor(tiles):
    return jnp.concatenate(
        [jnp.concatenate(tiles, axis=1), jnp.concatenate([self_energy(t) for t in tiles], axis=1)], axis=0
    )


def prepare_kernel(pos_ref, inside_ref, row_ref, ham_ref, window_ref, herm_ref):
    count = window_ref.shape[0]
    orbits = ham_ref.shape[0]
    for p in range(count):
        window_ref[p] = jnp.where(inside_ref[p] > 0, row_ref[pos_ref[p]], 0.0)
    real = ham_ref[:, :orbits]
    imag = ham_ref[:, orbits:]
    herm_ref[...] = jnp.concatenate([0.5 * (real + real.T), 0.5 * (imag - imag.T)], axis=0)


def prepare(pos, inside, green_row, hamiltonian):
    count = pos.shape[0]
    orbits = hamiltonian.shape[0]
    return pl.pallas_call(
        prepare_kernel,
        in_specs=[SMEM_SPEC, SMEM_SPEC, VMEM_SPEC, VMEM_SPEC],
        out_specs=[VMEM_SPEC, VMEM_SPEC],
        out_shape=[
            jax.ShapeDtypeStruct((count,) + green_row.shape[1:], f32),
            jax.ShapeDtypeStruct((2 * orbits, orbits), f32),
        ],
        name="prepare",
    )(pos, inside, green_row, hamiltonian)


def owner_kernel(
    pos_ref, inside_ref, quad_ref, index_ref, own_ref, win_ref, base_ref, herm_ref, hist_a, hist_b, out_ref, hi, lo,
    *, scale
):
    past_rows, orbits, width = win_ref.shape
    step = pl.program_id(0)

    @pl.when(step == 0)
    def _():
        for p in range(past_rows):
            high, low = split(left_factor(win_ref[p], quad_ref[index_ref[p]]))
            hi[:, p * width : (p + 1) * width] = high
            lo[:, p * width : (p + 1) * width] = low

    right = jnp.concatenate([right_factor([hist_a[p, 0], hist_b[p, 0]]) for p in range(past_rows)], axis=0)
    acc = dot3((hi[...], lo[...]), split(right))
    part = step_size * scale * jnp.concatenate(
        [minus_i_times(acc[:, :width], orbits)[None], minus_i_times(acc[:, width:], orbits)[None]], axis=0
    )
    for q in range(2):
        out_ref[q] = jnp.where(inside_ref[2 * step + q] > 0, part[q], 0.0)

    first = own_ref[0]

    @pl.when((2 * step >= first) & (2 * step < first + past_rows))
    def _():
        base = jnp.concatenate([base_ref[2 * step - first], base_ref[2 * step + 1 - first]], axis=1)
        acc_ham = dot3(split(herm_ref[...]), split(base))
        for q in range(2):
            cols = slice(q * width, (q + 1) * width)
            out_ref[q] += base[:, cols] + step_size * minus_i_times(acc_ham[:, cols], orbits)


def owner_part(pos, inside, quad_table, weight_index, first, window, base, herm, green_hist, scale):
    past_rows, _, orbits, width = green_hist.shape
    total = pos.shape[0]
    fixed = lambda shape: pl.BlockSpec(shape, lambda i, *_: (0,) * len(shape))
    return pl.pallas_call(
        lambda *refs: owner_kernel(*refs, scale=scale),
        grid_spec=pltpu.PrefetchScalarGridSpec(
            num_scalar_prefetch=5,
            grid=(total // 2,),
            in_specs=[
                fixed(window.shape),
                fixed(base.shape),
                fixed(herm.shape),
                pl.BlockSpec((past_rows, 1, orbits, width), lambda i, pos, *_: (0, pos[2 * i], 0, 0)),
                pl.BlockSpec((past_rows, 1, orbits, width), lambda i, pos, *_: (0, pos[2 * i + 1], 0, 0)),
            ],
            out_specs=pl.BlockSpec((2, orbits, width), lambda i, *_: (i, 0, 0)),
            scratch_shapes=[pltpu.VMEM((2 * orbits, past_rows * width), bf16)] * 2,
        ),
        out_shape=jax.ShapeDtypeStruct((total, orbits, width), f32),
        name="owner_part",
    )(pos, inside, quad_table, weight_index, first, window, base, herm, green_hist, green_hist)


def integral_kernel(quad_ref, index_ref, odd_ref, mine_ref, other_ref, hist_ref, out_ref, hi, lo, *, scale):
    past_rows, group, orbits, width = hist_ref.shape
    half = past_rows // 2

    @pl.when(pl.program_id(0) == 0)
    def _():
        for p in range(past_rows):
            here = odd_ref[0] == p // half
            tile = jnp.where(here, mine_ref[p % half], other_ref[p % half])
            high, low = split(left_factor(tile, quad_ref[index_ref[p]]))
            hi[:, p * width : (p + 1) * width] = high
            lo[:, p * width : (p + 1) * width] = low

    for s in range(0, group, 2):
        right = jnp.concatenate(
            [right_factor([hist_ref[p, s], hist_ref[p, s + 1]]) for p in range(past_rows)], axis=0
        )
        acc = dot3((hi[...], lo[...]), split(right))
        for q in range(2):
            out_ref[s + q] = scale * minus_i_times(acc[:, q * width : (q + 1) * width], orbits)


def integral(quad_table, weight_index, odd, mine, other, green_hist, scale, name):
    past_rows, sec_rows, orbits, width = green_hist.shape
    group = 4
    fixed = lambda shape: pl.BlockSpec(shape, lambda i: (0,) * len(shape))
    return pl.pallas_call(
        lambda *refs: integral_kernel(*refs, scale=scale),
        grid=(sec_rows // group,),
        in_specs=[
            SMEM_SPEC,
            SMEM_SPEC,
            SMEM_SPEC,
            fixed(mine.shape),
            fixed(other.shape),
            pl.BlockSpec((past_rows, group, orbits, width), lambda i: (0, i, 0, 0)),
        ],
        out_specs=pl.BlockSpec((group, orbits, width), lambda i: (i, 0, 0)),
        scratch_shapes=[pltpu.VMEM((2 * orbits, past_rows * width), bf16)] * 2,
        out_shape=jax.ShapeDtypeStruct((sec_rows, orbits, width), f32),
        name=name,
    )(quad_table, weight_index, odd, mine, other, green_hist)


def share_kernel(row_ref, sum_ref, herm_ref, out_base_ref, diff_base_ref):
    share, orbits, width = row_ref.shape
    herm = split(herm_ref[...])
    for s in range(0, share, 2):
        def pair(ref):
            return jnp.concatenate([ref[s], ref[s + 1]], axis=1)

        def ham(value):
            acc = dot3(herm, split(value))
            return jnp.concatenate(
                [minus_i_times(acc[:, q * width : (q + 1) * width], orbits) for q in range(2)], axis=1
            )

        row = pair(row_ref)
        slope = ham(row) + pair(sum_ref)
        turned = ham(row + step_size * slope)
        out_base = row + 0.5 * step_size * (slope + turned)
        diff_base = 0.5 * step_size * (turned - slope)
        for q in range(2):
            cols = slice(q * width, (q + 1) * width)
            out_base_ref[s + q] = out_base[:, cols]
            diff_base_ref[s + q] = diff_base[:, cols]


def share_bases(row, slope_sum, herm):
    shape = jax.ShapeDtypeStruct(row.shape, f32)
    return pl.pallas_call(
        share_kernel,
        in_specs=[VMEM_SPEC] * 3,
        out_specs=[VMEM_SPEC] * 2,
        out_shape=[shape, shape],
        name="share_bases",
    )(row, slope_sum, herm)


def exchange(value, axis, mask):
    size = lax.axis_size(axis)
    return lax.ppermute(value, axis, [(i, i ^ mask) for i in range(size)])


def pick(value, index, axis=0):
    return lax.dynamic_index_in_dim(value, index, axis, keepdims=False)


def scatter_past(value):
    size = lax.axis_size("past")
    index = lax.axis_index("past")
    while size > 1:
        half = size // 2
        value = value.reshape((2, half) + value.shape[1:])
        upper = (index // half) % 2
        value = pick(value, upper) + exchange(pick(value, 1 - upper), "past", half)
        size = half
    return value[0]


def gather_past(value):
    size = lax.axis_size("past")
    index = lax.axis_index("past")
    value = value[None]
    mask = 1
    while mask < size:
        other = exchange(value, "past", mask)
        upper = (index // mask) % 2 == 1
        value = jnp.concatenate([jnp.where(upper, other, value), jnp.where(upper, value, other)], axis=0)
        mask *= 2
    return value


def spread_second(value):
    mask = 2
    while mask < lax.axis_size("second"):
        value = value + exchange(value, "second", mask)
        mask *= 2
    return value


def local(green_row, green_hist, hamiltonian, quad_table, weight_index, block_start):
    orbits = hamiltonian.shape[0]
    sec_rows = green_row.shape[0]
    past_rows = green_hist.shape[0]
    width = green_row.shape[-1]
    past_size = lax.axis_size("past")
    second_size = lax.axis_size("second")
    total_past = past_rows * past_size
    past_index = lax.axis_index("past")
    second_index = lax.axis_index("second")
    odd = second_index % 2
    odd_arg = odd.reshape(1)
    scale = 1.0 / math.sqrt(orbits * total_past)

    spot = block_start[0] - second_index * sec_rows + jnp.arange(total_past, dtype=jnp.int32)
    inside = ((spot >= 0) & (spot < sec_rows)).astype(jnp.int32)
    pos = jnp.clip(spot, 0, sec_rows - 1)
    first = past_index * past_rows
    own_pos = lax.dynamic_slice_in_dim(pos, first, past_rows)
    own_inside = lax.dynamic_slice_in_dim(inside, first, past_rows)
    own_window, herm = prepare(own_pos, own_inside, green_row, hamiltonian)

    halves = own_window.reshape(2, past_rows // 2, orbits, width)
    row_mine = spread_second(pick(halves, odd) + exchange(pick(halves, 1 - odd), "second", 1))
    row_other = exchange(row_mine, "second", 1)

    owner = block_start[0] // sec_rows
    crossing = (block_start[0] + total_past - 1) // sec_rows > owner
    flips = owner ^ (owner + 1)
    branch = jnp.where(crossing, 1, 0)
    masks = []
    while 2 ** len(masks) < second_size:
        masks.append(2 ** (len(masks) + 1) - 1)
    for mask in masks[:-1]:
        branch = branch + jnp.where(crossing & (flips > mask), 1, 0)
    window = lax.switch(
        branch,
        [lambda w: w] + [lambda w, mask=mask: w + exchange(w, "second", mask) for mask in masks],
        own_window,
    )
    part = owner_part(
        pos, inside, quad_table, weight_index, first.reshape(1), window, own_window, herm, green_hist, scale
    )

    parts = part.reshape(past_size, 2, past_rows // 2, orbits, width)
    parts = pick(parts, odd, 1) + exchange(pick(parts, 1 - odd, 1), "second", 1)
    pred_mine = spread_second(scatter_past(parts))
    pred_other = exchange(pred_mine, "second", 1)

    share_rows = sec_rows // past_size
    row_share = lax.dynamic_slice_in_dim(green_row, past_index * share_rows, share_rows, 0)

    def by_share(value):
        return value.reshape((past_size, share_rows) + value.shape[1:])

    slope_part = integral(quad_table, weight_index, odd_arg, row_mine, row_other, green_hist, scale, "integral_row")
    slope_sum = scatter_past(by_share(slope_part))
    out_base, diff_base = share_bases(row_share, slope_sum, herm)

    last_part = integral(
        quad_table, weight_index, odd_arg, pred_mine, pred_other, green_hist, 0.5 * step_size * scale, "integral_pred"
    )
    last_sum = scatter_past(by_share(last_part))
    out_share = out_base + last_sum
    square_sum = jnp.sum((diff_base + last_sum) ** 2)
    green_next = gather_past(out_share).reshape(green_row.shape)

    devices = past_size * second_size
    lanes = jnp.broadcast_to(square_sum.reshape(1, 1), (devices, 128))
    sums = lax.all_to_all(lanes, ("past", "second"), 0, 0, tiled=True)
    total = jnp.sum(sums[:, :1])
    entry_count = sec_rows * second_size * orbits * width
    change = jnp.sqrt(total / entry_count) / step_size
    return (green_next, change.reshape(1))


def solution(mesh):
    placed = (P("second", None, None), P("past", "second", None, None), P(), P(), P("past"), P())
    return jax.shard_map(
        local, mesh=mesh, in_specs=placed, out_specs=(P("second", None, None), P()), check_vma=False
    )
```

time: 315 us -> 72.5 us (0.23)
  waiting for transfers between devices: 207 us -> 14.6 us
  blocking collectives: 56.7 us -> 0 us
  starting transfers between devices: 0.16 us -> 22 us
  Pallas kernels: 0 us -> 19.6 us
  between operations: 16.5 us -> 3.32 us
  matrix products: 11.9 us -> 0 us
  other arithmetic: 16.8 us -> 4.93 us
    psum x2 -> x0, waiting for transfers between devices: 178 us -> none  [window_of(): every_tile = lax.psum(select(tiles_in, wanted), 'second')]
    psum x1 -> x0, blocking collectives: 39.5 us -> none  [local(): lax.psum(jnp.sum((corrected - predicted) ** 2), ('past', 'second'))]
    reduce_scatter x2 -> x0, waiting for transfers between devices: 29.2 us -> none  [shared(): lax.psum_scatter(memory(tiles_in), 'past', scatter_dimension=0, tiled=True)]
    pallas_call x0 -> x5, Pallas kernels: none -> 19.6 us  [the longest x2 9.89 us: integral(): pl.pallas_call(lambda *refs: integral_kernel(*refs, scale=scale), grid=(s...]
    ppermute x0 -> x14, starting transfers between devices: none -> 18.3 us  [exchange(): return lax.ppermute(value, axis, [(i, i ^ mask) for i in range(size)])]
    all_gather x2 -> x0, blocking collectives: 17.2 us -> none  [spread(): return lax.all_gather(piece, 'past', axis=0, tiled=True)]
    dot_general x6 -> x0, matrix products: 11.9 us -> none  [the longest x2 8.27 us: memory(): jnp.einsum('cqpij,qpsjk->csik', left_side, right_side, precision=lax.Prec...]
    ppermute x0 -> x14, waiting for transfers between devices: none -> 7.46 us  [exchange(): return lax.ppermute(value, axis, [(i, i ^ mask) for i in range(size)])]
  transfers between devices with their start and end apart: 4 -> 15, of which waited for: 4 -> 6; matrix products, arithmetic and copies ran while one was open for 2% -> 10% of each run, Pallas kernels for 0% -> 24%
where the time goes in v1:
time: 72.5 us; the launch traced here: 72 us
  starting transfers between devices  22 us (30%)
  Pallas kernels  19.6 us (27%)
  waiting for transfers between devices  14.6 us (20%)
  local copies, waits for them, and re-layouts  7.54 us (10%)
  other arithmetic  4.93 us (7%)
  between operations  3.32 us (5%)
    ppermute x14, starting transfers between devices, exchange(): return lax.ppermute(value, axis, [(i, i ^ mask) for i in range(size)])  18.3 us
    pallas_call x2, Pallas kernels, integral(): pl.pallas_call(lambda *refs: integral_kernel(*refs, scale=scale), grid=(s...  9.89 us
    ppermute x14, waiting for transfers between devices, exchange(): return lax.ppermute(value, axis, [(i, i ^ mask) for i in range(size)])  7.46 us
    all_to_all x1, waiting for transfers between devices, local(): sums = lax.all_to_all(lanes, ('past', 'second'), 0, 0, tiled=True)  7.1 us
    pallas_call x1, Pallas kernels, owner_part(): pl.pallas_call(lambda *refs: owner_kernel(*refs, scale=scale), grid_spec=...  5.01 us
    all_to_all x1, starting transfers between devices, local(): sums = lax.all_to_all(lanes, ('past', 'second'), 0, 0, tiled=True)  3.75 us
    squeeze x5, local copies, waits for them, and re-layouts, pick(): return lax.dynamic_index_in_dim(value, index, axis, keepdims=False)  3.02 us
    pallas_call x1, Pallas kernels, share_bases(): pl.pallas_call(share_kernel, in_specs=[VMEM_SPEC] * 3, out_specs=[VMEM_SP...  2.71 us
  transfers between devices with their start and end apart: 15, of which 6 were waited for; matrix products, arithmetic and copies ran while one was open for 10% of the time, Pallas kernels for 24%

profile of v1, /device:TPU:0, one launch (start us, length us, event | category | flops | bytes accessed | tf_op | source)
XLA Modules:
  0.0 72.0 jit_solution(16105359623425011253)
XLA Ops:
  1.3 0.7 dynamic_slice.40.pos_ref
  2.0 0.6 dynamic_slice.41.inside_ref
  2.6 2.0 %prepare.1 = (f32[4,64,128]{2,1,0:T(8,128)S(1)}, f32[128,64]{1,0:T(8,128)}) custom-call(s32[4]{0:T(128)} %dynamic_slice.40.pos_ref, s32[4]{0:T(128)} %dynamic_slice.41.inside_ref, f32[16,64,128]{2,1,0:T(8,128)} %row_ref.1, f32[64,128]{1,0:T(8,128)} %ham_ref.1), custom_call_target="tpu_custom_call" | custom-call | tf_op jit(solution)/shard_map/prepare/pallas_call | solution.py:77
  4.6 0.6 collective-permute-start.4
  5.2 5.0 %owner_part.1 = f32[8,64,128]{2,1,0:T(8,128)} custom-call(s32[8]{0:T(128)} %copy-done.7, s32[8]{0:T(128)} %copy-done.8, f32[8]{0:T(128)} %refs_0_.3, s32[4]{0:T(128)} %refs_1_.3, s32[1]{0:T(128)} %bitcast.11.refs_4_, f32[4,64,128]{2,1,0:T(8,128)S(1)} %get-tuple-element.25.refs_5_, f32[4,64,128]{2,1,0:T(8,128)S(1)} %get-tuple-element.17.refs_6_, ...), custom_call_target="tpu_custom_call" | custom-call | tf_op jit(solution)/shard_map/owner_part/pallas_call | solution.py:126
  10.2 0.9 %dynamic-slice_bitcast_fusion.2 = f32[2,2,64,128]{3,2,1,0:T(8,128)S(1)} fusion(f32[2,2,2,64,128]{4,3,2,1,0:T(8,128)} %bitcast.65, s32[]{:T(128)S(6)} %select_n.88), kind=kLoop, calls=%fused_computation.12 | loop fusion | bytes 262148 | tf_op jit(solution)/shard_map/jit(dynamic_index_in_dim)/squeeze | solution.py:231
  11.1 0.2 collective-permute-start.10
  11.3 0.0 collective-permute-done.4
  11.3 3.0 %collective-permute-start.5 = (f32[2,64,128]{2,1,0:T(8,128)S(1)}, f32[2,64,128]{2,1,0:T(8,128)S(1)}, u32[]{:S(2)}, u32[]{:S(2)}) collective-permute-start(f32[2,64,128]{2,1,0:T(8,128)S(1)} %bitcast_add_fusion.5), channel_id=1, source_target_pairs={{0,2},{1,3},{2,0},{3,1},{4,6},{5,7},{6,4},{7,5},{8,10},{9,11},{10,... | collective-permute-start | bytes 196616 | tf_op jit(solution)/shard_map/ppermute | solution.py:227
  14.2 0.0 collective-permute-done.10
  14.2 0.9 %bitcast_add_fusion.4 = f32[2,2,64,128]{3,2,1,0:T(8,128)S(1)} fusion(f32[2,2,64,128]{3,2,1,0:T(8,128)S(1)} %collective-permute-done.10, f32[2,2,2,64,128]{4,3,2,1,0:T(8,128)} %bitcast.66, s32[]{:T(128)S(6)} %select_n.87), kind=kLoop, calls=%fused_computation.11 | loop fusion | flops 32768 | bytes 393220 | tf_op jit(solution)/shard_map/add | solution.py:312
  15.2 1.6 %collective-permute-start.11 = (f32[1,2,64,128]{3,2,1,0:T(8,128)S(1)}, f32[1,2,64,128]{3,2,1,0:T(8,128)S(1)}, u32[]{:S(2)}, u32[]{:S(2)}) collective-permute-start(f32[1,2,64,128]{3,2,1,0:T(8,128)S(1)} %constant_dynamic-slice_fusion), channel_id=1, source_target_pairs={{0,16},{16,0},{1,17},{17,1},{2,18},{18,2},{3,19},{19,3},{4,20},{20... | collective-permute-start | bytes 196616 | tf_op jit(solution)/shard_map/ppermute | solution.py:227
  16.8 0.0 collective-permute-done.5
  16.8 1.9 %collective-permute-start.6 = (f32[2,64,128]{2,1,0:T(8,128)S(1)}, f32[2,64,128]{2,1,0:T(8,128)S(1)}, u32[]{:S(2)}, u32[]{:S(2)}) collective-permute-start(f32[2,64,128]{2,1,0:T(8,128)S(1)} %add.126), channel_id=1, source_target_pairs={{0,4},{1,5},{2,6},{3,7},{4,0},{5,1},{6,2},{7,3},{8,12},{9,13},{10,... | collective-permute-start | bytes 196616 | tf_op jit(solution)/shard_map/ppermute | solution.py:227
  18.7 0.9 %collective-permute-done.11 = f32[1,2,64,128]{3,2,1,0:T(8,128)S(1)} collective-permute-done((f32[1,2,64,128]{3,2,1,0:T(8,128)S(1)}, f32[1,2,64,128]{3,2,1,0:T(8,128)S(1)}, u32[]{:S(2)}, u32[]{:S(2)}) %collective-permute-start.11) | collective-permute-done | bytes 65568 | tf_op jit(solution)/shard_map/ppermute | solution.py:227
  19.5 1.1 %collective-permute-start.12 = (f32[2,64,128]{2,1,0:T(8,128)S(1)}, f32[2,64,128]{2,1,0:T(8,128)S(1)}, u32[]{:S(2)}, u32[]{:S(2)}) collective-permute-start(f32[2,64,128]{2,1,0:T(8,128)S(1)} %add_bitcast_fusion), channel_id=1, source_target_pairs={{0,2},{1,3},{2,0},{3,1},{4,6},{5,7},{6,4},{7,5},{8,10},{9,11},{10,... | collective-permute-start | bytes 196616 | tf_op jit(solution)/shard_map/ppermute | solution.py:227
  20.6 0.5 collective-permute-done.6
  21.1 2.9 %collective-permute-start.7 = (f32[2,64,128]{2,1,0:T(8,128)S(1)}, f32[2,64,128]{2,1,0:T(8,128)S(1)}, u32[]{:S(2)}, u32[]{:S(2)}) collective-permute-start(f32[2,64,128]{2,1,0:T(8,128)S(1)} %add.127), channel_id=1, source_target_pairs={{0,8},{1,9},{2,10},{3,11},{4,12},{5,13},{6,14},{7,15},{8,0},{9,1},... | collective-permute-start | bytes 196616 | tf_op jit(solution)/shard_map/ppermute | solution.py:227
  24.0 0.0 collective-permute-done.12
  24.0 1.9 %collective-permute-start.13 = (f32[2,64,128]{2,1,0:T(8,128)S(1)}, f32[2,64,128]{2,1,0:T(8,128)S(1)}, u32[]{:S(2)}, u32[]{:S(2)}) collective-permute-start(f32[2,64,128]{2,1,0:T(8,128)S(1)} %add.138), channel_id=1, source_target_pairs={{0,4},{1,5},{2,6},{3,7},{4,0},{5,1},{6,2},{7,3},{8,12},{9,13},{10,... | collective-permute-start | bytes 196616 | tf_op jit(solution)/shard_map/ppermute | solution.py:227
  25.9 0.4 collective-permute-done.7
  26.4 0.1 collective-permute-start.8
  26.5 1.9 %collective-permute-done.13 = f32[2,64,128]{2,1,0:T(8,128)S(1)} collective-permute-done((f32[2,64,128]{2,1,0:T(8,128)S(1)}, f32[2,64,128]{2,1,0:T(8,128)S(1)}, u32[]{:S(2)}, u32[]{:S(2)}) %collective-permute-start.13) | collective-permute-done | bytes 65568 | tf_op jit(solution)/shard_map/ppermute | solution.py:227
  28.4 2.5 %collective-permute-start.14 = (f32[2,64,128]{2,1,0:T(8,128)S(1)}, f32[2,64,128]{2,1,0:T(8,128)S(1)}, u32[]{:S(2)}, u32[]{:S(2)}) collective-permute-start(f32[2,64,128]{2,1,0:T(8,128)S(1)} %add.139), channel_id=1, source_target_pairs={{0,8},{1,9},{2,10},{3,11},{4,12},{5,13},{6,14},{7,15},{8,0},{9,1},... | collective-permute-start | bytes 196616 | tf_op jit(solution)/shard_map/ppermute | solution.py:227
  30.9 0.0 collective-permute-done.8.refs_4_
  30.9 0.6 copy-done.6
  31.5 4.9 %integral_row.1 = f32[16,64,128]{2,1,0:T(8,128)} custom-call(f32[8]{0:T(128)} %refs_0_.3, s32[4]{0:T(128)} %refs_1_.3, s32[1]{0:T(128)} %bitcast.refs_2_, f32[2,64,128]{2,1,0:T(8,128)} %copy-done.4, f32[2,64,128]{2,1,0:T(8,128)} %copy-done.6, f32[4,16,64,128]{3,2,1,0:T(8,128)} %refs_5_.3), custom_call_target="tpu_custom_call" | custom-call | tf_op jit(solution)/shard_map/integral_row/pallas_call | solution.py:172
  36.5 0.1 collective-permute-start.15
  36.6 0.0 copy-start
  36.6 1.0 %dynamic-slice_bitcast_fusion.1 = f32[1,8,64,128]{3,2,1,0:T(8,128)S(1)} fusion(f32[2,1,8,64,128]{4,3,2,1,0:T(8,128)} %bitcast.61, s32[]{:T(128)S(6)} %select_n.90), kind=kLoop, calls=%fused_computation.10 | loop fusion | bytes 524292 | tf_op jit(solution)/shard_map/jit(dynamic_index_in_dim)/squeeze | solution.py:231
  37.6 1.6 %collective-permute-start.9 = (f32[1,8,64,128]{3,2,1,0:T(8,128)S(1)}, f32[1,8,64,128]{3,2,1,0:T(8,128)S(1)}, u32[]{:S(2)}, u32[]{:S(2)}) collective-permute-start(f32[1,8,64,128]{3,2,1,0:T(8,128)S(1)} %dynamic-slice_bitcast_fusion.1), channel_id=1, source_target_pairs={{0,16},{16,0},{1,17},{17,1},{2,18},{18,2},{3,19},{19,3},{4,20},{20... | collective-permute-start | bytes 786440 | tf_op jit(solution)/shard_map/ppermute | solution.py:227
  39.2 0.0 collective-permute-done.15.refs_4_
  39.2 0.6 copy-done.5
  39.9 4.9 %integral_pred.1 = f32[16,64,128]{2,1,0:T(8,128)} custom-call(f32[8]{0:T(128)} %refs_0_.3, s32[4]{0:T(128)} %refs_1_.3, s32[1]{0:T(128)} %bitcast.refs_2_, f32[2,64,128]{2,1,0:T(8,128)} %copy-done.3, f32[2,64,128]{2,1,0:T(8,128)} %copy-done.5, f32[4,16,64,128]{3,2,1,0:T(8,128)} %refs_5_.3), custom_call_target="tpu_custom_call" | custom-call | tf_op jit(solution)/shard_map/integral_pred/pallas_call | solution.py:172
  44.8 1.0 %dynamic-slice_bitcast_fusion = f32[1,8,64,128]{3,2,1,0:T(8,128)S(1)} fusion(f32[2,1,8,64,128]{4,3,2,0,1:T(8,128)} %bitcast.63, s32[]{:T(128)S(6)} %select_n.90), kind=kLoop, calls=%fused_computation.9 | loop fusion | bytes 524292 | tf_op jit(solution)/shard_map/jit(dynamic_index_in_dim)/squeeze | solution.py:231
  45.8 0.6 collective-permute-start.16
  46.4 0.7 %constant_dynamic-slice_fusion.1.row_ref = f32[8,64,128]{2,1,0:T(8,128)} fusion(f32[16,64,128]{2,1,0:T(8,128)S(1)} %copy-done.2, s32[]{:T(128)S(6)} %select_n.84), kind=kLoop, calls=%fused_computation.20 | loop fusion | bytes 524292 | tf_op jit(solution)/shard_map/dynamic_slice | solution.py:317
  47.1 0.0 collective-permute-done.9
  47.2 0.7 %fusion.3.sum_ref = f32[8,64,128]{2,1,0:T(8,128)} fusion(f32[1,8,64,128]{3,2,1,0:T(8,128)S(1)} %collective-permute-done.9, f32[2,1,8,64,128]{4,3,2,1,0:T(8,128)S(1)} %bitcast.62, s32[]{:T(128)S(6)} %select_n.89), kind=kLoop, calls=%fused_computation.8 | loop fusion | flops 65536 | bytes 786436 | tf_op jit(solution)/shard_map/squeeze | solution.py:243
  47.9 2.7 %share_bases.1 = (f32[8,64,128]{2,1,0:T(8,128)}, f32[8,64,128]{2,1,0:T(8,128)}) custom-call(f32[8,64,128]{2,1,0:T(8,128)} %constant_dynamic-slice_fusion.1.row_ref, f32[8,64,128]{2,1,0:T(8,128)} %fusion.3.sum_ref, f32[128,64]{1,0:T(8,128)} %get-tuple-element.18.herm_ref.refs_7_), custom_call_target="tpu_custom_call" | custom-call | tf_op jit(solution)/shard_map/share_bases/pallas_call | solution.py:216
  50.6 3.7 %collective-permute-done.16 = f32[1,8,64,128]{3,2,1,0:T(8,128)S(1)} collective-permute-done((f32[1,8,64,128]{3,2,1,0:T(8,128)S(1)}, f32[1,8,64,128]{3,2,1,0:T(8,128)S(1)}, u32[]{:S(2)}, u32[]{:S(2)}) %collective-permute-start.16) | collective-permute-done | bytes 262176 | tf_op jit(solution)/shard_map/ppermute | solution.py:227
  54.3 1.7 %fusion.2 = (f32[]{:T(128)}, f32[1,8,64,128]{3,2,1,0:T(8,128)S(1)}) fusion(f32[8,64,128]{2,1,0:T(8,128)} %get-tuple-element.20, f32[1,8,64,128]{3,2,1,0:T(8,128)S(1)} %collective-permute-done.16, f32[2,1,8,64,128]{4,3,2,0,1:T(8,128)S(1)} %bitcast.64, s32[]{:T(128)S(6)} %select_n.89, f32[8,64,128]{2,1,0:T(8,128)} %get-tuple-element.19), kind=kLoop, calls=%fused_computation.5 | loop fusion | flops 327679 | bytes 1310728 | tf_op jit(solution)/shard_map/reduce_sum | solution.py:331
  56.0 0.5 collective-permute-start.17
  56.5 1.3 %broadcast_in_dim.9 = f32[32,1,128]{2,1,0:T(1,128)} broadcast(f32[]{:T(128)} %get-tuple-element.21), dimensions={} | broadcast | bytes 16388 | tf_op jit(solution)/shard_map/broadcast_in_dim | solution.py:335
  57.8 3.7 %all-to-all-start = ((f32[32,1,128]{2,1,0:T(1,128)}), f32[32,1,128]{2,1,0:T(1,128)S(1)}, u32[]{:S(2)}, u32[]{:S(2)}) async-start(f32[32,1,128]{2,1,0:T(1,128)} %broadcast_in_dim.9), calls=%async_computation | async-start | bytes 32768 | tf_op jit(solution)/shard_map/all_to_all | solution.py:336
  61.6 7.1 %all-to-all-done = f32[32,1,128]{2,1,0:T(1,128)S(1)} async-done(((f32[32,1,128]{2,1,0:T(1,128)}), f32[32,1,128]{2,1,0:T(1,128)S(1)}, u32[]{:S(2)}, u32[]{:S(2)}) %all-to-all-start) | async-done | bytes 16416 | tf_op jit(solution)/shard_map/all_to_all | solution.py:336
  68.7 0.6 slice_reduce_fusion
  70.0 0.8 %pad_maximum_fusion = f32[2,8,64,128]{3,2,1,0:T(8,128)} fusion(f32[1,8,64,128]{3,2,1,0:T(8,128)S(1)} %get-tuple-element.24, f32[1,8,64,128]{3,2,1,0:T(8,128)S(1)} %get-tuple-element.23), kind=kLoop, calls=%fused_computation | loop fusion | flops 131072 | bytes 1048576 | tf_op jit(solution)/shard_map/concatenate | solution.py:254
  (32 shorter events, 0.2 us)
Async XLA Ops:
  1.3 3.9 %copy-start.7 = (s32[8]{0:T(128)}, s32[8]{0:T(128)S(1)}, u32[]{:S(2)}) copy-start(s32[8]{0:T(128)S(1)} %fusion.4.refs_0_) | copy-start | bytes 100
  1.3 3.9 %copy-start.8 = (s32[8]{0:T(128)}, s32[8]{0:T(128)S(1)}, u32[]{:S(2)}) copy-start(s32[8]{0:T(128)S(1)} %and_convert_fusion.refs_1_) | copy-start | bytes 100
  4.6 6.7 %collective-permute-start.4 = (f32[2,64,128]{2,1,0:T(8,128)S(1)}, f32[2,64,128]{2,1,0:T(8,128)S(1)}, u32[]{:S(2)}, u32[]{:S(2)}) collective-permute-start(f32[2,64,128]{2,1,0:T(8,128)S(1)} %dynamic-slice_bitcast_fusion.3), channel_id=1, source_target_pairs={{0,1},{1,0},{2,3},{3,2},{4,5},{5,4},{6,7},{7,6},{8,9},{9,8},{10,11... | collective-permute-start | bytes 196616 | tf_op jit(solution)/shard_map/ppermute | solution.py:227
  11.1 3.1 %collective-permute-start.10 = (f32[2,2,64,128]{3,2,1,0:T(8,128)S(1)}, f32[2,2,64,128]{3,2,1,0:T(8,128)S(1)}, u32[]{:S(2)}, u32[]{:S(2)}) collective-permute-start(f32[2,2,64,128]{3,2,1,0:T(8,128)S(1)} %dynamic-slice_bitcast_fusion.2), channel_id=1, source_target_pairs={{0,1},{1,0},{2,3},{3,2},{4,5},{5,4},{6,7},{7,6},{8,9},{9,8},{10,11... | collective-permute-start | bytes 393224 | tf_op jit(solution)/shard_map/ppermute | solution.py:227
  11.3 5.5 %collective-permute-start.5 = (f32[2,64,128]{2,1,0:T(8,128)S(1)}, f32[2,64,128]{2,1,0:T(8,128)S(1)}, u32[]{:S(2)}, u32[]{:S(2)}) collective-permute-start(f32[2,64,128]{2,1,0:T(8,128)S(1)} %bitcast_add_fusion.5), channel_id=1, source_target_pairs={{0,2},{1,3},{2,0},{3,1},{4,6},{5,7},{6,4},{7,5},{8,10},{9,11},{10,... | collective-permute-start | bytes 196616 | tf_op jit(solution)/shard_map/ppermute | solution.py:227
  15.2 4.3 %collective-permute-start.11 = (f32[1,2,64,128]{3,2,1,0:T(8,128)S(1)}, f32[1,2,64,128]{3,2,1,0:T(8,128)S(1)}, u32[]{:S(2)}, u32[]{:S(2)}) collective-permute-start(f32[1,2,64,128]{3,2,1,0:T(8,128)S(1)} %constant_dynamic-slice_fusion), channel_id=1, source_target_pairs={{0,16},{16,0},{1,17},{17,1},{2,18},{18,2},{3,19},{19,3},{4,20},{20... | collective-permute-start | bytes 196616 | tf_op jit(solution)/shard_map/ppermute | solution.py:227
  16.8 4.3 %collective-permute-start.6 = (f32[2,64,128]{2,1,0:T(8,128)S(1)}, f32[2,64,128]{2,1,0:T(8,128)S(1)}, u32[]{:S(2)}, u32[]{:S(2)}) collective-permute-start(f32[2,64,128]{2,1,0:T(8,128)S(1)} %add.126), channel_id=1, source_target_pairs={{0,4},{1,5},{2,6},{3,7},{4,0},{5,1},{6,2},{7,3},{8,12},{9,13},{10,... | collective-permute-start | bytes 196616 | tf_op jit(solution)/shard_map/ppermute | solution.py:227
  19.5 4.5 %collective-permute-start.12 = (f32[2,64,128]{2,1,0:T(8,128)S(1)}, f32[2,64,128]{2,1,0:T(8,128)S(1)}, u32[]{:S(2)}, u32[]{:S(2)}) collective-permute-start(f32[2,64,128]{2,1,0:T(8,128)S(1)} %add_bitcast_fusion), channel_id=1, source_target_pairs={{0,2},{1,3},{2,0},{3,1},{4,6},{5,7},{6,4},{7,5},{8,10},{9,11},{10,... | collective-permute-start | bytes 196616 | tf_op jit(solution)/shard_map/ppermute | solution.py:227
  21.1 5.2 %collective-permute-start.7 = (f32[2,64,128]{2,1,0:T(8,128)S(1)}, f32[2,64,128]{2,1,0:T(8,128)S(1)}, u32[]{:S(2)}, u32[]{:S(2)}) collective-permute-start(f32[2,64,128]{2,1,0:T(8,128)S(1)} %add.127), channel_id=1, source_target_pairs={{0,8},{1,9},{2,10},{3,11},{4,12},{5,13},{6,14},{7,15},{8,0},{9,1},... | collective-permute-start | bytes 196616 | tf_op jit(solution)/shard_map/ppermute | solution.py:227
  24.0 4.3 %collective-permute-start.13 = (f32[2,64,128]{2,1,0:T(8,128)S(1)}, f32[2,64,128]{2,1,0:T(8,128)S(1)}, u32[]{:S(2)}, u32[]{:S(2)}) collective-permute-start(f32[2,64,128]{2,1,0:T(8,128)S(1)} %add.138), channel_id=1, source_target_pairs={{0,4},{1,5},{2,6},{3,7},{4,0},{5,1},{6,2},{7,3},{8,12},{9,13},{10,... | collective-permute-start | bytes 196616 | tf_op jit(solution)/shard_map/ppermute | solution.py:227
  26.4 4.5 %copy-start.4 = (f32[2,64,128]{2,1,0:T(8,128)}, f32[2,64,128]{2,1,0:T(8,128)S(1)}, u32[]{:S(2)}) copy-start(f32[2,64,128]{2,1,0:T(8,128)S(1)} %add.128.refs_3_) | copy-start | bytes 196612
  26.4 4.5 %collective-permute-start.8 = (f32[2,64,128]{2,1,0:T(8,128)S(1)}, f32[2,64,128]{2,1,0:T(8,128)S(1)}, u32[]{:S(2)}, u32[]{:S(2)}) collective-permute-start(f32[2,64,128]{2,1,0:T(8,128)S(1)} %add.128.refs_3_), channel_id=1, source_target_pairs={{0,1},{1,0},{2,3},{3,2},{4,5},{5,4},{6,7},{7,6},{8,9},{9,8},{10,11... | collective-permute-start | bytes 196616 | tf_op jit(solution)/shard_map/ppermute | solution.py:227
  28.4 8.1 %collective-permute-start.14 = (f32[2,64,128]{2,1,0:T(8,128)S(1)}, f32[2,64,128]{2,1,0:T(8,128)S(1)}, u32[]{:S(2)}, u32[]{:S(2)}) collective-permute-start(f32[2,64,128]{2,1,0:T(8,128)S(1)} %add.139), channel_id=1, source_target_pairs={{0,8},{1,9},{2,10},{3,11},{4,12},{5,13},{6,14},{7,15},{8,0},{9,1},... | collective-permute-start | bytes 196616 | tf_op jit(solution)/shard_map/ppermute | solution.py:227
  30.9 0.6 copy-start.6
  36.5 10.0 %copy-start.2 = (f32[16,64,128]{2,1,0:T(8,128)S(1)}, f32[16,64,128]{2,1,0:T(8,128)}, u32[]{:S(2)}) copy-start(f32[16,64,128]{2,1,0:T(8,128)} %row_ref.1) | copy-start | bytes 1572868
  36.5 2.7 %copy-start.3 = (f32[2,64,128]{2,1,0:T(8,128)}, f32[2,64,128]{2,1,0:T(8,128)S(1)}, u32[]{:S(2)}) copy-start(f32[2,64,128]{2,1,0:T(8,128)S(1)} %add.140.refs_3_) | copy-start | bytes 196612
  36.5 2.7 %collective-permute-start.15 = (f32[2,64,128]{2,1,0:T(8,128)S(1)}, f32[2,64,128]{2,1,0:T(8,128)S(1)}, u32[]{:S(2)}, u32[]{:S(2)}) collective-permute-start(f32[2,64,128]{2,1,0:T(8,128)S(1)} %add.140.refs_3_), channel_id=1, source_target_pairs={{0,1},{1,0},{2,3},{3,2},{4,5},{5,4},{6,7},{7,6},{8,9},{9,8},{10,11... | collective-permute-start | bytes 196616 | tf_op jit(solution)/shard_map/ppermute | solution.py:227
  36.6 10.6 %copy-start = (f32[16,64,128]{2,1,0:T(8,128)S(1)}, f32[16,64,128]{2,1,0:T(8,128)}, u32[]{:S(2)}) copy-start(f32[16,64,128]{2,1,0:T(8,128)} %integral_row.1) | copy-start | bytes 1572868
  37.6 9.5 %collective-permute-start.9 = (f32[1,8,64,128]{3,2,1,0:T(8,128)S(1)}, f32[1,8,64,128]{3,2,1,0:T(8,128)S(1)}, u32[]{:S(2)}, u32[]{:S(2)}) collective-permute-start(f32[1,8,64,128]{3,2,1,0:T(8,128)S(1)} %dynamic-slice_bitcast_fusion.1), channel_id=1, source_target_pairs={{0,16},{16,0},{1,17},{17,1},{2,18},{18,2},{3,19},{19,3},{4,20},{20... | collective-permute-start | bytes 786440 | tf_op jit(solution)/shard_map/ppermute | solution.py:227
  39.2 0.6 copy-start.5
  44.8 9.5 %copy-start.1 = (f32[16,64,128]{2,1,0:T(8,128)S(1)}, f32[16,64,128]{2,1,0:T(8,128)}, u32[]{:S(2)}) copy-start(f32[16,64,128]{2,1,0:T(8,128)} %integral_pred.1) | copy-start | bytes 1572868
  45.8 8.5 %collective-permute-start.16 = (f32[1,8,64,128]{3,2,1,0:T(8,128)S(1)}, f32[1,8,64,128]{3,2,1,0:T(8,128)S(1)}, u32[]{:S(2)}, u32[]{:S(2)}) collective-permute-start(f32[1,8,64,128]{3,2,1,0:T(8,128)S(1)} %dynamic-slice_bitcast_fusion), channel_id=1, source_target_pairs={{0,16},{16,0},{1,17},{17,1},{2,18},{18,2},{3,19},{19,3},{4,20},{20... | collective-permute-start | bytes 786440 | tf_op jit(solution)/shard_map/ppermute | solution.py:227
  56.0 13.9 %collective-permute-start.17 = (f32[1,8,64,128]{3,2,1,0:T(8,128)S(1)}, f32[1,8,64,128]{3,2,1,0:T(8,128)S(1)}, u32[]{:S(2)}, u32[]{:S(2)}) collective-permute-start(f32[1,8,64,128]{3,2,1,0:T(8,128)S(1)} %get-tuple-element.22), channel_id=1, source_target_pairs={{0,16},{16,0},{1,17},{17,1},{2,18},{18,2},{3,19},{19,3},{4,20},{20... | collective-permute-start | bytes 786440 | tf_op jit(solution)/shard_map/ppermute | solution.py:227
  57.8 10.9 %all-to-all-start = ((f32[32,1,128]{2,1,0:T(1,128)}), f32[32,1,128]{2,1,0:T(1,128)S(1)}, u32[]{:S(2)}, u32[]{:S(2)}) async-start(f32[32,1,128]{2,1,0:T(1,128)} %broadcast_in_dim.9), calls=%async_computation | async-start | bytes 32768 | tf_op jit(solution)/shard_map/all_to_all | solution.py:336

commit v2 on v1

v2 whole, which is shorter than its diff:
```python
import math

import jax
import jax.numpy as jnp
from jax import lax
from jax.experimental import pallas as pl
from jax.experimental.pallas import tpu as pltpu
from jax.sharding import PartitionSpec as P

coupling = 0.5
step_size = 0.25

f32 = jnp.float32
bf16 = jnp.bfloat16
SMEM_SPEC = pl.BlockSpec(memory_space=pltpu.SMEM)
VMEM_SPEC = pl.BlockSpec(memory_space=pltpu.VMEM)
PARAMS = pltpu.CompilerParams(vmem_limit_bytes=12 << 20)


def split(value):
    high = value.astype(bf16)
    return high, (value - high.astype(f32)).astype(bf16)


def dot3(left, right):
    def one(a, b):
        return jnp.dot(a, b, preferred_element_type=f32)

    return one(left[0], right[0]) + (one(left[0], right[1]) + one(left[1], right[0]))


def swap_halves(tile):
    return pltpu.roll(tile, tile.shape[-1] // 2, tile.ndim - 1)


def is_real(shape):
    return lax.broadcasted_iota(jnp.int32, shape, len(shape) - 1) < shape[-1] // 2


def self_energy(tile):
    square = tile * tile
    return -coupling * (square + swap_halves(square)) * tile


def minus_i_times(acc, orbits):
    turned = swap_halves(acc[:orbits])
    return acc[orbits:] + jnp.where(is_real(turned.shape), turned, -turned)


def left_factor(tile, weight):
    scaled = weight * self_energy(tile)
    plain = weight * tile
    real = is_real(tile.shape)
    return jnp.concatenate(
        [jnp.where(real, scaled, swap_halves(plain)), jnp.where(real, swap_halves(scaled), plain)], axis=0
    )


def local_spot(start_ref, tile, sec_rows):
    spot = start_ref[0] - lax.axis_index("second") * sec_rows + tile
    return jnp.clip(spot, 0, sec_rows - 1), (spot >= 0) & (spot < sec_rows)


def prepare_kernel(start_ref, row_ref, ham_ref, window_ref, keep_ref, send_ref, herm_ref):
    count = window_ref.shape[0]
    half = count // 2
    orbits = ham_ref.shape[0]
    first = lax.axis_index("past") * count
    odd = lax.axis_index("second") % 2
    for p in range(count):
        pos, inside = local_spot(start_ref, first + p, row_ref.shape[0])
        window_ref[p] = jnp.where(inside, row_ref[pos], 0.0)
    for p in range(half):
        keep_ref[p] = window_ref[odd * half + p]
        send_ref[p] = window_ref[(1 - odd) * half + p]
    real = ham_ref[:, :orbits]
    imag = ham_ref[:, orbits:]
    herm_ref[...] = jnp.concatenate([0.5 * (real + real.T), 0.5 * (imag - imag.T)], axis=0)


def prepare(block_start, green_row, hamiltonian, count):
    orbits = hamiltonian.shape[0]
    tile = green_row.shape[1:]
    half = jax.ShapeDtypeStruct((count // 2,) + tile, f32)
    return pl.pallas_call(
        prepare_kernel,
        in_specs=[SMEM_SPEC, VMEM_SPEC, VMEM_SPEC],
        out_specs=[VMEM_SPEC] * 4,
        out_shape=[
            jax.ShapeDtypeStruct((count,) + tile, f32),
            half,
            half,
            jax.ShapeDtypeStruct((2 * orbits, orbits), f32),
        ],
        compiler_params=PARAMS,
        name="prepare",
    )(block_start, green_row, hamiltonian)


def right_kernel(hist_ref, high_ref, low_ref):
    past_rows, sec_rows, orbits, _ = hist_ref.shape

    def body(s, carry):
        for p in range(past_rows):
            tile = hist_ref[p, s]
            for q, part in enumerate((tile, self_energy(tile))):
                rows = slice((2 * p + q) * orbits, (2 * p + q + 1) * orbits)
                high_ref[s, rows], low_ref[s, rows] = split(part)
        return carry

    lax.fori_loop(0, sec_rows, body, 0, unroll=2)


def right_factors(green_hist):
    past_rows, sec_rows, orbits, width = green_hist.shape
    shape = jax.ShapeDtypeStruct((sec_rows, past_rows * 2 * orbits, width), bf16)
    return pl.pallas_call(
        right_kernel,
        in_specs=[VMEM_SPEC],
        out_specs=[VMEM_SPEC] * 2,
        out_shape=[shape, shape],
        compiler_params=PARAMS,
        name="right_factors",
    )(green_hist)


def put_left(left_high, left_low, p, tile, weight):
    width = tile.shape[-1]
    cols = slice(p * width, (p + 1) * width)
    left_high[:, cols], left_low[:, cols] = split(left_factor(tile, weight))


def contract(left, high_ref, low_ref, first, second):
    high = jnp.concatenate([high_ref[first], high_ref[second]], axis=1)
    low = jnp.concatenate([low_ref[first], low_ref[second]], axis=1)
    return dot3(left, (high, low))


def owner_kernel(
    start_ref, quad_ref, index_ref, win_ref, base_ref, herm_ref, high_ref, low_ref, keep_ref, send_ref, lh, ll, *, scale
):
    past_rows, orbits, width = win_ref.shape
    half = past_rows // 2
    sec_rows = high_ref.shape[0]
    odd = lax.axis_index("second") % 2
    past = lax.axis_index("past")
    for p in range(past_rows):
        put_left(lh, ll, p, win_ref[p], quad_ref[index_ref[p]])
    left = (lh[...], ll[...])
    for out_ref, side in ((send_ref, 1 - odd), (keep_ref, odd)):
        for g in range(out_ref.shape[0]):
            for t in range(0, half, 2):
                spots = [local_spot(start_ref, g * past_rows + side * half + t + q, sec_rows) for q in range(2)]
                acc = contract(left, high_ref, low_ref, spots[0][0], spots[1][0])
                for q in range(2):
                    value = step_size * scale * minus_i_times(acc[:, q * width : (q + 1) * width], orbits)
                    out_ref[g, t + q] = jnp.where(spots[q][1], value, 0.0)
        herm = split(herm_ref[...])
        for t in range(0, half, 2):
            base = jnp.concatenate([base_ref[side * half + t + q] for q in range(2)], axis=1)
            acc = dot3(herm, split(base))
            for q in range(2):
                cols = slice(q * width, (q + 1) * width)
                out_ref[past, t + q] += base[:, cols] + step_size * minus_i_times(acc[:, cols], orbits)


def owner_part(block_start, quad_table, weight_index, window, base, herm, high, low, past_size, scale):
    past_rows, orbits, width = window.shape
    shape = jax.ShapeDtypeStruct((past_size, past_rows // 2, orbits, width), f32)
    return pl.pallas_call(
        lambda *refs: owner_kernel(*refs, scale=scale),
        in_specs=[SMEM_SPEC] * 3 + [VMEM_SPEC] * 5,
        out_specs=[VMEM_SPEC] * 2,
        out_shape=[shape, shape],
        scratch_shapes=[pltpu.VMEM((2 * orbits, past_rows * width), bf16)] * 2,
        compiler_params=PARAMS,
        name="owner_part",
    )(block_start, quad_table, weight_index, window, base, herm, high, low)


def past_half(past_size):
    return lax.axis_index("past") // (past_size // 2) % 2


def integral_kernel(quad_ref, index_ref, mine_ref, other_ref, high_ref, low_ref, *refs, scale, sides, past_size):
    outs, (lh, ll) = refs[: len(sides)], refs[len(sides) :]
    half, orbits, width = mine_ref.shape
    past_rows = 2 * half
    odd = lax.axis_index("second") % 2
    for p in range(past_rows):
        tile = jnp.where(odd == p // half, mine_ref[p % half], other_ref[p % half])
        put_left(lh, ll, p, tile, quad_ref[index_ref[p]])
    left = (lh[...], ll[...])
    for out_ref, kept in zip(outs, sides):
        count = out_ref.shape[0]
        upper = past_half(past_size)
        first = (upper if kept else 1 - upper) * count
        for s in range(0, count, 2):
            acc = contract(left, high_ref, low_ref, first + s, first + s + 1)
            for q in range(2):
                out_ref[s + q] = scale * minus_i_times(acc[:, q * width : (q + 1) * width], orbits)


def integral(quad_table, weight_index, mine, other, high, low, past_size, sides, scale, name):
    half, orbits, width = mine.shape
    shape = jax.ShapeDtypeStruct((high.shape[0] // 2, orbits, width), f32)
    return pl.pallas_call(
        lambda *refs: integral_kernel(*refs, scale=scale, sides=sides, past_size=past_size),
        in_specs=[SMEM_SPEC] * 2 + [VMEM_SPEC] * 4,
        out_specs=[VMEM_SPEC] * len(sides),
        out_shape=[shape] * len(sides),
        scratch_shapes=[pltpu.VMEM((2 * orbits, 2 * half * width), bf16)] * 2,
        compiler_params=PARAMS,
        name=name,
    )(quad_table, weight_index, mine, other, high, low)


def share_kernel(row_ref, mine_ref, recv_ref, herm_ref, out_base_ref, diff_base_ref):
    share, orbits, width = mine_ref.shape
    first = lax.axis_index("past") * share
    herm = split(herm_ref[...])
    for s in range(0, share, 2):

        def pair(ref, start=0):
            return jnp.concatenate([ref[start + s], ref[start + s + 1]], axis=1)

        def ham(value):
            acc = dot3(herm, split(value))
            return jnp.concatenate(
                [minus_i_times(acc[:, q * width : (q + 1) * width], orbits) for q in range(2)], axis=1
            )

        row = pair(row_ref, first)
        slope = ham(row) + (pair(mine_ref) + pair(recv_ref))
        turned = ham(row + step_size * slope)
        out_base = row + 0.5 * step_size * (slope + turned)
        diff_base = 0.5 * step_size * (turned - slope)
        for q in range(2):
            cols = slice(q * width, (q + 1) * width)
            out_base_ref[s + q] = out_base[:, cols]
            diff_base_ref[s + q] = diff_base[:, cols]


def share_bases(green_row, mine, recv, herm):
    shape = jax.ShapeDtypeStruct(mine.shape, f32)
    return pl.pallas_call(
        share_kernel,
        in_specs=[VMEM_SPEC] * 4,
        out_specs=[VMEM_SPEC] * 2,
        out_shape=[shape, shape],
        compiler_params=PARAMS,
        name="share_bases",
    )(green_row, mine, recv, herm)


def finish_kernel(out_base_ref, diff_base_ref, mine_ref, recv_ref, out_ref, square_ref):
    total = jnp.zeros(out_ref.shape[1:], f32)
    for s in range(out_ref.shape[0]):
        last = mine_ref[s] + recv_ref[s]
        out_ref[s] = out_base_ref[s] + last
        diff = diff_base_ref[s] + last
        total = total + diff * diff
    square_ref[...] = jnp.broadcast_to(jnp.sum(total), square_ref.shape)


def finish(out_base, diff_base, mine, recv, devices):
    return pl.pallas_call(
        finish_kernel,
        in_specs=[VMEM_SPEC] * 4,
        out_specs=[VMEM_SPEC] * 2,
        out_shape=[jax.ShapeDtypeStruct(mine.shape, f32), jax.ShapeDtypeStruct((devices, 128), f32)],
        compiler_params=PARAMS,
        name="finish",
    )(out_base, diff_base, mine, recv)


def exchange(value, axis, mask):
    size = lax.axis_size(axis)
    return lax.ppermute(value, axis, [(i, i ^ mask) for i in range(size)])


def pick(value, index, axis=0):
    return lax.dynamic_index_in_dim(value, index, axis, keepdims=False)


def halve_past(value):
    size = value.shape[0]
    half = size // 2
    upper = lax.axis_index("past") // half % 2
    value = value.reshape((2, half) + value.shape[1:])
    return pick(value, upper), exchange(pick(value, 1 - upper), "past", half)


def scatter_past(value):
    while value.shape[0] > 1:
        own, received = halve_past(value)
        value = own + received
    return value[0]


def share_past(keep, send):
    half = lax.axis_size("past") // 2
    received = exchange(send, "past", half)
    while half > 1:
        keep = (keep + received).reshape((half, keep.shape[0] // half) + keep.shape[1:])
        keep, received = halve_past(keep)
        half //= 2
        keep, received = keep.reshape((-1,) + keep.shape[2:]), received.reshape((-1,) + received.shape[2:])
    return keep, received


def gather_past(value):
    size = lax.axis_size("past")
    index = lax.axis_index("past")
    value = value[None]
    mask = 1
    while mask < size:
        other = exchange(value, "past", mask)
        upper = (index // mask) % 2 == 1
        value = jnp.concatenate([jnp.where(upper, other, value), jnp.where(upper, value, other)], axis=0)
        mask *= 2
    return value


def spread_second(value):
    mask = 2
    while mask < lax.axis_size("second"):
        value = value + exchange(value, "second", mask)
        mask *= 2
    return value


def local(green_row, green_hist, hamiltonian, quad_table, weight_index, block_start):
    past_rows, sec_rows, orbits, width = green_hist.shape
    past_size = lax.axis_size("past")
    second_size = lax.axis_size("second")
    total_past = past_rows * past_size
    scale = 1.0 / math.sqrt(orbits * total_past)

    own_window, row_keep, row_send, herm = prepare(block_start, green_row, hamiltonian, past_rows)
    high, low = right_factors(green_hist)

    owner = block_start[0] // sec_rows
    crossing = (block_start[0] + total_past - 1) // sec_rows > owner
    flips = owner ^ (owner + 1)
    branch = jnp.where(crossing, 1, 0)
    masks = []
    while 2 ** len(masks) < second_size:
        masks.append(2 ** (len(masks) + 1) - 1)
    for mask in masks[:-1]:
        branch = branch + jnp.where(crossing & (flips > mask), 1, 0)
    window = lax.switch(
        branch,
        [lambda w: w] + [lambda w, mask=mask: w + exchange(w, "second", mask) for mask in masks],
        own_window,
    )
    part_keep, part_send = owner_part(
        block_start, quad_table, weight_index, window, own_window, herm, high, low, past_size, scale
    )

    row_mine = spread_second(row_keep + exchange(row_send, "second", 1))
    row_other = exchange(row_mine, "second", 1)

    pred_mine = spread_second(scatter_past(part_keep + exchange(part_send, "second", 1)))
    pred_other = exchange(pred_mine, "second", 1)

    slope_keep, slope_send = integral(
        quad_table, weight_index, row_mine, row_other, high, low, past_size, (True, False), scale, "integral_row"
    )
    out_base, diff_base = share_bases(green_row, *share_past(slope_keep, slope_send), herm)

    final = 0.5 * step_size * scale
    (last_send,) = integral(
        quad_table, weight_index, pred_mine, pred_other, high, low, past_size, (False,), final, "integral_send"
    )
    (last_keep,) = integral(
        quad_table, weight_index, pred_mine, pred_other, high, low, past_size, (True,), final, "integral_keep"
    )
    devices = past_size * second_size
    out_share, squares = finish(out_base, diff_base, *share_past(last_keep, last_send), devices)

    sums = lax.all_to_all(squares, ("past", "second"), 0, 0, tiled=True)
    green_next = gather_past(out_share).reshape(green_row.shape)
    total = jnp.sum(sums[:, :1])
    entry_count = sec_rows * second_size * orbits * width
    change = jnp.sqrt(total / entry_count) / step_size
    return (green_next, change.reshape(1))


def solution(mesh):
    placed = (P("second", None, None), P("past", "second", None, None), P(), P(), P("past"), P())
    return jax.shard_map(
        local, mesh=mesh, in_specs=placed, out_specs=(P("second", None, None), P()), check_vma=False
    )
```

time: 72.5 us -> 66.6 us (0.919)
  Pallas kernels: 19.6 us -> 8.96 us
  waiting for transfers between devices: 14.6 us -> 21.5 us
  other arithmetic: 4.93 us -> 1.58 us
  starting transfers between devices: 22 us -> 24.6 us
  local copies, waits for them, and re-layouts: 7.54 us -> 6.14 us
    pallas_call x5 -> x8, Pallas kernels: 19.6 us -> 8.96 us  [the longest x3 4.4 us: integral(): pl.pallas_call(lambda *refs: integral_kernel(*refs, scale=scale, sides=si...]
    ppermute x14, waiting for transfers between devices: 7.46 us -> 14.4 us  [exchange(): return lax.ppermute(value, axis, [(i, i ^ mask) for i in range(size)])]
    unnamed x18 -> x16, local copies, waits for them, and re-layouts: 1.3 us -> 6.12 us
    squeeze x5 -> x1, local copies, waits for them, and re-layouts: 3.02 us -> 0.01 us  [pick(): return lax.dynamic_index_in_dim(value, index, axis, keepdims=False)]
    dynamic_slice x3 -> x0, local copies, waits for them, and re-layouts: 1.96 us -> none  [the longest x1 0.72 us: local(): lax.dynamic_slice_in_dim(green_row, past_index * share_rows, share_rows, 0)]
    reduce_sum x1 -> x0, other arithmetic: 1.71 us -> none  [local(): square_sum = jnp.sum((diff_base + last_sum) ** 2)]
    all_to_all x1, starting transfers between devices: 3.75 us -> 5.34 us  [local(): sums = lax.all_to_all(squares, ('past', 'second'), 0, 0, tiled=True)]
    broadcast_in_dim x1 -> x0, local copies, waits for them, and re-layouts: 1.26 us -> none  [local(): lanes = jnp.broadcast_to(square_sum.reshape(1, 1), (devices, 128))]
  transfers between devices with their start and end apart: 15 -> 15, of which waited for: 6 -> 9; matrix products, arithmetic and copies ran while one was open for 10% -> 1% of each run, Pallas kernels for 24% -> 8%
where the time goes in v2:
time: 66.6 us; the launch traced here: 66.3 us
  starting transfers between devices  24.6 us (37%)
  waiting for transfers between devices  21.5 us (32%)
  Pallas kernels  8.96 us (13%)
  local copies, waits for them, and re-layouts  6.14 us (9%)
  between operations  3.44 us (5%)
  other arithmetic  1.58 us (2%)
    ppermute x14, starting transfers between devices, exchange(): return lax.ppermute(value, axis, [(i, i ^ mask) for i in range(size)])  19.3 us
    ppermute x14, waiting for transfers between devices, exchange(): return lax.ppermute(value, axis, [(i, i ^ mask) for i in range(size)])  14.4 us
    all_to_all x1, waiting for transfers between devices, local(): sums = lax.all_to_all(squares, ('past', 'second'), 0, 0, tiled=True)  7.1 us
    unnamed x16, local copies, waits for them, and re-layouts  6.12 us
    all_to_all x1, starting transfers between devices, local(): sums = lax.all_to_all(squares, ('past', 'second'), 0, 0, tiled=True)  5.34 us
    pallas_call x3, Pallas kernels, integral(): pl.pallas_call(lambda *refs: integral_kernel(*refs, scale=scale, sides=si...  4.4 us
    pallas_call x1, Pallas kernels, owner_part(): pl.pallas_call(lambda *refs: owner_kernel(*refs, scale=scale), in_specs=[...  1.45 us
  transfers between devices with their start and end apart: 15, of which 9 were waited for; matrix products, arithmetic and copies ran while one was open for 1% of the time, Pallas kernels for 8%

profile of v2, /device:TPU:0, one launch (start us, length us, event | category | flops | bytes accessed | tf_op | source)
XLA Modules:
  0.0 66.3 jit_solution(4206285590422893483)
XLA Ops:
  1.4 1.6 %copy-done.4 = f32[4,16,64,128]{3,2,1,0:T(8,128)S(1)} copy-done((f32[4,16,64,128]{3,2,1,0:T(8,128)S(1)}, f32[4,16,64,128]{3,2,1,0:T(8,128)}, u32[]{:S(2)}) %copy-start.4) | copy-done | bytes 2097176
  3.0 1.1 %right_factors.1 = (bf16[16,512,128]{2,1,0:T(8,128)(2,1)S(1)}, bf16[16,512,128]{2,1,0:T(8,128)(2,1)S(1)}) custom-call(f32[4,16,64,128]{3,2,1,0:T(8,128)S(1)} %copy-done.4), custom_call_target="tpu_custom_call" | custom-call | tf_op jit(solution)/shard_map/right_factors/pallas_call | solution.py:117
  4.2 0.0 copy-start
  4.2 1.3 %copy-done = bf16[16,512,128]{2,1,0:T(8,128)(2,1)} copy-done((bf16[16,512,128]{2,1,0:T(8,128)(2,1)}, bf16[16,512,128]{2,1,0:T(8,128)(2,1)S(1)}, u32[]{:S(2)}) %copy-start) | copy-done | bytes 2097176
  5.5 0.3 prepare.1
  5.9 0.0 copy-done.6
  5.9 0.0 copy-done.7
  5.9 0.0 copy-start.1
  5.9 1.6 %copy-done.1 = bf16[16,512,128]{2,1,0:T(8,128)(2,1)S(1)} copy-done((bf16[16,512,128]{2,1,0:T(8,128)(2,1)S(1)}, bf16[16,512,128]{2,1,0:T(8,128)(2,1)}, u32[]{:S(2)}) %copy-start.1) | copy-done | bytes 2097176
  7.5 1.4 %owner_part.1 = (f32[2,2,64,128]{3,2,1,0:T(8,128)S(1)}, f32[2,2,64,128]{3,2,1,0:T(8,128)S(1)}) custom-call(s32[1]{0:T(128)} %copy.14.start_ref.refs_0_, f32[8]{0:T(128)S(1)} %copy-done.6, s32[4]{0:T(128)S(1)} %copy-done.7, f32[4,64,128]{2,1,0:T(8,128)S(1)} %get-tuple-element.43.refs_3_, f32[4,64,128]{2,1,0:T(8,128)S(1)} %get-tuple-element.36.refs_4_, ...), custom_call_target="tpu_custom_call" | custom-call | tf_op jit(solution)/shard_map/owner_part/pallas_call | solution.py:170
  9.0 0.6 collective-permute-start.10
  9.5 0.1 collective-permute-start.4
  9.6 0.9 %collective-permute-done.10 = f32[2,2,64,128]{3,2,1,0:T(8,128)S(1)} collective-permute-done((f32[2,2,64,128]{3,2,1,0:T(8,128)S(1)}, f32[2,2,64,128]{3,2,1,0:T(8,128)S(1)}, u32[]{:S(2)}, u32[]{:S(2)}) %collective-permute-start.10) | collective-permute-done | bytes 131104 | tf_op jit(solution)/shard_map/ppermute | solution.py:279
  10.5 2.9 %collective-permute-start.11 = (f32[1,2,64,128]{3,2,1,0:T(8,128)S(1)}, f32[1,2,64,128]{3,2,1,0:T(8,128)S(1)}, u32[]{:S(2)}, u32[]{:S(2)}) collective-permute-start(f32[1,2,64,128]{3,2,1,0:T(8,128)S(1)} %constant_dynamic-slice_fusion), channel_id=1, source_target_pairs={{0,16},{16,0},{1,17},{17,1},{2,18},{18,2},{3,19},{19,3},{4,20},{20... | collective-permute-start | bytes 196616 | tf_op jit(solution)/shard_map/ppermute | solution.py:279
  13.5 0.0 collective-permute-done.4
  13.5 1.6 %collective-permute-start.5 = (f32[2,64,128]{2,1,0:T(8,128)S(1)}, f32[2,64,128]{2,1,0:T(8,128)S(1)}, u32[]{:S(2)}, u32[]{:S(2)}) collective-permute-start(f32[2,64,128]{2,1,0:T(8,128)S(1)} %add.72), channel_id=1, source_target_pairs={{0,2},{1,3},{2,0},{3,1},{4,6},{5,7},{6,4},{7,5},{8,10},{9,11},{10,... | collective-permute-start | bytes 196616 | tf_op jit(solution)/shard_map/ppermute | solution.py:279
  15.1 0.8 %collective-permute-done.11 = f32[1,2,64,128]{3,2,1,0:T(8,128)S(1)} collective-permute-done((f32[1,2,64,128]{3,2,1,0:T(8,128)S(1)}, f32[1,2,64,128]{3,2,1,0:T(8,128)S(1)}, u32[]{:S(2)}, u32[]{:S(2)}) %collective-permute-start.11) | collective-permute-done | bytes 65568 | tf_op jit(solution)/shard_map/ppermute | solution.py:279
  15.9 1.9 %collective-permute-start.12 = (f32[2,64,128]{2,1,0:T(8,128)S(1)}, f32[2,64,128]{2,1,0:T(8,128)S(1)}, u32[]{:S(2)}, u32[]{:S(2)}) collective-permute-start(f32[2,64,128]{2,1,0:T(8,128)S(1)} %add_bitcast_fusion), channel_id=1, source_target_pairs={{0,2},{1,3},{2,0},{3,1},{4,6},{5,7},{6,4},{7,5},{8,10},{9,11},{10,... | collective-permute-start | bytes 196616 | tf_op jit(solution)/shard_map/ppermute | solution.py:279
  17.8 0.0 collective-permute-done.5
  17.8 1.6 %collective-permute-start.6 = (f32[2,64,128]{2,1,0:T(8,128)S(1)}, f32[2,64,128]{2,1,0:T(8,128)S(1)}, u32[]{:S(2)}, u32[]{:S(2)}) collective-permute-start(f32[2,64,128]{2,1,0:T(8,128)S(1)} %add.73), channel_id=1, source_target_pairs={{0,4},{1,5},{2,6},{3,7},{4,0},{5,1},{6,2},{7,3},{8,12},{9,13},{10,... | collective-permute-start | bytes 196616 | tf_op jit(solution)/shard_map/ppermute | solution.py:279
  19.5 0.7 %collective-permute-done.12 = f32[2,64,128]{2,1,0:T(8,128)S(1)} collective-permute-done((f32[2,64,128]{2,1,0:T(8,128)S(1)}, f32[2,64,128]{2,1,0:T(8,128)S(1)}, u32[]{:S(2)}, u32[]{:S(2)}) %collective-permute-start.12) | collective-permute-done | bytes 65568 | tf_op jit(solution)/shard_map/ppermute | solution.py:279
  20.2 2.0 %collective-permute-start.13 = (f32[2,64,128]{2,1,0:T(8,128)S(1)}, f32[2,64,128]{2,1,0:T(8,128)S(1)}, u32[]{:S(2)}, u32[]{:S(2)}) collective-permute-start(f32[2,64,128]{2,1,0:T(8,128)S(1)} %add.84), channel_id=1, source_target_pairs={{0,4},{1,5},{2,6},{3,7},{4,0},{5,1},{6,2},{7,3},{8,12},{9,13},{10,... | collective-permute-start | bytes 196616 | tf_op jit(solution)/shard_map/ppermute | solution.py:279
  22.2 0.5 collective-permute-done.6
  22.7 2.4 %collective-permute-start.7 = (f32[2,64,128]{2,1,0:T(8,128)S(1)}, f32[2,64,128]{2,1,0:T(8,128)S(1)}, u32[]{:S(2)}, u32[]{:S(2)}) collective-permute-start(f32[2,64,128]{2,1,0:T(8,128)S(1)} %add.74), channel_id=1, source_target_pairs={{0,8},{1,9},{2,10},{3,11},{4,12},{5,13},{6,14},{7,15},{8,0},{9,1},... | collective-permute-start | bytes 196616 | tf_op jit(solution)/shard_map/ppermute | solution.py:279
  25.2 0.0 collective-permute-done.13
  25.2 2.4 %collective-permute-start.14 = (f32[2,64,128]{2,1,0:T(8,128)S(1)}, f32[2,64,128]{2,1,0:T(8,128)S(1)}, u32[]{:S(2)}, u32[]{:S(2)}) collective-permute-start(f32[2,64,128]{2,1,0:T(8,128)S(1)} %add.85), channel_id=1, source_target_pairs={{0,8},{1,9},{2,10},{3,11},{4,12},{5,13},{6,14},{7,15},{8,0},{9,1},... | collective-permute-start | bytes 196616 | tf_op jit(solution)/shard_map/ppermute | solution.py:279
  27.6 1.5 %collective-permute-done.7 = f32[2,64,128]{2,1,0:T(8,128)S(1)} collective-permute-done((f32[2,64,128]{2,1,0:T(8,128)S(1)}, f32[2,64,128]{2,1,0:T(8,128)S(1)}, u32[]{:S(2)}, u32[]{:S(2)}) %collective-permute-start.7) | collective-permute-done | bytes 65568 | tf_op jit(solution)/shard_map/ppermute | solution.py:279
  29.1 0.1 collective-permute-start.8
  29.2 1.2 %collective-permute-done.14 = f32[2,64,128]{2,1,0:T(8,128)S(1)} collective-permute-done((f32[2,64,128]{2,1,0:T(8,128)S(1)}, f32[2,64,128]{2,1,0:T(8,128)S(1)}, u32[]{:S(2)}, u32[]{:S(2)}) %collective-permute-start.14) | collective-permute-done | bytes 65568 | tf_op jit(solution)/shard_map/ppermute | solution.py:279
  30.4 0.1 collective-permute-start.15
  30.5 0.0 collective-permute-done.8.refs_3_
  30.5 1.6 %copy-done.2 = bf16[16,512,128]{2,1,0:T(8,128)(2,1)S(1)} copy-done((bf16[16,512,128]{2,1,0:T(8,128)(2,1)S(1)}, bf16[16,512,128]{2,1,0:T(8,128)(2,1)}, u32[]{:S(2)}) %copy-start.2) | copy-done | bytes 2097176
  32.1 1.7 %integral_row.1 = (f32[8,64,128]{2,1,0:T(8,128)S(1)}, f32[8,64,128]{2,1,0:T(8,128)S(1)}) custom-call(f32[8]{0:T(128)S(1)} %copy-done.6, s32[4]{0:T(128)S(1)} %copy-done.7, f32[2,64,128]{2,1,0:T(8,128)S(1)} %add.75.refs_2_, f32[2,64,128]{2,1,0:T(8,128)S(1)} %collective-permute-done.8.refs_3_, bf16[16,512,128]{2,1,0:T(8,128)(2,1)S(1)} %get-tuple-element.29.refs_4_.refs_6_, ...), custom_call_target="tpu_custom_call" | custom-call | tf_op jit(solution)/shard_map/integral_row/pallas_call | solution.py:207
  33.8 1.6 %collective-permute-start.9 = (f32[8,64,128]{2,1,0:T(8,128)S(1)}, f32[8,64,128]{2,1,0:T(8,128)S(1)}, u32[]{:S(2)}, u32[]{:S(2)}) collective-permute-start(f32[8,64,128]{2,1,0:T(8,128)S(1)} %get-tuple-element.32), channel_id=1, source_target_pairs={{0,16},{16,0},{1,17},{17,1},{2,18},{18,2},{3,19},{19,3},{4,20},{20... | collective-permute-start | bytes 786440 | tf_op jit(solution)/shard_map/ppermute | solution.py:279
  35.4 0.0 collective-permute-done.15.refs_3_
  35.4 1.3 %integral_send.1 = f32[8,64,128]{2,1,0:T(8,128)S(1)} custom-call(f32[8]{0:T(128)S(1)} %copy-done.6, s32[4]{0:T(128)S(1)} %copy-done.7, f32[2,64,128]{2,1,0:T(8,128)S(1)} %add.86.refs_2_, f32[2,64,128]{2,1,0:T(8,128)S(1)} %collective-permute-done.15.refs_3_, bf16[16,512,128]{2,1,0:T(8,128)(2,1)S(1)} %get-tuple-element.29.refs_4_.refs_6_, ...), custom_call_target="tpu_custom_call" | custom-call | tf_op jit(solution)/shard_map/integral_send/pallas_call | solution.py:207
  36.8 0.6 collective-permute-start.16
  37.4 1.3 %integral_keep.1.mine_ref = f32[8,64,128]{2,1,0:T(8,128)S(1)} custom-call(f32[8]{0:T(128)S(1)} %copy-done.6, s32[4]{0:T(128)S(1)} %copy-done.7, f32[2,64,128]{2,1,0:T(8,128)S(1)} %add.86.refs_2_, f32[2,64,128]{2,1,0:T(8,128)S(1)} %collective-permute-done.15.refs_3_, bf16[16,512,128]{2,1,0:T(8,128)(2,1)S(1)} %get-tuple-element.29.refs_4_.refs_6_, ...), custom_call_target="tpu_custom_call" | custom-call | tf_op jit(solution)/shard_map/integral_keep/pallas_call | solution.py:207
  38.7 4.4 %collective-permute-done.9.recv_ref = f32[8,64,128]{2,1,0:T(8,128)S(1)} collective-permute-done((f32[8,64,128]{2,1,0:T(8,128)S(1)}, f32[8,64,128]{2,1,0:T(8,128)S(1)}, u32[]{:S(2)}, u32[]{:S(2)}) %collective-permute-start.9) | collective-permute-done | bytes 262176 | tf_op jit(solution)/shard_map/ppermute | solution.py:279
  43.1 0.9 %share_bases.1 = (f32[8,64,128]{2,1,0:T(8,128)S(1)}, f32[8,64,128]{2,1,0:T(8,128)S(1)}) custom-call(f32[16,64,128]{2,1,0:T(8,128)S(1)} %copy-done.3, f32[8,64,128]{2,1,0:T(8,128)S(1)} %get-tuple-element.31.mine_ref, f32[8,64,128]{2,1,0:T(8,128)S(1)} %collective-permute-done.9.recv_ref, f32[128,64]{1,0:T(8,128)S(1)} %get-tuple-element.33.herm_ref.refs_5_), custom_call_target="tpu_custom_call" | custom-call | tf_op jit(solution)/shard_map/share_bases/pallas_call | solution.py:246
  44.0 4.3 %collective-permute-done.16.recv_ref = f32[8,64,128]{2,1,0:T(8,128)S(1)} collective-permute-done((f32[8,64,128]{2,1,0:T(8,128)S(1)}, f32[8,64,128]{2,1,0:T(8,128)S(1)}, u32[]{:S(2)}, u32[]{:S(2)}) %collective-permute-start.16) | collective-permute-done | bytes 262176 | tf_op jit(solution)/shard_map/ppermute | solution.py:279
  48.2 0.8 %finish.1 = (f32[8,64,128]{2,1,0:T(8,128)S(1)}, f32[32,128]{1,0:T(8,128)}) custom-call(f32[8,64,128]{2,1,0:T(8,128)S(1)} %get-tuple-element.34.out_base_ref, f32[8,64,128]{2,1,0:T(8,128)S(1)} %get-tuple-element.35.diff_base_ref, f32[8,64,128]{2,1,0:T(8,128)S(1)} %integral_keep.1.mine_ref, f32[8,64,128]{2,1,0:T(8,128)S(1)} %collective-permute-done.16.recv_ref), custom_call_target="tpu_custom_call" | custom-call | tf_op jit(solution)/shard_map/finish/pallas_call | solution.py:267
  49.0 1.5 %collective-permute-start.17 = (f32[1,8,64,128]{3,2,1,0:T(8,128)S(1)}, f32[1,8,64,128]{3,2,1,0:T(8,128)S(1)}, u32[]{:S(2)}, u32[]{:S(2)}) collective-permute-start(f32[1,8,64,128]{3,2,1,0:T(8,128)S(1)} %bitcast.17), channel_id=1, source_target_pairs={{0,16},{16,0},{1,17},{17,1},{2,18},{18,2},{3,19},{19,3},{4,20},{20... | collective-permute-start | bytes 786440 | tf_op jit(solution)/shard_map/ppermute | solution.py:279
  50.5 5.3 %all-to-all-start = ((f32[32,1,128]{2,1,0:T(1,128)}), f32[32,1,128]{2,1,0:T(1,128)S(1)}, u32[]{:S(2)}, u32[]{:S(2)}) async-start(f32[32,1,128]{2,1,0:T(1,128)} %bitcast.5), calls=%async_computation | async-start | bytes 32768 | tf_op jit(solution)/shard_map/all_to_all | solution.py:382
  55.9 7.1 %all-to-all-done = f32[32,1,128]{2,1,0:T(1,128)S(1)} async-done(((f32[32,1,128]{2,1,0:T(1,128)}), f32[32,1,128]{2,1,0:T(1,128)S(1)}, u32[]{:S(2)}, u32[]{:S(2)}) %all-to-all-start) | async-done | bytes 16416 | tf_op jit(solution)/shard_map/all_to_all | solution.py:382
  63.0 0.6 slice_reduce_fusion
  64.3 0.0 collective-permute-done.17
  64.4 0.8 %pad_maximum_fusion = f32[2,8,64,128]{3,2,1,0:T(8,128)} fusion(f32[1,8,64,128]{3,2,1,0:T(8,128)S(1)} %get-tuple-element.42, f32[1,8,64,128]{3,2,1,0:T(8,128)S(1)} %get-tuple-element.41), kind=kLoop, calls=%fused_computation | loop fusion | flops 131072 | bytes 1048576 | tf_op jit(solution)/shard_map/concatenate | solution.py:320
  (21 shorter events, 0.2 us)
Async XLA Ops:
  0.6 4.9 %copy-start.3 = (f32[16,64,128]{2,1,0:T(8,128)S(1)}, f32[16,64,128]{2,1,0:T(8,128)}, u32[]{:S(2)}) copy-start(f32[16,64,128]{2,1,0:T(8,128)} %row_ref.3) | copy-start | bytes 1572868
  1.4 1.6 %copy-start.4 = (f32[4,16,64,128]{3,2,1,0:T(8,128)S(1)}, f32[4,16,64,128]{3,2,1,0:T(8,128)}, u32[]{:S(2)}) copy-start(f32[4,16,64,128]{3,2,1,0:T(8,128)} %hist_ref.1) | copy-start | bytes 6291460
  3.0 2.5 %copy-start.5 = (f32[64,128]{1,0:T(8,128)S(1)}, f32[64,128]{1,0:T(8,128)}, u32[]{:S(2)}) copy-start(f32[64,128]{1,0:T(8,128)} %ham_ref.1) | copy-start | bytes 98308
  3.0 2.9 %copy-start.6 = (f32[8]{0:T(128)S(1)}, f32[8]{0:T(128)}, u32[]{:S(2)}) copy-start(f32[8]{0:T(128)} %refs_0_.6) | copy-start | bytes 100
  3.0 2.9 %copy-start.7 = (s32[4]{0:T(128)S(1)}, s32[4]{0:T(128)}, u32[]{:S(2)}) copy-start(s32[4]{0:T(128)} %refs_1_.7) | copy-start | bytes 52
  4.2 1.4 %copy-start = (bf16[16,512,128]{2,1,0:T(8,128)(2,1)}, bf16[16,512,128]{2,1,0:T(8,128)(2,1)S(1)}, u32[]{:S(2)}) copy-start(bf16[16,512,128]{2,1,0:T(8,128)(2,1)S(1)} %get-tuple-element.30.refs_5_.refs_7_) | copy-start | bytes 6291460
  5.9 1.6 %copy-start.1 = (bf16[16,512,128]{2,1,0:T(8,128)(2,1)S(1)}, bf16[16,512,128]{2,1,0:T(8,128)(2,1)}, u32[]{:S(2)}) copy-start(bf16[16,512,128]{2,1,0:T(8,128)(2,1)} %copy-done) | copy-start | bytes 6291460
  9.0 1.5 %collective-permute-start.10 = (f32[2,2,64,128]{3,2,1,0:T(8,128)S(1)}, f32[2,2,64,128]{3,2,1,0:T(8,128)S(1)}, u32[]{:S(2)}, u32[]{:S(2)}) collective-permute-start(f32[2,2,64,128]{3,2,1,0:T(8,128)S(1)} %get-tuple-element.38), channel_id=1, source_target_pairs={{0,1},{1,0},{2,3},{3,2},{4,5},{5,4},{6,7},{7,6},{8,9},{9,8},{10,11... | collective-permute-start | bytes 393224 | tf_op jit(solution)/shard_map/ppermute | solution.py:279
  9.5 4.0 %collective-permute-start.4 = (f32[2,64,128]{2,1,0:T(8,128)S(1)}, f32[2,64,128]{2,1,0:T(8,128)S(1)}, u32[]{:S(2)}, u32[]{:S(2)}) collective-permute-start(f32[2,64,128]{2,1,0:T(8,128)S(1)} %get-tuple-element.28), channel_id=1, source_target_pairs={{0,1},{1,0},{2,3},{3,2},{4,5},{5,4},{6,7},{7,6},{8,9},{9,8},{10,11... | collective-permute-start | bytes 196616 | tf_op jit(solution)/shard_map/ppermute | solution.py:279
  10.5 5.3 %collective-permute-start.11 = (f32[1,2,64,128]{3,2,1,0:T(8,128)S(1)}, f32[1,2,64,128]{3,2,1,0:T(8,128)S(1)}, u32[]{:S(2)}, u32[]{:S(2)}) collective-permute-start(f32[1,2,64,128]{3,2,1,0:T(8,128)S(1)} %constant_dynamic-slice_fusion), channel_id=1, source_target_pairs={{0,16},{16,0},{1,17},{17,1},{2,18},{18,2},{3,19},{19,3},{4,20},{20... | collective-permute-start | bytes 196616 | tf_op jit(solution)/shard_map/ppermute | solution.py:279
  13.5 4.3 %collective-permute-start.5 = (f32[2,64,128]{2,1,0:T(8,128)S(1)}, f32[2,64,128]{2,1,0:T(8,128)S(1)}, u32[]{:S(2)}, u32[]{:S(2)}) collective-permute-start(f32[2,64,128]{2,1,0:T(8,128)S(1)} %add.72), channel_id=1, source_target_pairs={{0,2},{1,3},{2,0},{3,1},{4,6},{5,7},{6,4},{7,5},{8,10},{9,11},{10,... | collective-permute-start | bytes 196616 | tf_op jit(solution)/shard_map/ppermute | solution.py:279
  15.9 4.3 %collective-permute-start.12 = (f32[2,64,128]{2,1,0:T(8,128)S(1)}, f32[2,64,128]{2,1,0:T(8,128)S(1)}, u32[]{:S(2)}, u32[]{:S(2)}) collective-permute-start(f32[2,64,128]{2,1,0:T(8,128)S(1)} %add_bitcast_fusion), channel_id=1, source_target_pairs={{0,2},{1,3},{2,0},{3,1},{4,6},{5,7},{6,4},{7,5},{8,10},{9,11},{10,... | collective-permute-start | bytes 196616 | tf_op jit(solution)/shard_map/ppermute | solution.py:279
  17.8 4.9 %collective-permute-start.6 = (f32[2,64,128]{2,1,0:T(8,128)S(1)}, f32[2,64,128]{2,1,0:T(8,128)S(1)}, u32[]{:S(2)}, u32[]{:S(2)}) collective-permute-start(f32[2,64,128]{2,1,0:T(8,128)S(1)} %add.73), channel_id=1, source_target_pairs={{0,4},{1,5},{2,6},{3,7},{4,0},{5,1},{6,2},{7,3},{8,12},{9,13},{10,... | collective-permute-start | bytes 196616 | tf_op jit(solution)/shard_map/ppermute | solution.py:279
  20.2 4.9 %collective-permute-start.13 = (f32[2,64,128]{2,1,0:T(8,128)S(1)}, f32[2,64,128]{2,1,0:T(8,128)S(1)}, u32[]{:S(2)}, u32[]{:S(2)}) collective-permute-start(f32[2,64,128]{2,1,0:T(8,128)S(1)} %add.84), channel_id=1, source_target_pairs={{0,4},{1,5},{2,6},{3,7},{4,0},{5,1},{6,2},{7,3},{8,12},{9,13},{10,... | collective-permute-start | bytes 196616 | tf_op jit(solution)/shard_map/ppermute | solution.py:279
  22.7 6.4 %collective-permute-start.7 = (f32[2,64,128]{2,1,0:T(8,128)S(1)}, f32[2,64,128]{2,1,0:T(8,128)S(1)}, u32[]{:S(2)}, u32[]{:S(2)}) collective-permute-start(f32[2,64,128]{2,1,0:T(8,128)S(1)} %add.74), channel_id=1, source_target_pairs={{0,8},{1,9},{2,10},{3,11},{4,12},{5,13},{6,14},{7,15},{8,0},{9,1},... | collective-permute-start | bytes 196616 | tf_op jit(solution)/shard_map/ppermute | solution.py:279
  25.2 5.2 %collective-permute-start.14 = (f32[2,64,128]{2,1,0:T(8,128)S(1)}, f32[2,64,128]{2,1,0:T(8,128)S(1)}, u32[]{:S(2)}, u32[]{:S(2)}) collective-permute-start(f32[2,64,128]{2,1,0:T(8,128)S(1)} %add.85), channel_id=1, source_target_pairs={{0,8},{1,9},{2,10},{3,11},{4,12},{5,13},{6,14},{7,15},{8,0},{9,1},... | collective-permute-start | bytes 196616 | tf_op jit(solution)/shard_map/ppermute | solution.py:279
  29.1 1.4 %collective-permute-start.8 = (f32[2,64,128]{2,1,0:T(8,128)S(1)}, f32[2,64,128]{2,1,0:T(8,128)S(1)}, u32[]{:S(2)}, u32[]{:S(2)}) collective-permute-start(f32[2,64,128]{2,1,0:T(8,128)S(1)} %add.75.refs_2_), channel_id=1, source_target_pairs={{0,1},{1,0},{2,3},{3,2},{4,5},{5,4},{6,7},{7,6},{8,9},{9,8},{10,11... | collective-permute-start | bytes 196616 | tf_op jit(solution)/shard_map/ppermute | solution.py:279
  30.4 5.0 %collective-permute-start.15 = (f32[2,64,128]{2,1,0:T(8,128)S(1)}, f32[2,64,128]{2,1,0:T(8,128)S(1)}, u32[]{:S(2)}, u32[]{:S(2)}) collective-permute-start(f32[2,64,128]{2,1,0:T(8,128)S(1)} %add.86.refs_2_), channel_id=1, source_target_pairs={{0,1},{1,0},{2,3},{3,2},{4,5},{5,4},{6,7},{7,6},{8,9},{9,8},{10,11... | collective-permute-start | bytes 196616 | tf_op jit(solution)/shard_map/ppermute | solution.py:279
  30.5 1.6 %copy-start.2 = (bf16[16,512,128]{2,1,0:T(8,128)(2,1)S(1)}, bf16[16,512,128]{2,1,0:T(8,128)(2,1)}, u32[]{:S(2)}) copy-start(bf16[16,512,128]{2,1,0:T(8,128)(2,1)} %copy-done) | copy-start | bytes 6291460
  33.8 9.2 %collective-permute-start.9 = (f32[8,64,128]{2,1,0:T(8,128)S(1)}, f32[8,64,128]{2,1,0:T(8,128)S(1)}, u32[]{:S(2)}, u32[]{:S(2)}) collective-permute-start(f32[8,64,128]{2,1,0:T(8,128)S(1)} %get-tuple-element.32), channel_id=1, source_target_pairs={{0,16},{16,0},{1,17},{17,1},{2,18},{18,2},{3,19},{19,3},{4,20},{20... | collective-permute-start | bytes 786440 | tf_op jit(solution)/shard_map/ppermute | solution.py:279
  36.8 11.5 %collective-permute-start.16 = (f32[8,64,128]{2,1,0:T(8,128)S(1)}, f32[8,64,128]{2,1,0:T(8,128)S(1)}, u32[]{:S(2)}, u32[]{:S(2)}) collective-permute-start(f32[8,64,128]{2,1,0:T(8,128)S(1)} %integral_send.1), channel_id=1, source_target_pairs={{0,16},{16,0},{1,17},{17,1},{2,18},{18,2},{3,19},{19,3},{4,20},{20... | collective-permute-start | bytes 786440 | tf_op jit(solution)/shard_map/ppermute | solution.py:279
  49.0 15.3 %collective-permute-start.17 = (f32[1,8,64,128]{3,2,1,0:T(8,128)S(1)}, f32[1,8,64,128]{3,2,1,0:T(8,128)S(1)}, u32[]{:S(2)}, u32[]{:S(2)}) collective-permute-start(f32[1,8,64,128]{3,2,1,0:T(8,128)S(1)} %bitcast.17), channel_id=1, source_target_pairs={{0,16},{16,0},{1,17},{17,1},{2,18},{18,2},{3,19},{19,3},{4,20},{20... | collective-permute-start | bytes 786440 | tf_op jit(solution)/shard_map/ppermute | solution.py:279
  50.5 12.5 %all-to-all-start = ((f32[32,1,128]{2,1,0:T(1,128)}), f32[32,1,128]{2,1,0:T(1,128)S(1)}, u32[]{:S(2)}, u32[]{:S(2)}) async-start(f32[32,1,128]{2,1,0:T(1,128)} %bitcast.5), calls=%async_computation | async-start | bytes 32768 | tf_op jit(solution)/shard_map/all_to_all | solution.py:382

commit v3 on v2

--- a/solution.py
+++ b/solution.py
@@ -7,6 +7,7 @@
 from jax.experimental.pallas import tpu as pltpu
 from jax.sharding import PartitionSpec as P
 
+
 coupling = 0.5
 step_size = 0.25
 
@@ -14,6 +15,7 @@
 bf16 = jnp.bfloat16
 SMEM_SPEC = pl.BlockSpec(memory_space=pltpu.SMEM)
 VMEM_SPEC = pl.BlockSpec(memory_space=pltpu.VMEM)
+HBM_SPEC = pl.BlockSpec(memory_space=pltpu.HBM)
 PARAMS = pltpu.CompilerParams(vmem_limit_bytes=12 << 20)
 
 
@@ -61,67 +63,57 @@
     return jnp.clip(spot, 0, sec_rows - 1), (spot >= 0) & (spot < sec_rows)
 
 
-def prepare_kernel(start_ref, row_ref, ham_ref, window_ref, keep_ref, send_ref, herm_ref):
+def prepare_kernel(
+    start_ref, row_ref, ham_hbm, window_ref, keep_ref, send_ref, herm_ref, raw, ham_ref, sems
+):
     count = window_ref.shape[0]
     half = count // 2
-    orbits = ham_ref.shape[0]
+    orbits = ham_hbm.shape[0]
+    sec_rows = row_ref.shape[0]
     first = lax.axis_index("past") * count
     odd = lax.axis_index("second") % 2
+    spots = [local_spot(start_ref, first + p, sec_rows) for p in range(count)]
+    copies = [pltpu.make_async_copy(row_ref.at[spots[p][0]], raw.at[p], sems.at[p]) for p in range(count)]
+    copies.append(pltpu.make_async_copy(ham_hbm, ham_ref, sems.at[count]))
+    for copy in copies:
+        copy.start()
+
+    copies[-1].wait()
+    real = ham_ref[:, :orbits]
+    imag = ham_ref[:, orbits:]
+    herm_ref[...] = jnp.concatenate([0.5 * (real + real.T), 0.5 * (imag - imag.T)], axis=0)
+    for copy in copies[:-1]:
+        copy.wait()
     for p in range(count):
-        pos, inside = local_spot(start_ref, first + p, row_ref.shape[0])
-        window_ref[p] = jnp.where(inside, row_ref[pos], 0.0)
+        window_ref[p] = jnp.where(spots[p][1], raw[p], 0.0)
     for p in range(half):
         keep_ref[p] = window_ref[odd * half + p]
         send_ref[p] = window_ref[(1 - odd) * half + p]
-    real = ham_ref[:, :orbits]
-    imag = ham_ref[:, orbits:]
-    herm_ref[...] = jnp.concatenate([0.5 * (real + real.T), 0.5 * (imag - imag.T)], axis=0)
 
 
 def prepare(block_start, green_row, hamiltonian, count):
     orbits = hamiltonian.shape[0]
     tile = green_row.shape[1:]
     half = jax.ShapeDtypeStruct((count // 2,) + tile, f32)
+    whole = jax.ShapeDtypeStruct((count,) + tile, f32)
     return pl.pallas_call(
         prepare_kernel,
-        in_specs=[SMEM_SPEC, VMEM_SPEC, VMEM_SPEC],
+        in_specs=[SMEM_SPEC, HBM_SPEC, HBM_SPEC],
         out_specs=[VMEM_SPEC] * 4,
         out_shape=[
-            jax.ShapeDtypeStruct((count,) + tile, f32),
+            whole,
             half,
             half,
             jax.ShapeDtypeStruct((2 * orbits, orbits), f32),
         ],
+        scratch_shapes=[
+            pltpu.VMEM(whole.shape, f32),
+            pltpu.VMEM(hamiltonian.shape, f32),
+            pltpu.SemaphoreType.DMA((count + 1,)),
+        ],
         compiler_params=PARAMS,
         name="prepare",
     )(block_start, green_row, hamiltonian)
-
-
-def right_kernel(hist_ref, high_ref, low_ref):
-    past_rows, sec_rows, orbits, _ = hist_ref.shape
-
-    def body(s, carry):
-        for p in range(past_rows):
-            tile = hist_ref[p, s]
-            for q, part in enumerate((tile, self_energy(tile))):
-                rows = slice((2 * p + q) * orbits, (2 * p + q + 1) * orbits)
-                high_ref[s, rows], low_ref[s, rows] = split(part)
-        return carry
-
-    lax.fori_loop(0, sec_rows, body, 0, unroll=2)
-
-
-def right_factors(green_hist):
-    past_rows, sec_rows, orbits, width = green_hist.shape
-    shape = jax.ShapeDtypeStruct((sec_rows, past_rows * 2 * orbits, width), bf16)
-    return pl.pallas_call(
-        right_kernel,
-        in_specs=[VMEM_SPEC],
-        out_specs=[VMEM_SPEC] * 2,
-        out_shape=[shape, shape],
-        compiler_params=PARAMS,
-        name="right_factors",
-    )(green_hist)
 
 
 def put_left(left_high, left_low, p, tile, weight):
@@ -130,28 +122,40 @@
     left_high[:, cols], left_low[:, cols] = split(left_factor(tile, weight))
 
 
-def contract(left, high_ref, low_ref, first, second):
-    high = jnp.concatenate([high_ref[first], high_ref[second]], axis=1)
-    low = jnp.concatenate([low_ref[first], low_ref[second]], axis=1)
-    return dot3(left, (high, low))
+def right_factor(tiles):
+    return jnp.concatenate(
+        [jnp.concatenate(tiles, axis=1), jnp.concatenate([self_energy(t) for t in tiles], axis=1)], axis=0
+    )
+
+
+def contract(left_high, left_low, hist_ref, first, second):
+    past_rows, _, _, width = hist_ref.shape
+    acc = None
+    for p in range(0, past_rows, 2):
+        right = jnp.concatenate(
+            [right_factor([hist_ref[p + q, first], hist_ref[p + q, second]]) for q in range(2)], axis=0
+        )
+        cols = slice(p * width, (p + 2) * width)
+        term = dot3((left_high[:, cols], left_low[:, cols]), split(right))
+        acc = term if acc is None else acc + term
+    return acc
 
 
 def owner_kernel(
-    start_ref, quad_ref, index_ref, win_ref, base_ref, herm_ref, high_ref, low_ref, keep_ref, send_ref, lh, ll, *, scale
+    start_ref, quad_ref, index_ref, win_ref, base_ref, herm_ref, hist_ref, keep_ref, send_ref, lh, ll, *, scale
 ):
     past_rows, orbits, width = win_ref.shape
     half = past_rows // 2
-    sec_rows = high_ref.shape[0]
+    sec_rows = hist_ref.shape[1]
     odd = lax.axis_index("second") % 2
     past = lax.axis_index("past")
     for p in range(past_rows):
         put_left(lh, ll, p, win_ref[p], quad_ref[index_ref[p]])
-    left = (lh[...], ll[...])
     for out_ref, side in ((send_ref, 1 - odd), (keep_ref, odd)):
         for g in range(out_ref.shape[0]):
             for t in range(0, half, 2):
                 spots = [local_spot(start_ref, g * past_rows + side * half + t + q, sec_rows) for q in range(2)]
-                acc = contract(left, high_ref, low_ref, spots[0][0], spots[1][0])
+                acc = contract(lh, ll, hist_ref, spots[0][0], spots[1][0])
                 for q in range(2):
                     value = step_size * scale * minus_i_times(acc[:, q * width : (q + 1) * width], orbits)
                     out_ref[g, t + q] = jnp.where(spots[q][1], value, 0.0)
@@ -164,25 +168,25 @@
                 out_ref[past, t + q] += base[:, cols] + step_size * minus_i_times(acc[:, cols], orbits)
 
 
-def owner_part(block_start, quad_table, weight_index, window, base, herm, high, low, past_size, scale):
+def owner_part(block_start, quad_table, weight_index, window, base, herm, green_hist, past_size, scale):
     past_rows, orbits, width = window.shape
     shape = jax.ShapeDtypeStruct((past_size, past_rows // 2, orbits, width), f32)
     return pl.pallas_call(
         lambda *refs: owner_kernel(*refs, scale=scale),
-        in_specs=[SMEM_SPEC] * 3 + [VMEM_SPEC] * 5,
+        in_specs=[SMEM_SPEC] * 3 + [VMEM_SPEC] * 4,
         out_specs=[VMEM_SPEC] * 2,
         out_shape=[shape, shape],
         scratch_shapes=[pltpu.VMEM((2 * orbits, past_rows * width), bf16)] * 2,
         compiler_params=PARAMS,
         name="owner_part",
-    )(block_start, quad_table, weight_index, window, base, herm, high, low)
+    )(block_start, quad_table, weight_index, window, base, herm, green_hist)
 
 
 def past_half(past_size):
     return lax.axis_index("past") // (past_size // 2) % 2
 
 
-def integral_kernel(quad_ref, index_ref, mine_ref, other_ref, high_ref, low_ref, *refs, scale, sides, past_size):
+def integral_kernel(quad_ref, index_ref, mine_ref, other_ref, hist_ref, *refs, scale, sides, past_size):
     outs, (lh, ll) = refs[: len(sides)], refs[len(sides) :]
     half, orbits, width = mine_ref.shape
     past_rows = 2 * half
@@ -190,29 +194,27 @@
     for p in range(past_rows):
         tile = jnp.where(odd == p // half, mine_ref[p % half], other_ref[p % half])
         put_left(lh, ll, p, tile, quad_ref[index_ref[p]])
-    left = (lh[...], ll[...])
     for out_ref, kept in zip(outs, sides):
         count = out_ref.shape[0]
         upper = past_half(past_size)
         first = (upper if kept else 1 - upper) * count
         for s in range(0, count, 2):
-            acc = contract(left, high_ref, low_ref, first + s, first + s + 1)
+            acc = contract(lh, ll, hist_ref, first + s, first + s + 1)
             for q in range(2):
                 out_ref[s + q] = scale * minus_i_times(acc[:, q * width : (q + 1) * width], orbits)
 
 
-def integral(quad_table, weight_index, mine, other, high, low, past_size, sides, scale, name):
+def integral(quad_table, weight_index, mine, other, green_hist, past_size, sides, scale):
     half, orbits, width = mine.shape
-    shape = jax.ShapeDtypeStruct((high.shape[0] // 2, orbits, width), f32)
+    shape = jax.ShapeDtypeStruct((green_hist.shape[1] // 2, orbits, width), f32)
     return pl.pallas_call(
         lambda *refs: integral_kernel(*refs, scale=scale, sides=sides, past_size=past_size),
-        in_specs=[SMEM_SPEC] * 2 + [VMEM_SPEC] * 4,
+        in_specs=[SMEM_SPEC] * 2 + [VMEM_SPEC] * 3,
         out_specs=[VMEM_SPEC] * len(sides),
         out_shape=[shape] * len(sides),
         scratch_shapes=[pltpu.VMEM((2 * orbits, 2 * half * width), bf16)] * 2,
         compiler_params=PARAMS,
-        name=name,
-    )(quad_table, weight_index, mine, other, high, low)
+    )(quad_table, weight_index, mine, other, green_hist)
 
 
 def share_kernel(row_ref, mine_ref, recv_ref, herm_ref, out_base_ref, diff_base_ref):
@@ -274,6 +276,47 @@
     )(out_base, diff_base, mine, recv)
 
 
+def norm_kernel(sums_ref, out_ref, *, entry_count):
+    total = jnp.sum(sums_ref[...], axis=0, keepdims=True)
+    out_ref[0] = (jnp.sqrt(total / entry_count) / step_size)[0, 0]
+
+
+def norm(sums, entry_count):
+    return pl.pallas_call(
+        lambda *refs: norm_kernel(*refs, entry_count=entry_count),
+        in_specs=[VMEM_SPEC],
+        out_specs=SMEM_SPEC,
+        out_shape=jax.ShapeDtypeStruct((1,), f32),
+        compiler_params=PARAMS,
+        name="norm",
+    )(sums)
+
+
+def join_kernel(own_ref, other_ref, out_ref, sems, *, mask):
+    count = own_ref.shape[0]
+    upper = lax.axis_index("past") // mask % 2
+    copies = [
+        pltpu.make_async_copy(own_ref, out_ref.at[pl.ds(upper * count, count)], sems.at[0]),
+        pltpu.make_async_copy(other_ref, out_ref.at[pl.ds((1 - upper) * count, count)], sems.at[1]),
+    ]
+    for copy in copies:
+        copy.start()
+    for copy in copies:
+        copy.wait()
+
+
+def join(own, other, mask):
+    return pl.pallas_call(
+        lambda *refs: join_kernel(*refs, mask=mask),
+        in_specs=[VMEM_SPEC, VMEM_SPEC],
+        out_specs=HBM_SPEC,
+        out_shape=jax.ShapeDtypeStruct((2 * own.shape[0],) + own.shape[1:], f32),
+        scratch_shapes=[pltpu.SemaphoreType.DMA((2,))],
+        compiler_params=PARAMS,
+        name="join",
+    )(own, other)
+
+
 def exchange(value, axis, mask):
     size = lax.axis_size(axis)
     return lax.ppermute(value, axis, [(i, i ^ mask) for i in range(size)])
@@ -310,14 +353,9 @@
 
 
 def gather_past(value):
-    size = lax.axis_size("past")
-    index = lax.axis_index("past")
-    value = value[None]
     mask = 1
-    while mask < size:
-        other = exchange(value, "past", mask)
-        upper = (index // mask) % 2 == 1
-        value = jnp.concatenate([jnp.where(upper, other, value), jnp.where(upper, value, other)], axis=0)
+    while mask < lax.axis_size("past"):
+        value = join(value, exchange(value, "past", mask), mask)
         mask *= 2
     return value
 
@@ -330,7 +368,7 @@
     return value
 
 
-def local(green_row, green_hist, hamiltonian, quad_table, weight_index, block_start):
+def step(green_row, green_hist, hamiltonian, quad_table, weight_index, block_start):
     past_rows, sec_rows, orbits, width = green_hist.shape
     past_size = lax.axis_size("past")
     second_size = lax.axis_size("second")
@@ -338,10 +376,9 @@
     scale = 1.0 / math.sqrt(orbits * total_past)
 
     own_window, row_keep, row_send, herm = prepare(block_start, green_row, hamiltonian, past_rows)
-    high, low = right_factors(green_hist)
-
-    owner = block_start[0] // sec_rows
-    crossing = (block_start[0] + total_past - 1) // sec_rows > owner
+
+    owner = lax.div(block_start[0], sec_rows)
+    crossing = lax.div(block_start[0] + total_past - 1, sec_rows) > owner
     flips = owner ^ (owner + 1)
     branch = jnp.where(crossing, 1, 0)
     masks = []
@@ -355,7 +392,7 @@
         own_window,
     )
     part_keep, part_send = owner_part(
-        block_start, quad_table, weight_index, window, own_window, herm, high, low, past_size, scale
+        block_start, quad_table, weight_index, window, own_window, herm, green_hist, past_size, scale
     )
 
     row_mine = spread_second(row_keep + exchange(row_send, "second", 1))
@@ -365,30 +402,21 @@
     pred_other = exchange(pred_mine, "second", 1)
 
     slope_keep, slope_send = integral(
-        quad_table, weight_index, row_mine, row_other, high, low, past_size, (True, False), scale, "integral_row"
+        quad_table, weight_index, row_mine, row_other, green_hist, past_size, (True, False), scale
     )
     out_base, diff_base = share_bases(green_row, *share_past(slope_keep, slope_send), herm)
 
     final = 0.5 * step_size * scale
-    (last_send,) = integral(
-        quad_table, weight_index, pred_mine, pred_other, high, low, past_size, (False,), final, "integral_send"
-    )
-    (last_keep,) = integral(
-        quad_table, weight_index, pred_mine, pred_other, high, low, past_size, (True,), final, "integral_keep"
-    )
+    (last_send,) = integral(quad_table, weight_index, pred_mine, pred_other, green_hist, past_size, (False,), final)
+    (last_keep,) = integral(quad_table, weight_index, pred_mine, pred_other, green_hist, past_size, (True,), final)
     devices = past_size * second_size
     out_share, squares = finish(out_base, diff_base, *share_past(last_keep, last_send), devices)
 
     sums = lax.all_to_all(squares, ("past", "second"), 0, 0, tiled=True)
-    green_next = gather_past(out_share).reshape(green_row.shape)
-    total = jnp.sum(sums[:, :1])
-    entry_count = sec_rows * second_size * orbits * width
-    change = jnp.sqrt(total / entry_count) / step_size
-    return (green_next, change.reshape(1))
+    green_next = gather_past(out_share)
+    return (green_next, norm(sums, sec_rows * second_size * orbits * width))
 
 
 def solution(mesh):
     placed = (P("second", None, None), P("past", "second", None, None), P(), P(), P("past"), P())
-    return jax.shard_map(
-        local, mesh=mesh, in_specs=placed, out_specs=(P("second", None, None), P()), check_vma=False
-    )
+    return jax.shard_map(step, mesh=mesh, in_specs=placed, out_specs=(P("second", None, None), P()), check_vma=False)

time: 66.6 us -> 59.3 us (0.89)
  blocking collectives: 0 us -> 12.3 us
  waiting for transfers between devices: 21.5 us -> 14.2 us
  starting transfers between devices: 24.6 us -> 19.3 us
  local copies, waits for them, and re-layouts: 6.14 us -> 1.84 us
  between operations: 3.44 us -> 1.66 us
  other arithmetic: 1.58 us -> 0.1 us
    all_to_all x0 -> x1, blocking collectives: none -> 12.3 us  [step(): sums = lax.all_to_all(squares, ('past', 'second'), 0, 0, tiled=True)]
    all_to_all x1 -> x0, waiting for transfers between devices: 7.1 us -> none  [local(): sums = lax.all_to_all(squares, ('past', 'second'), 0, 0, tiled=True)]
    all_to_all x1 -> x0, starting transfers between devices: 5.34 us -> none  [local(): sums = lax.all_to_all(squares, ('past', 'second'), 0, 0, tiled=True)]
    unnamed x16 -> x12, local copies, waits for them, and re-layouts: 6.12 us -> 1.81 us
    concatenate x1 -> x0, other arithmetic: 0.83 us -> none  [gather_past(): jnp.concatenate([jnp.where(upper, other, value), jnp.where(upper, value,...]
    pallas_call x2 -> x3, Pallas kernels: 1.46 us -> 1.98 us  [the longest x1 0.82 us: join(): pl.pallas_call(lambda *refs: join_kernel(*refs, mask=mask), in_specs=[VME...]
  transfers between devices with their start and end apart: 15 -> 14, of which waited for: 9 -> 8; matrix products, arithmetic and copies ran while one was open for 1% -> 0% of each run, Pallas kernels for 8% -> 11%
where the time goes in v3:
time: 59.3 us; the launch traced here: 59 us
  starting transfers between devices  19.3 us (33%)
  waiting for transfers between devices  14.2 us (24%)
  blocking collectives  12.3 us (21%)
  Pallas kernels  9.59 us (16%)
  local copies, waits for them, and re-layouts  1.84 us (3%)
  between operations  1.66 us (3%)
    ppermute x14, starting transfers between devices, exchange(): return lax.ppermute(value, axis, [(i, i ^ mask) for i in range(size)])  19.3 us
    ppermute x14, waiting for transfers between devices, exchange(): return lax.ppermute(value, axis, [(i, i ^ mask) for i in range(size)])  14.2 us
    all_to_all x1, blocking collectives, step(): sums = lax.all_to_all(squares, ('past', 'second'), 0, 0, tiled=True)  12.3 us
    pallas_call x3, Pallas kernels, integral(): pl.pallas_call(lambda *refs: integral_kernel(*refs, scale=scale, sides=si...  5.01 us
    unnamed x12, local copies, waits for them, and re-layouts  1.81 us
    pallas_call x1, Pallas kernels, owner_part(): pl.pallas_call(lambda *refs: owner_kernel(*refs, scale=scale), in_specs=[...  1.55 us
  transfers between devices with their start and end apart: 14, of which 8 were waited for; matrix products, arithmetic and copies ran while one was open for 0% of the time, Pallas kernels for 11%

profile of v3, /device:TPU:0, one launch (start us, length us, event | category | flops | bytes accessed | tf_op | source)
XLA Modules:
  0.0 59.0 jit_solution(5866154537577335811)
XLA Ops:
  0.6 0.0 copy-start
  1.5 0.0 copy-start.1
  1.5 1.0 %copy-done.1 = f32[16,64,128]{2,1,0:T(8,128)S(1)} copy-done((f32[16,64,128]{2,1,0:T(8,128)S(1)}, f32[16,64,128]{2,1,0:T(8,128)}, u32[]{:S(2)}) %copy-start.1) | copy-done | bytes 524312
  2.5 0.0 copy-start.3
  2.5 0.8 %copy-done.3 = f32[64,128]{1,0:T(8,128)S(1)} copy-done((f32[64,128]{1,0:T(8,128)S(1)}, f32[64,128]{1,0:T(8,128)}, u32[]{:S(2)}) %copy-start.3) | copy-done | bytes 32792
  3.3 0.6 prepare.1
  3.9 0.0 copy-done
  3.9 0.0 copy-done.4
  4.0 0.0 copy-done.5
  4.0 1.5 %owner_part.1 = (f32[2,2,64,128]{3,2,1,0:T(8,128)S(1)}, f32[2,2,64,128]{3,2,1,0:T(8,128)S(1)}) custom-call(s32[1]{0:T(128)} %copy.14.start_ref.refs_0_, f32[8]{0:T(128)S(1)} %copy-done.4, s32[4]{0:T(128)S(1)} %copy-done.5, f32[4,64,128]{2,1,0:T(8,128)S(1)} %get-tuple-element.37.refs_3_, f32[4,64,128]{2,1,0:T(8,128)S(1)} %get-tuple-element.32.refs_4_, ...), custom_call_target="tpu_custom_call" | custom-call | tf_op jit(solution)/shard_map/owner_part/pallas_call | solution.py:174
  5.5 0.6 collective-permute-start.10
  6.1 0.1 collective-permute-start.4
  6.2 0.9 %collective-permute-done.10 = f32[2,2,64,128]{3,2,1,0:T(8,128)S(1)} collective-permute-done((f32[2,2,64,128]{3,2,1,0:T(8,128)S(1)}, f32[2,2,64,128]{3,2,1,0:T(8,128)S(1)}, u32[]{:S(2)}, u32[]{:S(2)}) %collective-permute-start.10) | collective-permute-done | bytes 131104 | tf_op jit(solution)/shard_map/ppermute | solution.py:322
  7.1 2.9 %collective-permute-start.11 = (f32[1,2,64,128]{3,2,1,0:T(8,128)S(1)}, f32[1,2,64,128]{3,2,1,0:T(8,128)S(1)}, u32[]{:S(2)}, u32[]{:S(2)}) collective-permute-start(f32[1,2,64,128]{3,2,1,0:T(8,128)S(1)} %constant_dynamic-slice_fusion), channel_id=1, source_target_pairs={{0,16},{16,0},{1,17},{17,1},{2,18},{18,2},{3,19},{19,3},{4,20},{20... | collective-permute-start | bytes 196616 | tf_op jit(solution)/shard_map/ppermute | solution.py:322
  10.0 0.0 collective-permute-done.4
  10.1 1.6 %collective-permute-start.5 = (f32[2,64,128]{2,1,0:T(8,128)S(1)}, f32[2,64,128]{2,1,0:T(8,128)S(1)}, u32[]{:S(2)}, u32[]{:S(2)}) collective-permute-start(f32[2,64,128]{2,1,0:T(8,128)S(1)} %add.68), channel_id=1, source_target_pairs={{0,2},{1,3},{2,0},{3,1},{4,6},{5,7},{6,4},{7,5},{8,10},{9,11},{10,... | collective-permute-start | bytes 196616 | tf_op jit(solution)/shard_map/ppermute | solution.py:322
  11.6 0.8 %collective-permute-done.11 = f32[1,2,64,128]{3,2,1,0:T(8,128)S(1)} collective-permute-done((f32[1,2,64,128]{3,2,1,0:T(8,128)S(1)}, f32[1,2,64,128]{3,2,1,0:T(8,128)S(1)}, u32[]{:S(2)}, u32[]{:S(2)}) %collective-permute-start.11) | collective-permute-done | bytes 65568 | tf_op jit(solution)/shard_map/ppermute | solution.py:322
  12.5 1.9 %collective-permute-start.12 = (f32[2,64,128]{2,1,0:T(8,128)S(1)}, f32[2,64,128]{2,1,0:T(8,128)S(1)}, u32[]{:S(2)}, u32[]{:S(2)}) collective-permute-start(f32[2,64,128]{2,1,0:T(8,128)S(1)} %add_bitcast_fusion), channel_id=1, source_target_pairs={{0,2},{1,3},{2,0},{3,1},{4,6},{5,7},{6,4},{7,5},{8,10},{9,11},{10,... | collective-permute-start | bytes 196616 | tf_op jit(solution)/shard_map/ppermute | solution.py:322
  14.3 0.0 collective-permute-done.5
  14.4 1.6 %collective-permute-start.6 = (f32[2,64,128]{2,1,0:T(8,128)S(1)}, f32[2,64,128]{2,1,0:T(8,128)S(1)}, u32[]{:S(2)}, u32[]{:S(2)}) collective-permute-start(f32[2,64,128]{2,1,0:T(8,128)S(1)} %add.69), channel_id=1, source_target_pairs={{0,4},{1,5},{2,6},{3,7},{4,0},{5,1},{6,2},{7,3},{8,12},{9,13},{10,... | collective-permute-start | bytes 196616 | tf_op jit(solution)/shard_map/ppermute | solution.py:322
  16.0 0.7 %collective-permute-done.12 = f32[2,64,128]{2,1,0:T(8,128)S(1)} collective-permute-done((f32[2,64,128]{2,1,0:T(8,128)S(1)}, f32[2,64,128]{2,1,0:T(8,128)S(1)}, u32[]{:S(2)}, u32[]{:S(2)}) %collective-permute-start.12) | collective-permute-done | bytes 65568 | tf_op jit(solution)/shard_map/ppermute | solution.py:322
  16.8 2.0 %collective-permute-start.13 = (f32[2,64,128]{2,1,0:T(8,128)S(1)}, f32[2,64,128]{2,1,0:T(8,128)S(1)}, u32[]{:S(2)}, u32[]{:S(2)}) collective-permute-start(f32[2,64,128]{2,1,0:T(8,128)S(1)} %add.81), channel_id=1, source_target_pairs={{0,4},{1,5},{2,6},{3,7},{4,0},{5,1},{6,2},{7,3},{8,12},{9,13},{10,... | collective-permute-start | bytes 196616 | tf_op jit(solution)/shard_map/ppermute | solution.py:322
  18.8 0.5 collective-permute-done.6
  19.3 2.4 %collective-permute-start.7 = (f32[2,64,128]{2,1,0:T(8,128)S(1)}, f32[2,64,128]{2,1,0:T(8,128)S(1)}, u32[]{:S(2)}, u32[]{:S(2)}) collective-permute-start(f32[2,64,128]{2,1,0:T(8,128)S(1)} %add.70), channel_id=1, source_target_pairs={{0,8},{1,9},{2,10},{3,11},{4,12},{5,13},{6,14},{7,15},{8,0},{9,1},... | collective-permute-start | bytes 196616 | tf_op jit(solution)/shard_map/ppermute | solution.py:322
  21.7 0.0 collective-permute-done.13
  21.7 2.4 %collective-permute-start.14 = (f32[2,64,128]{2,1,0:T(8,128)S(1)}, f32[2,64,128]{2,1,0:T(8,128)S(1)}, u32[]{:S(2)}, u32[]{:S(2)}) collective-permute-start(f32[2,64,128]{2,1,0:T(8,128)S(1)} %add.82), channel_id=1, source_target_pairs={{0,8},{1,9},{2,10},{3,11},{4,12},{5,13},{6,14},{7,15},{8,0},{9,1},... | collective-permute-start | bytes 196616 | tf_op jit(solution)/shard_map/ppermute | solution.py:322
  24.1 1.5 %collective-permute-done.7 = f32[2,64,128]{2,1,0:T(8,128)S(1)} collective-permute-done((f32[2,64,128]{2,1,0:T(8,128)S(1)}, f32[2,64,128]{2,1,0:T(8,128)S(1)}, u32[]{:S(2)}, u32[]{:S(2)}) %collective-permute-start.7) | collective-permute-done | bytes 65568 | tf_op jit(solution)/shard_map/ppermute | solution.py:322
  25.7 0.1 collective-permute-start.8
  25.8 1.2 %collective-permute-done.14 = f32[2,64,128]{2,1,0:T(8,128)S(1)} collective-permute-done((f32[2,64,128]{2,1,0:T(8,128)S(1)}, f32[2,64,128]{2,1,0:T(8,128)S(1)}, u32[]{:S(2)}, u32[]{:S(2)}) %collective-permute-start.14) | collective-permute-done | bytes 65568 | tf_op jit(solution)/shard_map/ppermute | solution.py:322
  27.0 0.1 collective-permute-start.15
  27.1 0.0 collective-permute-done.8.refs_3_
  27.1 2.1 %shard_map.77 = (f32[8,64,128]{2,1,0:T(8,128)S(1)}, f32[8,64,128]{2,1,0:T(8,128)S(1)}) custom-call(f32[8]{0:T(128)S(1)} %copy-done.4, s32[4]{0:T(128)S(1)} %copy-done.5, f32[2,64,128]{2,1,0:T(8,128)S(1)} %add.71.refs_2_, f32[2,64,128]{2,1,0:T(8,128)S(1)} %collective-permute-done.8.refs_3_, f32[4,16,64,128]{3,2,1,0:T(8,128)S(1)} %copy-done), custom_call_target="tpu_custom_call" | custom-call | tf_op jit(solution)/shard_map/pallas_call | solution.py:210
  29.1 0.0 copy-start.2
  29.2 1.6 %collective-permute-start.9 = (f32[8,64,128]{2,1,0:T(8,128)S(1)}, f32[8,64,128]{2,1,0:T(8,128)S(1)}, u32[]{:S(2)}, u32[]{:S(2)}) collective-permute-start(f32[8,64,128]{2,1,0:T(8,128)S(1)} %get-tuple-element.28), channel_id=1, source_target_pairs={{0,16},{16,0},{1,17},{17,1},{2,18},{18,2},{3,19},{19,3},{4,20},{20... | collective-permute-start | bytes 786440 | tf_op jit(solution)/shard_map/ppermute | solution.py:322
  30.7 0.0 collective-permute-done.15.refs_3_
  30.7 1.5 %shard_map.79 = f32[8,64,128]{2,1,0:T(8,128)S(1)} custom-call(f32[8]{0:T(128)S(1)} %copy-done.4, s32[4]{0:T(128)S(1)} %copy-done.5, f32[2,64,128]{2,1,0:T(8,128)S(1)} %add.83.refs_2_, f32[2,64,128]{2,1,0:T(8,128)S(1)} %collective-permute-done.15.refs_3_, f32[4,16,64,128]{3,2,1,0:T(8,128)S(1)} %copy-done), custom_call_target="tpu_custom_call" | custom-call | tf_op jit(solution)/shard_map/pallas_call | solution.py:210
  32.2 0.6 collective-permute-start.16
  32.8 1.5 %shard_map.78.mine_ref = f32[8,64,128]{2,1,0:T(8,128)S(1)} custom-call(f32[8]{0:T(128)S(1)} %copy-done.4, s32[4]{0:T(128)S(1)} %copy-done.5, f32[2,64,128]{2,1,0:T(8,128)S(1)} %add.83.refs_2_, f32[2,64,128]{2,1,0:T(8,128)S(1)} %collective-permute-done.15.refs_3_, f32[4,16,64,128]{3,2,1,0:T(8,128)S(1)} %copy-done), custom_call_target="tpu_custom_call" | custom-call | tf_op jit(solution)/shard_map/pallas_call | solution.py:210
  34.3 4.1 %collective-permute-done.9.recv_ref = f32[8,64,128]{2,1,0:T(8,128)S(1)} collective-permute-done((f32[8,64,128]{2,1,0:T(8,128)S(1)}, f32[8,64,128]{2,1,0:T(8,128)S(1)}, u32[]{:S(2)}, u32[]{:S(2)}) %collective-permute-start.9) | collective-permute-done | bytes 262176 | tf_op jit(solution)/shard_map/ppermute | solution.py:322
  38.4 0.0 copy-done.2
  38.4 0.9 %share_bases.1 = (f32[8,64,128]{2,1,0:T(8,128)S(1)}, f32[8,64,128]{2,1,0:T(8,128)S(1)}) custom-call(f32[16,64,128]{2,1,0:T(8,128)S(1)} %copy-done.2, f32[8,64,128]{2,1,0:T(8,128)S(1)} %get-tuple-element.27.mine_ref, f32[8,64,128]{2,1,0:T(8,128)S(1)} %collective-permute-done.9.recv_ref, f32[128,64]{1,0:T(8,128)S(1)} %get-tuple-element.29.herm_ref.refs_5_), custom_call_target="tpu_custom_call" | custom-call | tf_op jit(solution)/shard_map/share_bases/pallas_call | solution.py:248
  39.3 4.3 %collective-permute-done.16.recv_ref = f32[8,64,128]{2,1,0:T(8,128)S(1)} collective-permute-done((f32[8,64,128]{2,1,0:T(8,128)S(1)}, f32[8,64,128]{2,1,0:T(8,128)S(1)}, u32[]{:S(2)}, u32[]{:S(2)}) %collective-permute-start.16) | collective-permute-done | bytes 262176 | tf_op jit(solution)/shard_map/ppermute | solution.py:322
  43.5 0.2 finish.1
  43.7 1.6 %collective-permute-start.17 = (f32[8,64,128]{2,1,0:T(8,128)S(1)}, f32[8,64,128]{2,1,0:T(8,128)S(1)}, u32[]{:S(2)}, u32[]{:S(2)}) collective-permute-start(f32[8,64,128]{2,1,0:T(8,128)S(1)} %get-tuple-element.35.refs_0_), channel_id=1, source_target_pairs={{0,16},{16,0},{1,17},{17,1},{2,18},{18,2},{3,19},{19,3},{4,20},{20... | collective-permute-start | bytes 786440 | tf_op jit(solution)/shard_map/ppermute | solution.py:322
  45.3 12.3 %all_to_all.11 = f32[32,1,128]{2,1,0:T(1,128)S(1)} all-to-all(f32[32,1,128]{2,1,0:T(1,128)S(1)} %bitcast.12), channel_id=1, replica_groups=mesh['past'=2,'second'=16] {'past','second'}, dimensions={0} | all-to-all | bytes 32768 | tf_op jit(solution)/shard_map/all_to_all | solution.py:415
  57.6 0.6 norm.1
  58.2 0.0 collective-permute-done.17.refs_1_
  58.2 0.8 %join.1 = f32[16,64,128]{2,1,0:T(8,128)} custom-call(f32[8,64,128]{2,1,0:T(8,128)S(1)} %get-tuple-element.35.refs_0_, f32[8,64,128]{2,1,0:T(8,128)S(1)} %collective-permute-done.17.refs_1_), custom_call_target="tpu_custom_call" | custom-call | tf_op jit(solution)/shard_map/join/pallas_call | solution.py:309
  (14 shorter events, 0.2 us)
Async XLA Ops:
  0.6 3.3 %copy-start = (f32[4,16,64,128]{3,2,1,0:T(8,128)S(1)}, f32[4,16,64,128]{3,2,1,0:T(8,128)}, u32[]{:S(2)}) copy-start(f32[4,16,64,128]{3,2,1,0:T(8,128)} %refs_4_.5) | copy-start | bytes 6291460
  1.5 1.0 %copy-start.1 = (f32[16,64,128]{2,1,0:T(8,128)S(1)}, f32[16,64,128]{2,1,0:T(8,128)}, u32[]{:S(2)}) copy-start(f32[16,64,128]{2,1,0:T(8,128)} %row_ref.3) | copy-start | bytes 1572868
  2.5 0.8 %copy-start.3 = (f32[64,128]{1,0:T(8,128)S(1)}, f32[64,128]{1,0:T(8,128)}, u32[]{:S(2)}) copy-start(f32[64,128]{1,0:T(8,128)} %ham_hbm.1) | copy-start | bytes 98308
  3.3 0.7 %copy-start.4 = (f32[8]{0:T(128)S(1)}, f32[8]{0:T(128)}, u32[]{:S(2)}) copy-start(f32[8]{0:T(128)} %refs_0_.6) | copy-start | bytes 100
  3.3 0.7 %copy-start.5 = (s32[4]{0:T(128)S(1)}, s32[4]{0:T(128)}, u32[]{:S(2)}) copy-start(s32[4]{0:T(128)} %refs_1_.7) | copy-start | bytes 52
  5.5 1.5 %collective-permute-start.10 = (f32[2,2,64,128]{3,2,1,0:T(8,128)S(1)}, f32[2,2,64,128]{3,2,1,0:T(8,128)S(1)}, u32[]{:S(2)}, u32[]{:S(2)}) collective-permute-start(f32[2,2,64,128]{3,2,1,0:T(8,128)S(1)} %get-tuple-element.34), channel_id=1, source_target_pairs={{0,1},{1,0},{2,3},{3,2},{4,5},{5,4},{6,7},{7,6},{8,9},{9,8},{10,11... | collective-permute-start | bytes 393224 | tf_op jit(solution)/shard_map/ppermute | solution.py:322
  6.1 4.0 %collective-permute-start.4 = (f32[2,64,128]{2,1,0:T(8,128)S(1)}, f32[2,64,128]{2,1,0:T(8,128)S(1)}, u32[]{:S(2)}, u32[]{:S(2)}) collective-permute-start(f32[2,64,128]{2,1,0:T(8,128)S(1)} %get-tuple-element.26), channel_id=1, source_target_pairs={{0,1},{1,0},{2,3},{3,2},{4,5},{5,4},{6,7},{7,6},{8,9},{9,8},{10,11... | collective-permute-start | bytes 196616 | tf_op jit(solution)/shard_map/ppermute | solution.py:322
  7.1 5.3 %collective-permute-start.11 = (f32[1,2,64,128]{3,2,1,0:T(8,128)S(1)}, f32[1,2,64,128]{3,2,1,0:T(8,128)S(1)}, u32[]{:S(2)}, u32[]{:S(2)}) collective-permute-start(f32[1,2,64,128]{3,2,1,0:T(8,128)S(1)} %constant_dynamic-slice_fusion), channel_id=1, source_target_pairs={{0,16},{16,0},{1,17},{17,1},{2,18},{18,2},{3,19},{19,3},{4,20},{20... | collective-permute-start | bytes 196616 | tf_op jit(solution)/shard_map/ppermute | solution.py:322
  10.1 4.3 %collective-permute-start.5 = (f32[2,64,128]{2,1,0:T(8,128)S(1)}, f32[2,64,128]{2,1,0:T(8,128)S(1)}, u32[]{:S(2)}, u32[]{:S(2)}) collective-permute-start(f32[2,64,128]{2,1,0:T(8,128)S(1)} %add.68), channel_id=1, source_target_pairs={{0,2},{1,3},{2,0},{3,1},{4,6},{5,7},{6,4},{7,5},{8,10},{9,11},{10,... | collective-permute-start | bytes 196616 | tf_op jit(solution)/shard_map/ppermute | solution.py:322
  12.5 4.3 %collective-permute-start.12 = (f32[2,64,128]{2,1,0:T(8,128)S(1)}, f32[2,64,128]{2,1,0:T(8,128)S(1)}, u32[]{:S(2)}, u32[]{:S(2)}) collective-permute-start(f32[2,64,128]{2,1,0:T(8,128)S(1)} %add_bitcast_fusion), channel_id=1, source_target_pairs={{0,2},{1,3},{2,0},{3,1},{4,6},{5,7},{6,4},{7,5},{8,10},{9,11},{10,... | collective-permute-start | bytes 196616 | tf_op jit(solution)/shard_map/ppermute | solution.py:322
  14.4 4.9 %collective-permute-start.6 = (f32[2,64,128]{2,1,0:T(8,128)S(1)}, f32[2,64,128]{2,1,0:T(8,128)S(1)}, u32[]{:S(2)}, u32[]{:S(2)}) collective-permute-start(f32[2,64,128]{2,1,0:T(8,128)S(1)} %add.69), channel_id=1, source_target_pairs={{0,4},{1,5},{2,6},{3,7},{4,0},{5,1},{6,2},{7,3},{8,12},{9,13},{10,... | collective-permute-start | bytes 196616 | tf_op jit(solution)/shard_map/ppermute | solution.py:322
  16.8 4.9 %collective-permute-start.13 = (f32[2,64,128]{2,1,0:T(8,128)S(1)}, f32[2,64,128]{2,1,0:T(8,128)S(1)}, u32[]{:S(2)}, u32[]{:S(2)}) collective-permute-start(f32[2,64,128]{2,1,0:T(8,128)S(1)} %add.81), channel_id=1, source_target_pairs={{0,4},{1,5},{2,6},{3,7},{4,0},{5,1},{6,2},{7,3},{8,12},{9,13},{10,... | collective-permute-start | bytes 196616 | tf_op jit(solution)/shard_map/ppermute | solution.py:322
  19.3 6.4 %collective-permute-start.7 = (f32[2,64,128]{2,1,0:T(8,128)S(1)}, f32[2,64,128]{2,1,0:T(8,128)S(1)}, u32[]{:S(2)}, u32[]{:S(2)}) collective-permute-start(f32[2,64,128]{2,1,0:T(8,128)S(1)} %add.70), channel_id=1, source_target_pairs={{0,8},{1,9},{2,10},{3,11},{4,12},{5,13},{6,14},{7,15},{8,0},{9,1},... | collective-permute-start | bytes 196616 | tf_op jit(solution)/shard_map/ppermute | solution.py:322
  21.7 5.2 %collective-permute-start.14 = (f32[2,64,128]{2,1,0:T(8,128)S(1)}, f32[2,64,128]{2,1,0:T(8,128)S(1)}, u32[]{:S(2)}, u32[]{:S(2)}) collective-permute-start(f32[2,64,128]{2,1,0:T(8,128)S(1)} %add.82), channel_id=1, source_target_pairs={{0,8},{1,9},{2,10},{3,11},{4,12},{5,13},{6,14},{7,15},{8,0},{9,1},... | collective-permute-start | bytes 196616 | tf_op jit(solution)/shard_map/ppermute | solution.py:322
  25.7 1.4 %collective-permute-start.8 = (f32[2,64,128]{2,1,0:T(8,128)S(1)}, f32[2,64,128]{2,1,0:T(8,128)S(1)}, u32[]{:S(2)}, u32[]{:S(2)}) collective-permute-start(f32[2,64,128]{2,1,0:T(8,128)S(1)} %add.71.refs_2_), channel_id=1, source_target_pairs={{0,1},{1,0},{2,3},{3,2},{4,5},{5,4},{6,7},{7,6},{8,9},{9,8},{10,11... | collective-permute-start | bytes 196616 | tf_op jit(solution)/shard_map/ppermute | solution.py:322
  27.0 3.8 %collective-permute-start.15 = (f32[2,64,128]{2,1,0:T(8,128)S(1)}, f32[2,64,128]{2,1,0:T(8,128)S(1)}, u32[]{:S(2)}, u32[]{:S(2)}) collective-permute-start(f32[2,64,128]{2,1,0:T(8,128)S(1)} %add.83.refs_2_), channel_id=1, source_target_pairs={{0,1},{1,0},{2,3},{3,2},{4,5},{5,4},{6,7},{7,6},{8,9},{9,8},{10,11... | collective-permute-start | bytes 196616 | tf_op jit(solution)/shard_map/ppermute | solution.py:322
  29.1 9.3 %copy-start.2 = (f32[16,64,128]{2,1,0:T(8,128)S(1)}, f32[16,64,128]{2,1,0:T(8,128)}, u32[]{:S(2)}) copy-start(f32[16,64,128]{2,1,0:T(8,128)} %row_ref.3) | copy-start | bytes 1572868
  29.2 9.2 %collective-permute-start.9 = (f32[8,64,128]{2,1,0:T(8,128)S(1)}, f32[8,64,128]{2,1,0:T(8,128)S(1)}, u32[]{:S(2)}, u32[]{:S(2)}) collective-permute-start(f32[8,64,128]{2,1,0:T(8,128)S(1)} %get-tuple-element.28), channel_id=1, source_target_pairs={{0,16},{16,0},{1,17},{17,1},{2,18},{18,2},{3,19},{19,3},{4,20},{20... | collective-permute-start | bytes 786440 | tf_op jit(solution)/shard_map/ppermute | solution.py:322
  32.2 11.3 %collective-permute-start.16 = (f32[8,64,128]{2,1,0:T(8,128)S(1)}, f32[8,64,128]{2,1,0:T(8,128)S(1)}, u32[]{:S(2)}, u32[]{:S(2)}) collective-permute-start(f32[8,64,128]{2,1,0:T(8,128)S(1)} %shard_map.79), channel_id=1, source_target_pairs={{0,16},{16,0},{1,17},{17,1},{2,18},{18,2},{3,19},{19,3},{4,20},{20... | collective-permute-start | bytes 786440 | tf_op jit(solution)/shard_map/ppermute | solution.py:322
  43.7 14.5 %collective-permute-start.17 = (f32[8,64,128]{2,1,0:T(8,128)S(1)}, f32[8,64,128]{2,1,0:T(8,128)S(1)}, u32[]{:S(2)}, u32[]{:S(2)}) collective-permute-start(f32[8,64,128]{2,1,0:T(8,128)S(1)} %get-tuple-element.35.refs_0_), channel_id=1, source_target_pairs={{0,16},{16,0},{1,17},{17,1},{2,18},{18,2},{3,19},{19,3},{4,20},{20... | collective-permute-start | bytes 786440 | tf_op jit(solution)/shard_map/ppermute | solution.py:322

commit v4 on v3

--- a/solution.py
+++ b/solution.py
@@ -56,6 +56,10 @@
     return jnp.concatenate(
         [jnp.where(real, scaled, swap_halves(plain)), jnp.where(real, swap_halves(scaled), plain)], axis=0
     )
+
+
+def in_hbm(value):
+    return pltpu.with_memory_space_constraint(value, pltpu.HBM)
 
 
 def local_spot(start_ref, tile, sec_rows):
@@ -113,7 +117,7 @@
         ],
         compiler_params=PARAMS,
         name="prepare",
-    )(block_start, green_row, hamiltonian)
+    )(block_start, in_hbm(green_row), in_hbm(hamiltonian))
 
 
 def put_left(left_high, left_low, p, tile, weight):
@@ -255,22 +259,25 @@
     )(green_row, mine, recv, herm)
 
 
-def finish_kernel(out_base_ref, diff_base_ref, mine_ref, recv_ref, out_ref, square_ref):
-    total = jnp.zeros(out_ref.shape[1:], f32)
-    for s in range(out_ref.shape[0]):
+def finish_kernel(out_base_ref, diff_base_ref, mine_ref, recv_ref, square_ref, *out_refs):
+    total = jnp.zeros(mine_ref.shape[1:], f32)
+    for s in range(mine_ref.shape[0]):
         last = mine_ref[s] + recv_ref[s]
-        out_ref[s] = out_base_ref[s] + last
+        rows = out_refs[0].shape[0]
+        out_refs[s // rows][s % rows] = out_base_ref[s] + last
         diff = diff_base_ref[s] + last
         total = total + diff * diff
     square_ref[...] = jnp.broadcast_to(jnp.sum(total), square_ref.shape)
 
 
 def finish(out_base, diff_base, mine, recv, devices):
+    chunks = 2 if mine.shape[0] % 2 == 0 else 1
+    chunk = jax.ShapeDtypeStruct((mine.shape[0] // chunks,) + mine.shape[1:], f32)
     return pl.pallas_call(
         finish_kernel,
         in_specs=[VMEM_SPEC] * 4,
-        out_specs=[VMEM_SPEC] * 2,
-        out_shape=[jax.ShapeDtypeStruct(mine.shape, f32), jax.ShapeDtypeStruct((devices, 128), f32)],
+        out_specs=[VMEM_SPEC] * (1 + chunks),
+        out_shape=[jax.ShapeDtypeStruct((devices, 128), f32)] + [chunk] * chunks,
         compiler_params=PARAMS,
         name="finish",
     )(out_base, diff_base, mine, recv)
@@ -292,13 +299,15 @@
     )(sums)
 
 
-def join_kernel(own_ref, other_ref, out_ref, sems, *, mask):
-    count = own_ref.shape[0]
+def join_kernel(*refs, mask, chunks):
+    own, other, out_ref, sems = refs[:chunks], refs[chunks : 2 * chunks], refs[-2], refs[-1]
+    rows = own[0].shape[0]
     upper = lax.axis_index("past") // mask % 2
-    copies = [
-        pltpu.make_async_copy(own_ref, out_ref.at[pl.ds(upper * count, count)], sems.at[0]),
-        pltpu.make_async_copy(other_ref, out_ref.at[pl.ds((1 - upper) * count, count)], sems.at[1]),
-    ]
+    copies = []
+    for side, parts in ((upper, own), (1 - upper, other)):
+        for i, part in enumerate(parts):
+            target = out_ref.at[pl.ds((side * chunks + i) * rows, rows)]
+            copies.append(pltpu.make_async_copy(part, target, sems.at[len(copies)]))
     for copy in copies:
         copy.start()
     for copy in copies:
@@ -306,15 +315,17 @@
 
 
 def join(own, other, mask):
-    return pl.pallas_call(
-        lambda *refs: join_kernel(*refs, mask=mask),
-        in_specs=[VMEM_SPEC, VMEM_SPEC],
+    chunks = len(own)
+    rows = 2 * chunks * own[0].shape[0]
+    return pl.pallas_call(
+        lambda *refs: join_kernel(*refs, mask=mask, chunks=chunks),
+        in_specs=[VMEM_SPEC] * (2 * chunks),
         out_specs=HBM_SPEC,
-        out_shape=jax.ShapeDtypeStruct((2 * own.shape[0],) + own.shape[1:], f32),
-        scratch_shapes=[pltpu.SemaphoreType.DMA((2,))],
+        out_shape=jax.ShapeDtypeStruct((rows,) + own[0].shape[1:], f32),
+        scratch_shapes=[pltpu.SemaphoreType.DMA((2 * chunks,))],
         compiler_params=PARAMS,
         name="join",
-    )(own, other)
+    )(*own, *other)
 
 
 def exchange(value, axis, mask):
@@ -352,12 +363,13 @@
     return keep, received
 
 
-def gather_past(value):
+def gather_past(chunks):
     mask = 1
     while mask < lax.axis_size("past"):
-        value = join(value, exchange(value, "past", mask), mask)
+        others = [exchange(c, "past", mask) for c in chunks]
+        chunks = [join(chunks, others, mask)]
         mask *= 2
-    return value
+    return chunks[0]
 
 
 def spread_second(value):
@@ -410,10 +422,10 @@
     (last_send,) = integral(quad_table, weight_index, pred_mine, pred_other, green_hist, past_size, (False,), final)
     (last_keep,) = integral(quad_table, weight_index, pred_mine, pred_other, green_hist, past_size, (True,), final)
     devices = past_size * second_size
-    out_share, squares = finish(out_base, diff_base, *share_past(last_keep, last_send), devices)
+    squares, *out_chunks = finish(out_base, diff_base, *share_past(last_keep, last_send), devices)
 
     sums = lax.all_to_all(squares, ("past", "second"), 0, 0, tiled=True)
-    green_next = gather_past(out_share)
+    green_next = gather_past(out_chunks)
     return (green_next, norm(sums, sec_rows * second_size * orbits * width))
 
 

time: 59.3 us -> 59.6 us (level)
  local copies, waits for them, and re-layouts: 1.84 us -> 0.04 us
  blocking collectives: 12.3 us -> 13.3 us
  Pallas kernels: 9.59 us -> 10.2 us
    unnamed x12 -> x8, local copies, waits for them, and re-layouts: 1.81 us -> 0.02 us
    all_to_all x1, blocking collectives: 12.3 us -> 13.3 us  [step(): sums = lax.all_to_all(squares, ('past', 'second'), 0, 0, tiled=True)]
    pallas_call x1, Pallas kernels: 0.59 us -> 1.24 us  [prepare(): pl.pallas_call(prepare_kernel, in_specs=[SMEM_SPEC, HBM_SPEC, HBM_SPEC],...]
    ppermute x14 -> x15, starting transfers between devices: 19.3 us -> 19.8 us  [exchange(): return lax.ppermute(value, axis, [(i, i ^ mask) for i in range(size)])]
    ppermute x14 -> x15, waiting for transfers between devices: 14.2 us -> 14.2 us  [exchange(): return lax.ppermute(value, axis, [(i, i ^ mask) for i in range(size)])]
  transfers between devices with their start and end apart: 14 -> 15, of which waited for: 8 -> 8; matrix products, arithmetic and copies ran while one was open for 0% -> 0% of each run, Pallas kernels for 11% -> 11%
where the time goes in v4:
time: 59.6 us; the launch traced here: 59.4 us
  starting transfers between devices  19.8 us (33%)
  waiting for transfers between devices  14.2 us (24%)
  blocking collectives  13.3 us (22%)
  Pallas kernels  10.2 us (17%)
  between operations  1.67 us (3%)
    ppermute x15, starting transfers between devices, exchange(): return lax.ppermute(value, axis, [(i, i ^ mask) for i in range(size)])  19.8 us
    ppermute x15, waiting for transfers between devices, exchange(): return lax.ppermute(value, axis, [(i, i ^ mask) for i in range(size)])  14.2 us
    all_to_all x1, blocking collectives, step(): sums = lax.all_to_all(squares, ('past', 'second'), 0, 0, tiled=True)  13.3 us
    pallas_call x3, Pallas kernels, integral(): pl.pallas_call(lambda *refs: integral_kernel(*refs, scale=scale, sides=si...  5.01 us
    pallas_call x1, Pallas kernels, owner_part(): pl.pallas_call(lambda *refs: owner_kernel(*refs, scale=scale), in_specs=[...  1.55 us
    pallas_call x1, Pallas kernels, prepare(): pl.pallas_call(prepare_kernel, in_specs=[SMEM_SPEC, HBM_SPEC, HBM_SPEC],...  1.24 us
  transfers between devices with their start and end apart: 15, of which 8 were waited for; matrix products, arithmetic and copies ran while one was open for 0% of the time, Pallas kernels for 11%

profile of v4, /device:TPU:0, one launch (start us, length us, event | category | flops | bytes accessed | tf_op | source)
XLA Modules:
  0.0 59.4 jit_solution(1218471963598295887)
XLA Ops:
  0.6 0.0 copy-start.2
  0.6 0.0 copy-start.3
  0.7 0.0 copy-start
  1.5 1.2 %prepare.1 = (f32[4,64,128]{2,1,0:T(8,128)S(1)}, f32[2,64,128]{2,1,0:T(8,128)S(1)}, f32[2,64,128]{2,1,0:T(8,128)S(1)}, f32[128,64]{1,0:T(8,128)S(1)}) custom-call(s32[1]{0:T(128)} %copy.14.start_ref.refs_0_, f32[16,64,128]{2,1,0:T(8,128)} %row_ref.3, f32[64,128]{1,0:T(8,128)} %ham_hbm.1), custom_call_target="tpu_custom_call" | custom-call | tf_op jit(solution)/shard_map/prepare/pallas_call | solution.py:103
  2.8 0.0 copy-done.2
  2.8 0.0 copy-done.3
  2.8 0.0 copy-done
  2.8 1.5 %owner_part.1 = (f32[2,2,64,128]{3,2,1,0:T(8,128)S(1)}, f32[2,2,64,128]{3,2,1,0:T(8,128)S(1)}) custom-call(s32[1]{0:T(128)} %copy.14.start_ref.refs_0_, f32[8]{0:T(128)S(1)} %copy-done.2, s32[4]{0:T(128)S(1)} %copy-done.3, f32[4,64,128]{2,1,0:T(8,128)S(1)} %get-tuple-element.39.refs_3_, f32[4,64,128]{2,1,0:T(8,128)S(1)} %get-tuple-element.33.refs_4_, ...), custom_call_target="tpu_custom_call" | custom-call | tf_op jit(solution)/shard_map/owner_part/pallas_call | solution.py:178
  4.4 0.6 collective-permute-start.10
  4.9 0.1 collective-permute-start.4
  5.0 0.9 %collective-permute-done.10 = f32[2,2,64,128]{3,2,1,0:T(8,128)S(1)} collective-permute-done((f32[2,2,64,128]{3,2,1,0:T(8,128)S(1)}, f32[2,2,64,128]{3,2,1,0:T(8,128)S(1)}, u32[]{:S(2)}, u32[]{:S(2)}) %collective-permute-start.10) | collective-permute-done | bytes 131104 | tf_op jit(solution)/shard_map/ppermute | solution.py:333
  6.0 2.9 %collective-permute-start.11 = (f32[1,2,64,128]{3,2,1,0:T(8,128)S(1)}, f32[1,2,64,128]{3,2,1,0:T(8,128)S(1)}, u32[]{:S(2)}, u32[]{:S(2)}) collective-permute-start(f32[1,2,64,128]{3,2,1,0:T(8,128)S(1)} %constant_dynamic-slice_fusion), channel_id=1, source_target_pairs={{0,16},{16,0},{1,17},{17,1},{2,18},{18,2},{3,19},{19,3},{4,20},{20... | collective-permute-start | bytes 196616 | tf_op jit(solution)/shard_map/ppermute | solution.py:333
  8.9 0.0 collective-permute-done.4
  8.9 1.6 %collective-permute-start.5 = (f32[2,64,128]{2,1,0:T(8,128)S(1)}, f32[2,64,128]{2,1,0:T(8,128)S(1)}, u32[]{:S(2)}, u32[]{:S(2)}) collective-permute-start(f32[2,64,128]{2,1,0:T(8,128)S(1)} %add.68), channel_id=1, source_target_pairs={{0,2},{1,3},{2,0},{3,1},{4,6},{5,7},{6,4},{7,5},{8,10},{9,11},{10,... | collective-permute-start | bytes 196616 | tf_op jit(solution)/shard_map/ppermute | solution.py:333
  10.5 0.8 %collective-permute-done.11 = f32[1,2,64,128]{3,2,1,0:T(8,128)S(1)} collective-permute-done((f32[1,2,64,128]{3,2,1,0:T(8,128)S(1)}, f32[1,2,64,128]{3,2,1,0:T(8,128)S(1)}, u32[]{:S(2)}, u32[]{:S(2)}) %collective-permute-start.11) | collective-permute-done | bytes 65568 | tf_op jit(solution)/shard_map/ppermute | solution.py:333
  11.3 1.9 %collective-permute-start.12 = (f32[2,64,128]{2,1,0:T(8,128)S(1)}, f32[2,64,128]{2,1,0:T(8,128)S(1)}, u32[]{:S(2)}, u32[]{:S(2)}) collective-permute-start(f32[2,64,128]{2,1,0:T(8,128)S(1)} %add_bitcast_fusion), channel_id=1, source_target_pairs={{0,2},{1,3},{2,0},{3,1},{4,6},{5,7},{6,4},{7,5},{8,10},{9,11},{10,... | collective-permute-start | bytes 196616 | tf_op jit(solution)/shard_map/ppermute | solution.py:333
  13.2 0.0 collective-permute-done.5
  13.3 1.6 %collective-permute-start.6 = (f32[2,64,128]{2,1,0:T(8,128)S(1)}, f32[2,64,128]{2,1,0:T(8,128)S(1)}, u32[]{:S(2)}, u32[]{:S(2)}) collective-permute-start(f32[2,64,128]{2,1,0:T(8,128)S(1)} %add.69), channel_id=1, source_target_pairs={{0,4},{1,5},{2,6},{3,7},{4,0},{5,1},{6,2},{7,3},{8,12},{9,13},{10,... | collective-permute-start | bytes 196616 | tf_op jit(solution)/shard_map/ppermute | solution.py:333
  14.9 0.7 %collective-permute-done.12 = f32[2,64,128]{2,1,0:T(8,128)S(1)} collective-permute-done((f32[2,64,128]{2,1,0:T(8,128)S(1)}, f32[2,64,128]{2,1,0:T(8,128)S(1)}, u32[]{:S(2)}, u32[]{:S(2)}) %collective-permute-start.12) | collective-permute-done | bytes 65568 | tf_op jit(solution)/shard_map/ppermute | solution.py:333
  15.7 2.0 %collective-permute-start.13 = (f32[2,64,128]{2,1,0:T(8,128)S(1)}, f32[2,64,128]{2,1,0:T(8,128)S(1)}, u32[]{:S(2)}, u32[]{:S(2)}) collective-permute-start(f32[2,64,128]{2,1,0:T(8,128)S(1)} %add.81), channel_id=1, source_target_pairs={{0,4},{1,5},{2,6},{3,7},{4,0},{5,1},{6,2},{7,3},{8,12},{9,13},{10,... | collective-permute-start | bytes 196616 | tf_op jit(solution)/shard_map/ppermute | solution.py:333
  17.6 0.5 collective-permute-done.6
  18.2 2.4 %collective-permute-start.7 = (f32[2,64,128]{2,1,0:T(8,128)S(1)}, f32[2,64,128]{2,1,0:T(8,128)S(1)}, u32[]{:S(2)}, u32[]{:S(2)}) collective-permute-start(f32[2,64,128]{2,1,0:T(8,128)S(1)} %add.70), channel_id=1, source_target_pairs={{0,8},{1,9},{2,10},{3,11},{4,12},{5,13},{6,14},{7,15},{8,0},{9,1},... | collective-permute-start | bytes 196616 | tf_op jit(solution)/shard_map/ppermute | solution.py:333
  20.6 0.0 collective-permute-done.13
  20.6 2.4 %collective-permute-start.14 = (f32[2,64,128]{2,1,0:T(8,128)S(1)}, f32[2,64,128]{2,1,0:T(8,128)S(1)}, u32[]{:S(2)}, u32[]{:S(2)}) collective-permute-start(f32[2,64,128]{2,1,0:T(8,128)S(1)} %add.82), channel_id=1, source_target_pairs={{0,8},{1,9},{2,10},{3,11},{4,12},{5,13},{6,14},{7,15},{8,0},{9,1},... | collective-permute-start | bytes 196616 | tf_op jit(solution)/shard_map/ppermute | solution.py:333
  23.0 1.5 %collective-permute-done.7 = f32[2,64,128]{2,1,0:T(8,128)S(1)} collective-permute-done((f32[2,64,128]{2,1,0:T(8,128)S(1)}, f32[2,64,128]{2,1,0:T(8,128)S(1)}, u32[]{:S(2)}, u32[]{:S(2)}) %collective-permute-start.7) | collective-permute-done | bytes 65568 | tf_op jit(solution)/shard_map/ppermute | solution.py:333
  24.5 0.1 collective-permute-start.8
  24.6 1.2 %collective-permute-done.14 = f32[2,64,128]{2,1,0:T(8,128)S(1)} collective-permute-done((f32[2,64,128]{2,1,0:T(8,128)S(1)}, f32[2,64,128]{2,1,0:T(8,128)S(1)}, u32[]{:S(2)}, u32[]{:S(2)}) %collective-permute-start.14) | collective-permute-done | bytes 65568 | tf_op jit(solution)/shard_map/ppermute | solution.py:333
  25.8 0.1 collective-permute-start.15
  25.9 0.0 collective-permute-done.8.refs_3_
  25.9 2.1 %shard_map.77 = (f32[8,64,128]{2,1,0:T(8,128)S(1)}, f32[8,64,128]{2,1,0:T(8,128)S(1)}) custom-call(f32[8]{0:T(128)S(1)} %copy-done.2, s32[4]{0:T(128)S(1)} %copy-done.3, f32[2,64,128]{2,1,0:T(8,128)S(1)} %add.71.refs_2_, f32[2,64,128]{2,1,0:T(8,128)S(1)} %collective-permute-done.8.refs_3_, f32[4,16,64,128]{3,2,1,0:T(8,128)S(1)} %copy-done), custom_call_target="tpu_custom_call" | custom-call | tf_op jit(solution)/shard_map/pallas_call | solution.py:214
  28.0 0.0 copy-start.1
  28.0 1.6 %collective-permute-start.9 = (f32[8,64,128]{2,1,0:T(8,128)S(1)}, f32[8,64,128]{2,1,0:T(8,128)S(1)}, u32[]{:S(2)}, u32[]{:S(2)}) collective-permute-start(f32[8,64,128]{2,1,0:T(8,128)S(1)} %get-tuple-element.29), channel_id=1, source_target_pairs={{0,16},{16,0},{1,17},{17,1},{2,18},{18,2},{3,19},{19,3},{4,20},{20... | collective-permute-start | bytes 786440 | tf_op jit(solution)/shard_map/ppermute | solution.py:333
  29.6 0.0 collective-permute-done.15.refs_3_
  29.6 1.5 %shard_map.79 = f32[8,64,128]{2,1,0:T(8,128)S(1)} custom-call(f32[8]{0:T(128)S(1)} %copy-done.2, s32[4]{0:T(128)S(1)} %copy-done.3, f32[2,64,128]{2,1,0:T(8,128)S(1)} %add.83.refs_2_, f32[2,64,128]{2,1,0:T(8,128)S(1)} %collective-permute-done.15.refs_3_, f32[4,16,64,128]{3,2,1,0:T(8,128)S(1)} %copy-done), custom_call_target="tpu_custom_call" | custom-call | tf_op jit(solution)/shard_map/pallas_call | solution.py:214
  31.1 0.6 collective-permute-start.16
  31.6 1.5 %shard_map.78.mine_ref = f32[8,64,128]{2,1,0:T(8,128)S(1)} custom-call(f32[8]{0:T(128)S(1)} %copy-done.2, s32[4]{0:T(128)S(1)} %copy-done.3, f32[2,64,128]{2,1,0:T(8,128)S(1)} %add.83.refs_2_, f32[2,64,128]{2,1,0:T(8,128)S(1)} %collective-permute-done.15.refs_3_, f32[4,16,64,128]{3,2,1,0:T(8,128)S(1)} %copy-done), custom_call_target="tpu_custom_call" | custom-call | tf_op jit(solution)/shard_map/pallas_call | solution.py:214
  33.1 4.1 %collective-permute-done.9.recv_ref = f32[8,64,128]{2,1,0:T(8,128)S(1)} collective-permute-done((f32[8,64,128]{2,1,0:T(8,128)S(1)}, f32[8,64,128]{2,1,0:T(8,128)S(1)}, u32[]{:S(2)}, u32[]{:S(2)}) %collective-permute-start.9) | collective-permute-done | bytes 262176 | tf_op jit(solution)/shard_map/ppermute | solution.py:333
  37.3 0.0 copy-done.1
  37.3 0.9 %share_bases.1 = (f32[8,64,128]{2,1,0:T(8,128)S(1)}, f32[8,64,128]{2,1,0:T(8,128)S(1)}) custom-call(f32[16,64,128]{2,1,0:T(8,128)S(1)} %copy-done.1, f32[8,64,128]{2,1,0:T(8,128)S(1)} %get-tuple-element.28.mine_ref, f32[8,64,128]{2,1,0:T(8,128)S(1)} %collective-permute-done.9.recv_ref, f32[128,64]{1,0:T(8,128)S(1)} %get-tuple-element.30.herm_ref.refs_5_), custom_call_target="tpu_custom_call" | custom-call | tf_op jit(solution)/shard_map/share_bases/pallas_call | solution.py:252
  38.1 4.3 %collective-permute-done.16.recv_ref = f32[8,64,128]{2,1,0:T(8,128)S(1)} collective-permute-done((f32[8,64,128]{2,1,0:T(8,128)S(1)}, f32[8,64,128]{2,1,0:T(8,128)S(1)}, u32[]{:S(2)}, u32[]{:S(2)}) %collective-permute-start.16) | collective-permute-done | bytes 262176 | tf_op jit(solution)/shard_map/ppermute | solution.py:333
  42.4 0.2 finish.1
  42.6 1.6 %collective-permute-start.17 = (f32[4,64,128]{2,1,0:T(8,128)S(1)}, f32[4,64,128]{2,1,0:T(8,128)S(1)}, u32[]{:S(2)}, u32[]{:S(2)}) collective-permute-start(f32[4,64,128]{2,1,0:T(8,128)S(1)} %get-tuple-element.36.refs_0_), channel_id=1, source_target_pairs={{0,16},{16,0},{1,17},{17,1},{2,18},{18,2},{3,19},{19,3},{4,20},{20... | collective-permute-start | bytes 393224 | tf_op jit(solution)/shard_map/ppermute | solution.py:333
  44.2 0.5 collective-permute-start.18
  44.7 13.3 %all_to_all.11 = f32[32,1,128]{2,1,0:T(1,128)S(1)} all-to-all(f32[32,1,128]{2,1,0:T(1,128)S(1)} %bitcast.12), channel_id=1, replica_groups=mesh['past'=2,'second'=16] {'past','second'}, dimensions={0} | all-to-all | bytes 32768 | tf_op jit(solution)/shard_map/all_to_all | solution.py:427
  57.9 0.6 norm.1
  58.5 0.0 collective-permute-done.17.refs_2_
  58.5 0.0 collective-permute-done.18.refs_3_
  58.5 0.8 %join.1 = f32[16,64,128]{2,1,0:T(8,128)} custom-call(f32[4,64,128]{2,1,0:T(8,128)S(1)} %get-tuple-element.36.refs_0_, f32[4,64,128]{2,1,0:T(8,128)S(1)} %get-tuple-element.37.refs_1_, f32[4,64,128]{2,1,0:T(8,128)S(1)} %collective-permute-done.17.refs_2_, f32[4,64,128]{2,1,0:T(8,128)S(1)} %collective-permute-done.18.refs_3_), custom_call_target="tpu_custom_call" | custom-call | tf_op jit(solution)/shard_map/join/pallas_call | solution.py:320
  (12 shorter events, 0.2 us)
Async XLA Ops:
  0.6 2.2 %copy-start.2 = (f32[8]{0:T(128)S(1)}, f32[8]{0:T(128)}, u32[]{:S(2)}) copy-start(f32[8]{0:T(128)} %refs_0_.6) | copy-start | bytes 100
  0.6 2.2 %copy-start.3 = (s32[4]{0:T(128)S(1)}, s32[4]{0:T(128)}, u32[]{:S(2)}) copy-start(s32[4]{0:T(128)} %refs_1_.7) | copy-start | bytes 52
  0.7 2.2 %copy-start = (f32[4,16,64,128]{3,2,1,0:T(8,128)S(1)}, f32[4,16,64,128]{3,2,1,0:T(8,128)}, u32[]{:S(2)}) copy-start(f32[4,16,64,128]{3,2,1,0:T(8,128)} %refs_4_.5) | copy-start | bytes 6291460
  4.4 1.5 %collective-permute-start.10 = (f32[2,2,64,128]{3,2,1,0:T(8,128)S(1)}, f32[2,2,64,128]{3,2,1,0:T(8,128)S(1)}, u32[]{:S(2)}, u32[]{:S(2)}) collective-permute-start(f32[2,2,64,128]{3,2,1,0:T(8,128)S(1)} %get-tuple-element.35), channel_id=1, source_target_pairs={{0,1},{1,0},{2,3},{3,2},{4,5},{5,4},{6,7},{7,6},{8,9},{9,8},{10,11... | collective-permute-start | bytes 393224 | tf_op jit(solution)/shard_map/ppermute | solution.py:333
  4.9 4.0 %collective-permute-start.4 = (f32[2,64,128]{2,1,0:T(8,128)S(1)}, f32[2,64,128]{2,1,0:T(8,128)S(1)}, u32[]{:S(2)}, u32[]{:S(2)}) collective-permute-start(f32[2,64,128]{2,1,0:T(8,128)S(1)} %get-tuple-element.27), channel_id=1, source_target_pairs={{0,1},{1,0},{2,3},{3,2},{4,5},{5,4},{6,7},{7,6},{8,9},{9,8},{10,11... | collective-permute-start | bytes 196616 | tf_op jit(solution)/shard_map/ppermute | solution.py:333
  6.0 5.3 %collective-permute-start.11 = (f32[1,2,64,128]{3,2,1,0:T(8,128)S(1)}, f32[1,2,64,128]{3,2,1,0:T(8,128)S(1)}, u32[]{:S(2)}, u32[]{:S(2)}) collective-permute-start(f32[1,2,64,128]{3,2,1,0:T(8,128)S(1)} %constant_dynamic-slice_fusion), channel_id=1, source_target_pairs={{0,16},{16,0},{1,17},{17,1},{2,18},{18,2},{3,19},{19,3},{4,20},{20... | collective-permute-start | bytes 196616 | tf_op jit(solution)/shard_map/ppermute | solution.py:333
  8.9 4.3 %collective-permute-start.5 = (f32[2,64,128]{2,1,0:T(8,128)S(1)}, f32[2,64,128]{2,1,0:T(8,128)S(1)}, u32[]{:S(2)}, u32[]{:S(2)}) collective-permute-start(f32[2,64,128]{2,1,0:T(8,128)S(1)} %add.68), channel_id=1, source_target_pairs={{0,2},{1,3},{2,0},{3,1},{4,6},{5,7},{6,4},{7,5},{8,10},{9,11},{10,... | collective-permute-start | bytes 196616 | tf_op jit(solution)/shard_map/ppermute | solution.py:333
  11.3 4.3 %collective-permute-start.12 = (f32[2,64,128]{2,1,0:T(8,128)S(1)}, f32[2,64,128]{2,1,0:T(8,128)S(1)}, u32[]{:S(2)}, u32[]{:S(2)}) collective-permute-start(f32[2,64,128]{2,1,0:T(8,128)S(1)} %add_bitcast_fusion), channel_id=1, source_target_pairs={{0,2},{1,3},{2,0},{3,1},{4,6},{5,7},{6,4},{7,5},{8,10},{9,11},{10,... | collective-permute-start | bytes 196616 | tf_op jit(solution)/shard_map/ppermute | solution.py:333
  13.3 4.9 %collective-permute-start.6 = (f32[2,64,128]{2,1,0:T(8,128)S(1)}, f32[2,64,128]{2,1,0:T(8,128)S(1)}, u32[]{:S(2)}, u32[]{:S(2)}) collective-permute-start(f32[2,64,128]{2,1,0:T(8,128)S(1)} %add.69), channel_id=1, source_target_pairs={{0,4},{1,5},{2,6},{3,7},{4,0},{5,1},{6,2},{7,3},{8,12},{9,13},{10,... | collective-permute-start | bytes 196616 | tf_op jit(solution)/shard_map/ppermute | solution.py:333
  15.7 4.9 %collective-permute-start.13 = (f32[2,64,128]{2,1,0:T(8,128)S(1)}, f32[2,64,128]{2,1,0:T(8,128)S(1)}, u32[]{:S(2)}, u32[]{:S(2)}) collective-permute-start(f32[2,64,128]{2,1,0:T(8,128)S(1)} %add.81), channel_id=1, source_target_pairs={{0,4},{1,5},{2,6},{3,7},{4,0},{5,1},{6,2},{7,3},{8,12},{9,13},{10,... | collective-permute-start | bytes 196616 | tf_op jit(solution)/shard_map/ppermute | solution.py:333
  18.2 6.4 %collective-permute-start.7 = (f32[2,64,128]{2,1,0:T(8,128)S(1)}, f32[2,64,128]{2,1,0:T(8,128)S(1)}, u32[]{:S(2)}, u32[]{:S(2)}) collective-permute-start(f32[2,64,128]{2,1,0:T(8,128)S(1)} %add.70), channel_id=1, source_target_pairs={{0,8},{1,9},{2,10},{3,11},{4,12},{5,13},{6,14},{7,15},{8,0},{9,1},... | collective-permute-start | bytes 196616 | tf_op jit(solution)/shard_map/ppermute | solution.py:333
  20.6 5.2 %collective-permute-start.14 = (f32[2,64,128]{2,1,0:T(8,128)S(1)}, f32[2,64,128]{2,1,0:T(8,128)S(1)}, u32[]{:S(2)}, u32[]{:S(2)}) collective-permute-start(f32[2,64,128]{2,1,0:T(8,128)S(1)} %add.82), channel_id=1, source_target_pairs={{0,8},{1,9},{2,10},{3,11},{4,12},{5,13},{6,14},{7,15},{8,0},{9,1},... | collective-permute-start | bytes 196616 | tf_op jit(solution)/shard_map/ppermute | solution.py:333
  24.5 1.4 %collective-permute-start.8 = (f32[2,64,128]{2,1,0:T(8,128)S(1)}, f32[2,64,128]{2,1,0:T(8,128)S(1)}, u32[]{:S(2)}, u32[]{:S(2)}) collective-permute-start(f32[2,64,128]{2,1,0:T(8,128)S(1)} %add.71.refs_2_), channel_id=1, source_target_pairs={{0,1},{1,0},{2,3},{3,2},{4,5},{5,4},{6,7},{7,6},{8,9},{9,8},{10,11... | collective-permute-start | bytes 196616 | tf_op jit(solution)/shard_map/ppermute | solution.py:333
  25.8 3.8 %collective-permute-start.15 = (f32[2,64,128]{2,1,0:T(8,128)S(1)}, f32[2,64,128]{2,1,0:T(8,128)S(1)}, u32[]{:S(2)}, u32[]{:S(2)}) collective-permute-start(f32[2,64,128]{2,1,0:T(8,128)S(1)} %add.83.refs_2_), channel_id=1, source_target_pairs={{0,1},{1,0},{2,3},{3,2},{4,5},{5,4},{6,7},{7,6},{8,9},{9,8},{10,11... | collective-permute-start | bytes 196616 | tf_op jit(solution)/shard_map/ppermute | solution.py:333
  28.0 9.3 %copy-start.1 = (f32[16,64,128]{2,1,0:T(8,128)S(1)}, f32[16,64,128]{2,1,0:T(8,128)}, u32[]{:S(2)}) copy-start(f32[16,64,128]{2,1,0:T(8,128)} %row_ref.3) | copy-start | bytes 1572868
  28.0 9.2 %collective-permute-start.9 = (f32[8,64,128]{2,1,0:T(8,128)S(1)}, f32[8,64,128]{2,1,0:T(8,128)S(1)}, u32[]{:S(2)}, u32[]{:S(2)}) collective-permute-start(f32[8,64,128]{2,1,0:T(8,128)S(1)} %get-tuple-element.29), channel_id=1, source_target_pairs={{0,16},{16,0},{1,17},{17,1},{2,18},{18,2},{3,19},{19,3},{4,20},{20... | collective-permute-start | bytes 786440 | tf_op jit(solution)/shard_map/ppermute | solution.py:333
  31.1 11.3 %collective-permute-start.16 = (f32[8,64,128]{2,1,0:T(8,128)S(1)}, f32[8,64,128]{2,1,0:T(8,128)S(1)}, u32[]{:S(2)}, u32[]{:S(2)}) collective-permute-start(f32[8,64,128]{2,1,0:T(8,128)S(1)} %shard_map.79), channel_id=1, source_target_pairs={{0,16},{16,0},{1,17},{17,1},{2,18},{18,2},{3,19},{19,3},{4,20},{20... | collective-permute-start | bytes 786440 | tf_op jit(solution)/shard_map/ppermute | solution.py:333
  42.6 16.0 %collective-permute-start.17 = (f32[4,64,128]{2,1,0:T(8,128)S(1)}, f32[4,64,128]{2,1,0:T(8,128)S(1)}, u32[]{:S(2)}, u32[]{:S(2)}) collective-permute-start(f32[4,64,128]{2,1,0:T(8,128)S(1)} %get-tuple-element.36.refs_0_), channel_id=1, source_target_pairs={{0,16},{16,0},{1,17},{17,1},{2,18},{18,2},{3,19},{19,3},{4,20},{20... | collective-permute-start | bytes 393224 | tf_op jit(solution)/shard_map/ppermute | solution.py:333
  44.2 14.4 %collective-permute-start.18 = (f32[4,64,128]{2,1,0:T(8,128)S(1)}, f32[4,64,128]{2,1,0:T(8,128)S(1)}, u32[]{:S(2)}, u32[]{:S(2)}) collective-permute-start(f32[4,64,128]{2,1,0:T(8,128)S(1)} %get-tuple-element.37.refs_1_), channel_id=1, source_target_pairs={{0,16},{16,0},{1,17},{17,1},{2,18},{18,2},{3,19},{19,3},{4,20},{20... | collective-permute-start | bytes 393224 | tf_op jit(solution)/shard_map/ppermute | solution.py:333

commit v5 on v4

--- a/solution.py
+++ b/solution.py
@@ -10,6 +10,7 @@
 
 coupling = 0.5
 step_size = 0.25
+LATE_PART = 8
 
 f32 = jnp.float32
 bf16 = jnp.bfloat16
@@ -263,21 +264,25 @@
     total = jnp.zeros(mine_ref.shape[1:], f32)
     for s in range(mine_ref.shape[0]):
         last = mine_ref[s] + recv_ref[s]
-        rows = out_refs[0].shape[0]
-        out_refs[s // rows][s % rows] = out_base_ref[s] + last
+        chunk, first = 0, 0
+        while s >= first + out_refs[chunk].shape[0]:
+            first += out_refs[chunk].shape[0]
+            chunk += 1
+        out_refs[chunk][s - first] = out_base_ref[s] + last
         diff = diff_base_ref[s] + last
         total = total + diff * diff
     square_ref[...] = jnp.broadcast_to(jnp.sum(total), square_ref.shape)
 
 
 def finish(out_base, diff_base, mine, recv, devices):
-    chunks = 2 if mine.shape[0] % 2 == 0 else 1
-    chunk = jax.ShapeDtypeStruct((mine.shape[0] // chunks,) + mine.shape[1:], f32)
+    late = mine.shape[0] // LATE_PART
+    sizes = [mine.shape[0] - late, late] if late else [mine.shape[0]]
     return pl.pallas_call(
         finish_kernel,
         in_specs=[VMEM_SPEC] * 4,
-        out_specs=[VMEM_SPEC] * (1 + chunks),
-        out_shape=[jax.ShapeDtypeStruct((devices, 128), f32)] + [chunk] * chunks,
+        out_specs=[VMEM_SPEC] * (1 + len(sizes)),
+        out_shape=[jax.ShapeDtypeStruct((devices, 128), f32)]
+        + [jax.ShapeDtypeStruct((size,) + mine.shape[1:], f32) for size in sizes],
         compiler_params=PARAMS,
         name="finish",
     )(out_base, diff_base, mine, recv)
@@ -301,12 +306,14 @@
 
 def join_kernel(*refs, mask, chunks):
     own, other, out_ref, sems = refs[:chunks], refs[chunks : 2 * chunks], refs[-2], refs[-1]
-    rows = own[0].shape[0]
     upper = lax.axis_index("past") // mask % 2
     copies = []
     for side, parts in ((upper, own), (1 - upper, other)):
-        for i, part in enumerate(parts):
-            target = out_ref.at[pl.ds((side * chunks + i) * rows, rows)]
+        first = side * (out_ref.shape[0] // 2)
+        for part in parts:
+            rows = part.shape[0]
+            target = out_ref.at[pl.ds(first, rows)]
+            first = first + rows
             copies.append(pltpu.make_async_copy(part, target, sems.at[len(copies)]))
     for copy in copies:
         copy.start()
@@ -316,7 +323,7 @@
 
 def join(own, other, mask):
     chunks = len(own)
-    rows = 2 * chunks * own[0].shape[0]
+    rows = 2 * sum(part.shape[0] for part in own)
     return pl.pallas_call(
         lambda *refs: join_kernel(*refs, mask=mask, chunks=chunks),
         in_specs=[VMEM_SPEC] * (2 * chunks),
@@ -413,9 +420,11 @@
     pred_mine = spread_second(scatter_past(part_keep + exchange(part_send, "second", 1)))
     pred_other = exchange(pred_mine, "second", 1)
 
-    slope_keep, slope_send = integral(
-        quad_table, weight_index, row_mine, row_other, green_hist, past_size, (True, False), scale
-    )
+    def slope_half(kept):
+        return integral(quad_table, weight_index, row_mine, row_other, green_hist, past_size, (kept,), scale)[0]
+
+    slope_send = slope_half(False)
+    slope_keep = slope_half(True)
     out_base, diff_base = share_bases(green_row, *share_past(slope_keep, slope_send), herm)
 
     final = 0.5 * step_size * scale

time: 59.6 us -> 58.9 us (0.988)
  waiting for transfers between devices: 14.2 us -> 12.7 us
  Pallas kernels: 10.2 us -> 11.1 us
    ppermute x15, waiting for transfers between devices: 14.2 us -> 12.7 us  [exchange(): return lax.ppermute(value, axis, [(i, i ^ mask) for i in range(size)])]
    pallas_call x3 -> x4, Pallas kernels: 5.01 us -> 5.88 us  [integral(): pl.pallas_call(lambda *refs: integral_kernel(*refs, scale=scale, sides=si...]
  transfers between devices with their start and end apart: 15 -> 15, of which waited for: 8 -> 8; matrix products, arithmetic and copies ran while one was open for 0% -> 0% of each run, Pallas kernels for 11% -> 12%
where the time goes in v5:
time: 58.9 us; the launch traced here: 58.8 us
  starting transfers between devices  19.8 us (34%)
  blocking collectives  13.3 us (23%)
  waiting for transfers between devices  12.7 us (22%)
  Pallas kernels  11.1 us (19%)
  between operations  1.68 us (3%)
    ppermute x15, starting transfers between devices, exchange(): return lax.ppermute(value, axis, [(i, i ^ mask) for i in range(size)])  19.8 us
    all_to_all x1, blocking collectives, step(): sums = lax.all_to_all(squares, ('past', 'second'), 0, 0, tiled=True)  13.3 us
    ppermute x15, waiting for transfers between devices, exchange(): return lax.ppermute(value, axis, [(i, i ^ mask) for i in range(size)])  12.7 us
    pallas_call x4, Pallas kernels, integral(): pl.pallas_call(lambda *refs: integral_kernel(*refs, scale=scale, sides=si...  5.88 us
    pallas_call x1, Pallas kernels, owner_part(): pl.pallas_call(lambda *refs: owner_kernel(*refs, scale=scale), in_specs=[...  1.55 us
    pallas_call x1, Pallas kernels, prepare(): pl.pallas_call(prepare_kernel, in_specs=[SMEM_SPEC, HBM_SPEC, HBM_SPEC],...  1.24 us
  transfers between devices with their start and end apart: 15, of which 8 were waited for; matrix products, arithmetic and copies ran while one was open for 0% of the time, Pallas kernels for 12%

profile of v5, /device:TPU:0, one launch (start us, length us, event | category | flops | bytes accessed | tf_op | source)
XLA Modules:
  0.0 58.8 jit_solution(8475163371989034769)
XLA Ops:
  0.6 0.0 copy-start.2
  0.6 0.0 copy-start.3
  0.7 0.0 copy-start
  1.5 1.2 %prepare.1 = (f32[4,64,128]{2,1,0:T(8,128)S(1)}, f32[2,64,128]{2,1,0:T(8,128)S(1)}, f32[2,64,128]{2,1,0:T(8,128)S(1)}, f32[128,64]{1,0:T(8,128)S(1)}) custom-call(s32[1]{0:T(128)} %copy.14.start_ref.refs_0_, f32[16,64,128]{2,1,0:T(8,128)} %row_ref.3, f32[64,128]{1,0:T(8,128)} %ham_hbm.1), custom_call_target="tpu_custom_call" | custom-call | tf_op jit(solution)/shard_map/prepare/pallas_call | solution.py:104
  2.8 0.0 copy-done.2
  2.8 0.0 copy-done.3
  2.8 0.0 copy-done
  2.8 1.5 %owner_part.1 = (f32[2,2,64,128]{3,2,1,0:T(8,128)S(1)}, f32[2,2,64,128]{3,2,1,0:T(8,128)S(1)}) custom-call(s32[1]{0:T(128)} %copy.14.start_ref.refs_0_, f32[8]{0:T(128)S(1)} %copy-done.2, s32[4]{0:T(128)S(1)} %copy-done.3, f32[4,64,128]{2,1,0:T(8,128)S(1)} %get-tuple-element.35.refs_3_, f32[4,64,128]{2,1,0:T(8,128)S(1)} %get-tuple-element.29.refs_4_, ...), custom_call_target="tpu_custom_call" | custom-call | tf_op jit(solution)/shard_map/owner_part/pallas_call | solution.py:179
  4.4 0.6 collective-permute-start.10
  4.9 0.1 collective-permute-start.4
  5.0 0.9 %collective-permute-done.10 = f32[2,2,64,128]{3,2,1,0:T(8,128)S(1)} collective-permute-done((f32[2,2,64,128]{3,2,1,0:T(8,128)S(1)}, f32[2,2,64,128]{3,2,1,0:T(8,128)S(1)}, u32[]{:S(2)}, u32[]{:S(2)}) %collective-permute-start.10) | collective-permute-done | bytes 131104 | tf_op jit(solution)/shard_map/ppermute | solution.py:340
  6.0 2.9 %collective-permute-start.11 = (f32[1,2,64,128]{3,2,1,0:T(8,128)S(1)}, f32[1,2,64,128]{3,2,1,0:T(8,128)S(1)}, u32[]{:S(2)}, u32[]{:S(2)}) collective-permute-start(f32[1,2,64,128]{3,2,1,0:T(8,128)S(1)} %constant_dynamic-slice_fusion), channel_id=1, source_target_pairs={{0,16},{16,0},{1,17},{17,1},{2,18},{18,2},{3,19},{19,3},{4,20},{20... | collective-permute-start | bytes 196616 | tf_op jit(solution)/shard_map/ppermute | solution.py:340
  8.9 0.0 collective-permute-done.4
  8.9 1.6 %collective-permute-start.5 = (f32[2,64,128]{2,1,0:T(8,128)S(1)}, f32[2,64,128]{2,1,0:T(8,128)S(1)}, u32[]{:S(2)}, u32[]{:S(2)}) collective-permute-start(f32[2,64,128]{2,1,0:T(8,128)S(1)} %add.68), channel_id=1, source_target_pairs={{0,2},{1,3},{2,0},{3,1},{4,6},{5,7},{6,4},{7,5},{8,10},{9,11},{10,... | collective-permute-start | bytes 196616 | tf_op jit(solution)/shard_map/ppermute | solution.py:340
  10.5 0.8 %collective-permute-done.11 = f32[1,2,64,128]{3,2,1,0:T(8,128)S(1)} collective-permute-done((f32[1,2,64,128]{3,2,1,0:T(8,128)S(1)}, f32[1,2,64,128]{3,2,1,0:T(8,128)S(1)}, u32[]{:S(2)}, u32[]{:S(2)}) %collective-permute-start.11) | collective-permute-done | bytes 65568 | tf_op jit(solution)/shard_map/ppermute | solution.py:340
  11.3 1.9 %collective-permute-start.12 = (f32[2,64,128]{2,1,0:T(8,128)S(1)}, f32[2,64,128]{2,1,0:T(8,128)S(1)}, u32[]{:S(2)}, u32[]{:S(2)}) collective-permute-start(f32[2,64,128]{2,1,0:T(8,128)S(1)} %add_bitcast_fusion), channel_id=1, source_target_pairs={{0,2},{1,3},{2,0},{3,1},{4,6},{5,7},{6,4},{7,5},{8,10},{9,11},{10,... | collective-permute-start | bytes 196616 | tf_op jit(solution)/shard_map/ppermute | solution.py:340
  13.2 0.0 collective-permute-done.5
  13.3 1.6 %collective-permute-start.6 = (f32[2,64,128]{2,1,0:T(8,128)S(1)}, f32[2,64,128]{2,1,0:T(8,128)S(1)}, u32[]{:S(2)}, u32[]{:S(2)}) collective-permute-start(f32[2,64,128]{2,1,0:T(8,128)S(1)} %add.69), channel_id=1, source_target_pairs={{0,4},{1,5},{2,6},{3,7},{4,0},{5,1},{6,2},{7,3},{8,12},{9,13},{10,... | collective-permute-start | bytes 196616 | tf_op jit(solution)/shard_map/ppermute | solution.py:340
  14.9 0.7 %collective-permute-done.12 = f32[2,64,128]{2,1,0:T(8,128)S(1)} collective-permute-done((f32[2,64,128]{2,1,0:T(8,128)S(1)}, f32[2,64,128]{2,1,0:T(8,128)S(1)}, u32[]{:S(2)}, u32[]{:S(2)}) %collective-permute-start.12) | collective-permute-done | bytes 65568 | tf_op jit(solution)/shard_map/ppermute | solution.py:340
  15.7 2.0 %collective-permute-start.13 = (f32[2,64,128]{2,1,0:T(8,128)S(1)}, f32[2,64,128]{2,1,0:T(8,128)S(1)}, u32[]{:S(2)}, u32[]{:S(2)}) collective-permute-start(f32[2,64,128]{2,1,0:T(8,128)S(1)} %add.81), channel_id=1, source_target_pairs={{0,4},{1,5},{2,6},{3,7},{4,0},{5,1},{6,2},{7,3},{8,12},{9,13},{10,... | collective-permute-start | bytes 196616 | tf_op jit(solution)/shard_map/ppermute | solution.py:340
  17.6 0.5 collective-permute-done.6
  18.2 2.4 %collective-permute-start.7 = (f32[2,64,128]{2,1,0:T(8,128)S(1)}, f32[2,64,128]{2,1,0:T(8,128)S(1)}, u32[]{:S(2)}, u32[]{:S(2)}) collective-permute-start(f32[2,64,128]{2,1,0:T(8,128)S(1)} %add.70), channel_id=1, source_target_pairs={{0,8},{1,9},{2,10},{3,11},{4,12},{5,13},{6,14},{7,15},{8,0},{9,1},... | collective-permute-start | bytes 196616 | tf_op jit(solution)/shard_map/ppermute | solution.py:340
  20.6 0.0 collective-permute-done.13
  20.6 2.4 %collective-permute-start.14 = (f32[2,64,128]{2,1,0:T(8,128)S(1)}, f32[2,64,128]{2,1,0:T(8,128)S(1)}, u32[]{:S(2)}, u32[]{:S(2)}) collective-permute-start(f32[2,64,128]{2,1,0:T(8,128)S(1)} %add.82), channel_id=1, source_target_pairs={{0,8},{1,9},{2,10},{3,11},{4,12},{5,13},{6,14},{7,15},{8,0},{9,1},... | collective-permute-start | bytes 196616 | tf_op jit(solution)/shard_map/ppermute | solution.py:340
  23.0 1.5 %collective-permute-done.7 = f32[2,64,128]{2,1,0:T(8,128)S(1)} collective-permute-done((f32[2,64,128]{2,1,0:T(8,128)S(1)}, f32[2,64,128]{2,1,0:T(8,128)S(1)}, u32[]{:S(2)}, u32[]{:S(2)}) %collective-permute-start.7) | collective-permute-done | bytes 65568 | tf_op jit(solution)/shard_map/ppermute | solution.py:340
  24.5 0.1 collective-permute-start.8
  24.6 1.2 %collective-permute-done.14 = f32[2,64,128]{2,1,0:T(8,128)S(1)} collective-permute-done((f32[2,64,128]{2,1,0:T(8,128)S(1)}, f32[2,64,128]{2,1,0:T(8,128)S(1)}, u32[]{:S(2)}, u32[]{:S(2)}) %collective-permute-start.14) | collective-permute-done | bytes 65568 | tf_op jit(solution)/shard_map/ppermute | solution.py:340
  25.8 0.1 collective-permute-start.15
  25.9 0.0 collective-permute-done.8.refs_3_
  25.9 1.5 %shard_map.78 = f32[8,64,128]{2,1,0:T(8,128)S(1)} custom-call(f32[8]{0:T(128)S(1)} %copy-done.2, s32[4]{0:T(128)S(1)} %copy-done.3, f32[2,64,128]{2,1,0:T(8,128)S(1)} %add.71.refs_2_, f32[2,64,128]{2,1,0:T(8,128)S(1)} %collective-permute-done.8.refs_3_, f32[4,16,64,128]{3,2,1,0:T(8,128)S(1)} %copy-done), custom_call_target="tpu_custom_call" | custom-call | tf_op jit(solution)/shard_map/pallas_call | solution.py:215
  27.4 1.6 %collective-permute-start.9 = (f32[8,64,128]{2,1,0:T(8,128)S(1)}, f32[8,64,128]{2,1,0:T(8,128)S(1)}, u32[]{:S(2)}, u32[]{:S(2)}) collective-permute-start(f32[8,64,128]{2,1,0:T(8,128)S(1)} %shard_map.78), channel_id=1, source_target_pairs={{0,16},{16,0},{1,17},{17,1},{2,18},{18,2},{3,19},{19,3},{4,20},{20... | collective-permute-start | bytes 786440 | tf_op jit(solution)/shard_map/ppermute | solution.py:340
  29.0 0.0 collective-permute-done.15.refs_3_
  29.0 1.5 %shard_map.80 = f32[8,64,128]{2,1,0:T(8,128)S(1)} custom-call(f32[8]{0:T(128)S(1)} %copy-done.2, s32[4]{0:T(128)S(1)} %copy-done.3, f32[2,64,128]{2,1,0:T(8,128)S(1)} %add.83.refs_2_, f32[2,64,128]{2,1,0:T(8,128)S(1)} %collective-permute-done.15.refs_3_, f32[4,16,64,128]{3,2,1,0:T(8,128)S(1)} %copy-done), custom_call_target="tpu_custom_call" | custom-call | tf_op jit(solution)/shard_map/pallas_call | solution.py:215
  30.5 0.0 copy-start.1
  30.5 0.6 collective-permute-start.16
  31.1 1.5 %shard_map.77.mine_ref = f32[8,64,128]{2,1,0:T(8,128)S(1)} custom-call(f32[8]{0:T(128)S(1)} %copy-done.2, s32[4]{0:T(128)S(1)} %copy-done.3, f32[2,64,128]{2,1,0:T(8,128)S(1)} %add.71.refs_2_, f32[2,64,128]{2,1,0:T(8,128)S(1)} %collective-permute-done.8.refs_3_, f32[4,16,64,128]{3,2,1,0:T(8,128)S(1)} %copy-done), custom_call_target="tpu_custom_call" | custom-call | tf_op jit(solution)/shard_map/pallas_call | solution.py:215
  32.5 1.5 %shard_map.79.mine_ref = f32[8,64,128]{2,1,0:T(8,128)S(1)} custom-call(f32[8]{0:T(128)S(1)} %copy-done.2, s32[4]{0:T(128)S(1)} %copy-done.3, f32[2,64,128]{2,1,0:T(8,128)S(1)} %add.83.refs_2_, f32[2,64,128]{2,1,0:T(8,128)S(1)} %collective-permute-done.15.refs_3_, f32[4,16,64,128]{3,2,1,0:T(8,128)S(1)} %copy-done), custom_call_target="tpu_custom_call" | custom-call | tf_op jit(solution)/shard_map/pallas_call | solution.py:215
  34.0 2.6 %collective-permute-done.9.recv_ref = f32[8,64,128]{2,1,0:T(8,128)S(1)} collective-permute-done((f32[8,64,128]{2,1,0:T(8,128)S(1)}, f32[8,64,128]{2,1,0:T(8,128)S(1)}, u32[]{:S(2)}, u32[]{:S(2)}) %collective-permute-start.9) | collective-permute-done | bytes 262176 | tf_op jit(solution)/shard_map/ppermute | solution.py:340
  36.6 0.9 %share_bases.1 = (f32[8,64,128]{2,1,0:T(8,128)S(1)}, f32[8,64,128]{2,1,0:T(8,128)S(1)}) custom-call(f32[16,64,128]{2,1,0:T(8,128)S(1)} %copy-done.1, f32[8,64,128]{2,1,0:T(8,128)S(1)} %shard_map.77.mine_ref, f32[8,64,128]{2,1,0:T(8,128)S(1)} %collective-permute-done.9.recv_ref, f32[128,64]{1,0:T(8,128)S(1)} %get-tuple-element.26.herm_ref.refs_5_), custom_call_target="tpu_custom_call" | custom-call | tf_op jit(solution)/shard_map/share_bases/pallas_call | solution.py:253
  37.5 4.3 %collective-permute-done.16.recv_ref = f32[8,64,128]{2,1,0:T(8,128)S(1)} collective-permute-done((f32[8,64,128]{2,1,0:T(8,128)S(1)}, f32[8,64,128]{2,1,0:T(8,128)S(1)}, u32[]{:S(2)}, u32[]{:S(2)}) %collective-permute-start.16) | collective-permute-done | bytes 262176 | tf_op jit(solution)/shard_map/ppermute | solution.py:340
  41.8 0.2 finish.1
  42.0 1.6 %collective-permute-start.17 = (f32[7,64,128]{2,1,0:T(8,128)S(1)}, f32[7,64,128]{2,1,0:T(8,128)S(1)}, u32[]{:S(2)}, u32[]{:S(2)}) collective-permute-start(f32[7,64,128]{2,1,0:T(8,128)S(1)} %get-tuple-element.32.refs_0_), channel_id=1, source_target_pairs={{0,16},{16,0},{1,17},{17,1},{2,18},{18,2},{3,19},{19,3},{4,20},{20... | collective-permute-start | bytes 688136 | tf_op jit(solution)/shard_map/ppermute | solution.py:340
  43.6 0.5 collective-permute-start.18
  44.1 13.3 %all_to_all.11 = f32[32,1,128]{2,1,0:T(1,128)S(1)} all-to-all(f32[32,1,128]{2,1,0:T(1,128)S(1)} %bitcast.12), channel_id=1, replica_groups=mesh['past'=2,'second'=16] {'past','second'}, dimensions={0} | all-to-all | bytes 32768 | tf_op jit(solution)/shard_map/all_to_all | solution.py:436
  57.3 0.6 norm.1
  57.9 0.0 collective-permute-done.18.refs_3_
  57.9 0.0 collective-permute-done.17.refs_2_
  57.9 0.8 %join.1 = f32[16,64,128]{2,1,0:T(8,128)} custom-call(f32[7,64,128]{2,1,0:T(8,128)S(1)} %get-tuple-element.32.refs_0_, f32[1,64,128]{2,1,0:T(8,128)S(1)} %get-tuple-element.33.refs_1_, f32[7,64,128]{2,1,0:T(8,128)S(1)} %collective-permute-done.17.refs_2_, f32[1,64,128]{2,1,0:T(8,128)S(1)} %collective-permute-done.18.refs_3_), custom_call_target="tpu_custom_call" | custom-call | tf_op jit(solution)/shard_map/join/pallas_call | solution.py:327
  (13 shorter events, 0.2 us)
Async XLA Ops:
  0.6 2.2 %copy-start.2 = (f32[8]{0:T(128)S(1)}, f32[8]{0:T(128)}, u32[]{:S(2)}) copy-start(f32[8]{0:T(128)} %refs_0_.8) | copy-start | bytes 100
  0.6 2.2 %copy-start.3 = (s32[4]{0:T(128)S(1)}, s32[4]{0:T(128)}, u32[]{:S(2)}) copy-start(s32[4]{0:T(128)} %refs_1_.9) | copy-start | bytes 52
  0.7 2.2 %copy-start = (f32[4,16,64,128]{3,2,1,0:T(8,128)S(1)}, f32[4,16,64,128]{3,2,1,0:T(8,128)}, u32[]{:S(2)}) copy-start(f32[4,16,64,128]{3,2,1,0:T(8,128)} %refs_4_.7) | copy-start | bytes 6291460
  4.4 1.5 %collective-permute-start.10 = (f32[2,2,64,128]{3,2,1,0:T(8,128)S(1)}, f32[2,2,64,128]{3,2,1,0:T(8,128)S(1)}, u32[]{:S(2)}, u32[]{:S(2)}) collective-permute-start(f32[2,2,64,128]{3,2,1,0:T(8,128)S(1)} %get-tuple-element.31), channel_id=1, source_target_pairs={{0,1},{1,0},{2,3},{3,2},{4,5},{5,4},{6,7},{7,6},{8,9},{9,8},{10,11... | collective-permute-start | bytes 393224 | tf_op jit(solution)/shard_map/ppermute | solution.py:340
  4.9 4.0 %collective-permute-start.4 = (f32[2,64,128]{2,1,0:T(8,128)S(1)}, f32[2,64,128]{2,1,0:T(8,128)S(1)}, u32[]{:S(2)}, u32[]{:S(2)}) collective-permute-start(f32[2,64,128]{2,1,0:T(8,128)S(1)} %get-tuple-element.25), channel_id=1, source_target_pairs={{0,1},{1,0},{2,3},{3,2},{4,5},{5,4},{6,7},{7,6},{8,9},{9,8},{10,11... | collective-permute-start | bytes 196616 | tf_op jit(solution)/shard_map/ppermute | solution.py:340
  6.0 5.3 %collective-permute-start.11 = (f32[1,2,64,128]{3,2,1,0:T(8,128)S(1)}, f32[1,2,64,128]{3,2,1,0:T(8,128)S(1)}, u32[]{:S(2)}, u32[]{:S(2)}) collective-permute-start(f32[1,2,64,128]{3,2,1,0:T(8,128)S(1)} %constant_dynamic-slice_fusion), channel_id=1, source_target_pairs={{0,16},{16,0},{1,17},{17,1},{2,18},{18,2},{3,19},{19,3},{4,20},{20... | collective-permute-start | bytes 196616 | tf_op jit(solution)/shard_map/ppermute | solution.py:340
  8.9 4.3 %collective-permute-start.5 = (f32[2,64,128]{2,1,0:T(8,128)S(1)}, f32[2,64,128]{2,1,0:T(8,128)S(1)}, u32[]{:S(2)}, u32[]{:S(2)}) collective-permute-start(f32[2,64,128]{2,1,0:T(8,128)S(1)} %add.68), channel_id=1, source_target_pairs={{0,2},{1,3},{2,0},{3,1},{4,6},{5,7},{6,4},{7,5},{8,10},{9,11},{10,... | collective-permute-start | bytes 196616 | tf_op jit(solution)/shard_map/ppermute | solution.py:340
  11.3 4.3 %collective-permute-start.12 = (f32[2,64,128]{2,1,0:T(8,128)S(1)}, f32[2,64,128]{2,1,0:T(8,128)S(1)}, u32[]{:S(2)}, u32[]{:S(2)}) collective-permute-start(f32[2,64,128]{2,1,0:T(8,128)S(1)} %add_bitcast_fusion), channel_id=1, source_target_pairs={{0,2},{1,3},{2,0},{3,1},{4,6},{5,7},{6,4},{7,5},{8,10},{9,11},{10,... | collective-permute-start | bytes 196616 | tf_op jit(solution)/shard_map/ppermute | solution.py:340
  13.3 4.9 %collective-permute-start.6 = (f32[2,64,128]{2,1,0:T(8,128)S(1)}, f32[2,64,128]{2,1,0:T(8,128)S(1)}, u32[]{:S(2)}, u32[]{:S(2)}) collective-permute-start(f32[2,64,128]{2,1,0:T(8,128)S(1)} %add.69), channel_id=1, source_target_pairs={{0,4},{1,5},{2,6},{3,7},{4,0},{5,1},{6,2},{7,3},{8,12},{9,13},{10,... | collective-permute-start | bytes 196616 | tf_op jit(solution)/shard_map/ppermute | solution.py:340
  15.7 4.9 %collective-permute-start.13 = (f32[2,64,128]{2,1,0:T(8,128)S(1)}, f32[2,64,128]{2,1,0:T(8,128)S(1)}, u32[]{:S(2)}, u32[]{:S(2)}) collective-permute-start(f32[2,64,128]{2,1,0:T(8,128)S(1)} %add.81), channel_id=1, source_target_pairs={{0,4},{1,5},{2,6},{3,7},{4,0},{5,1},{6,2},{7,3},{8,12},{9,13},{10,... | collective-permute-start | bytes 196616 | tf_op jit(solution)/shard_map/ppermute | solution.py:340
  18.2 6.4 %collective-permute-start.7 = (f32[2,64,128]{2,1,0:T(8,128)S(1)}, f32[2,64,128]{2,1,0:T(8,128)S(1)}, u32[]{:S(2)}, u32[]{:S(2)}) collective-permute-start(f32[2,64,128]{2,1,0:T(8,128)S(1)} %add.70), channel_id=1, source_target_pairs={{0,8},{1,9},{2,10},{3,11},{4,12},{5,13},{6,14},{7,15},{8,0},{9,1},... | collective-permute-start | bytes 196616 | tf_op jit(solution)/shard_map/ppermute | solution.py:340
  20.6 5.2 %collective-permute-start.14 = (f32[2,64,128]{2,1,0:T(8,128)S(1)}, f32[2,64,128]{2,1,0:T(8,128)S(1)}, u32[]{:S(2)}, u32[]{:S(2)}) collective-permute-start(f32[2,64,128]{2,1,0:T(8,128)S(1)} %add.82), channel_id=1, source_target_pairs={{0,8},{1,9},{2,10},{3,11},{4,12},{5,13},{6,14},{7,15},{8,0},{9,1},... | collective-permute-start | bytes 196616 | tf_op jit(solution)/shard_map/ppermute | solution.py:340
  24.5 1.4 %collective-permute-start.8 = (f32[2,64,128]{2,1,0:T(8,128)S(1)}, f32[2,64,128]{2,1,0:T(8,128)S(1)}, u32[]{:S(2)}, u32[]{:S(2)}) collective-permute-start(f32[2,64,128]{2,1,0:T(8,128)S(1)} %add.71.refs_2_), channel_id=1, source_target_pairs={{0,1},{1,0},{2,3},{3,2},{4,5},{5,4},{6,7},{7,6},{8,9},{9,8},{10,11... | collective-permute-start | bytes 196616 | tf_op jit(solution)/shard_map/ppermute | solution.py:340
  25.8 3.2 %collective-permute-start.15 = (f32[2,64,128]{2,1,0:T(8,128)S(1)}, f32[2,64,128]{2,1,0:T(8,128)S(1)}, u32[]{:S(2)}, u32[]{:S(2)}) collective-permute-start(f32[2,64,128]{2,1,0:T(8,128)S(1)} %add.83.refs_2_), channel_id=1, source_target_pairs={{0,1},{1,0},{2,3},{3,2},{4,5},{5,4},{6,7},{7,6},{8,9},{9,8},{10,11... | collective-permute-start | bytes 196616 | tf_op jit(solution)/shard_map/ppermute | solution.py:340
  27.4 9.2 %collective-permute-start.9 = (f32[8,64,128]{2,1,0:T(8,128)S(1)}, f32[8,64,128]{2,1,0:T(8,128)S(1)}, u32[]{:S(2)}, u32[]{:S(2)}) collective-permute-start(f32[8,64,128]{2,1,0:T(8,128)S(1)} %shard_map.78), channel_id=1, source_target_pairs={{0,16},{16,0},{1,17},{17,1},{2,18},{18,2},{3,19},{19,3},{4,20},{20... | collective-permute-start | bytes 786440 | tf_op jit(solution)/shard_map/ppermute | solution.py:340
  30.5 6.2 %copy-start.1 = (f32[16,64,128]{2,1,0:T(8,128)S(1)}, f32[16,64,128]{2,1,0:T(8,128)}, u32[]{:S(2)}) copy-start(f32[16,64,128]{2,1,0:T(8,128)} %row_ref.3) | copy-start | bytes 1572868
  30.5 11.3 %collective-permute-start.16 = (f32[8,64,128]{2,1,0:T(8,128)S(1)}, f32[8,64,128]{2,1,0:T(8,128)S(1)}, u32[]{:S(2)}, u32[]{:S(2)}) collective-permute-start(f32[8,64,128]{2,1,0:T(8,128)S(1)} %shard_map.80), channel_id=1, source_target_pairs={{0,16},{16,0},{1,17},{17,1},{2,18},{18,2},{3,19},{19,3},{4,20},{20... | collective-permute-start | bytes 786440 | tf_op jit(solution)/shard_map/ppermute | solution.py:340
  42.0 16.0 %collective-permute-start.17 = (f32[7,64,128]{2,1,0:T(8,128)S(1)}, f32[7,64,128]{2,1,0:T(8,128)S(1)}, u32[]{:S(2)}, u32[]{:S(2)}) collective-permute-start(f32[7,64,128]{2,1,0:T(8,128)S(1)} %get-tuple-element.32.refs_0_), channel_id=1, source_target_pairs={{0,16},{16,0},{1,17},{17,1},{2,18},{18,2},{3,19},{19,3},{4,20},{20... | collective-permute-start | bytes 688136 | tf_op jit(solution)/shard_map/ppermute | solution.py:340
  43.6 14.4 %collective-permute-start.18 = (f32[1,64,128]{2,1,0:T(8,128)S(1)}, f32[1,64,128]{2,1,0:T(8,128)S(1)}, u32[]{:S(2)}, u32[]{:S(2)}) collective-permute-start(f32[1,64,128]{2,1,0:T(8,128)S(1)} %get-tuple-element.33.refs_1_), channel_id=1, source_target_pairs={{0,16},{16,0},{1,17},{17,1},{2,18},{18,2},{3,19},{19,3},{4,20},{20... | collective-permute-start | bytes 98312 | tf_op jit(solution)/shard_map/ppermute | solution.py:340
